TPU v7x, 32 devices: a whole 2x2x4 slice. The times are simulated.
32 devices in a mesh: stn: 8 (over z, x), tf: 4 (over y, core).
Axes of the slice: x: 2, y: 2, z: 4, core: 2. Of those that a mesh axis runs over, the one named last changes fastest.
Arguments:
- voltages: bfloat16 [2, 64, 2, 131072], P(None, 'stn', None, 'tf'), may hold values from -6 to 6
- delay_table: float32 [128, 64], replicated, may hold values from -512 to 512
- beam_pointing: int32 [32], replicated, may hold values from 0 to 127
- station_group: int32 [64], replicated, may hold values from 0 to 3
Outputs:
- beams: bfloat16 [32, 2, 2, 32, 32, 128], P('stn', None, None, None, 'tf')
All inputs are finite; a program needn't handle non-finite values.
Results may differ from a plain program's by a relative error of at most 0.0082.
Values may be sent and summed in bfloat16 or wider, within the bound.
No kernel may reach another device: no remote copies, remote signals or barrier semaphores. Data moves between devices by JAX's collectives and lax.ppermute only.
A program may use at most 128 MiB of HBM per device.

v0:
```python
import math

import jax
import jax.numpy as jnp
from jax import lax
from jax.sharding import PartitionSpec as P

TAPS = 16
CH_LO = 32
CH_HI = 128
GROUPS = 4


TWO_PI = 2.0 * math.pi


def passed_along(value, axis, steps):
    count = lax.axis_size(axis)
    first, last = (max(0, -steps), min(count, count - steps))
    return lax.ppermute(value, axis, [(source, source + steps) for source in range(first, last)])


def filter_window(tap_count, points):
    position = jnp.arange(tap_count * points, dtype=jnp.int32).astype(jnp.float32)
    total_len = float(tap_count * points)
    hann_taper = 0.5 - 0.5 * jnp.cos(TWO_PI / total_len * position)
    kernel = jnp.sinc((position - 0.5 * total_len) / float(points)) * hann_taper
    return kernel.reshape(tap_count, points)


def dft_table(points):
    counter = jnp.arange(points, dtype=jnp.int32)
    product = counter[:, None] * counter[None, :] % points
    angles = TWO_PI / points * product.astype(jnp.float32)
    factor = 1.0 / math.sqrt(points)
    cosine = jnp.cos(angles) * factor
    sine_part = jnp.sin(angles) * factor
    stacked = jnp.stack([jnp.stack([cosine, sine_part]), jnp.stack([-sine_part, cosine])])
    return stacked.astype(jnp.bfloat16)


def channelize(extended, frame_count):
    points = CH_LO * CH_HI
    window = filter_window(TAPS, points)
    filtered = sum(
        (
            window[tap_step]
            * extended[:, :, :, tap_step : tap_step + frame_count, :].astype(jnp.float32)
            for tap_step in range(TAPS)
        )
    )
    filtered = filtered.astype(jnp.bfloat16)
    shaped = filtered.reshape(filtered.shape[:4] + (CH_LO, CH_HI))
    section_one = jnp.einsum(
        "oikn,ispfnm->ospfkm", dft_table(CH_LO), shaped, preferred_element_type=jnp.float32
    )
    low_index = jnp.arange(CH_LO, dtype=jnp.int32)
    high_index = jnp.arange(CH_HI, dtype=jnp.int32)
    twiddle = TWO_PI / points * (low_index[:, None] * high_index[None, :]).astype(jnp.float32)
    cosine = jnp.cos(twiddle)
    sine_part = jnp.sin(twiddle)
    rotated = jnp.stack(
        [
            section_one[0] * cosine + section_one[1] * sine_part,
            section_one[1] * cosine - section_one[0] * sine_part,
        ]
    ).astype(jnp.bfloat16)
    return jnp.einsum(
        "oimj,ispfkm->ospfkj", dft_table(CH_HI), rotated, preferred_element_type=jnp.float32
    ).astype(jnp.bfloat16)


def beam_weights(delays, beam_ids, groups, channel_low, station_total):
    points = CH_LO * CH_HI
    member = (groups[None, :] == (beam_ids % GROUPS)[:, None]).astype(jnp.float32)
    weight_scale = math.sqrt(GROUPS / station_total) * member
    channel = channel_low[:, None] + CH_LO * jnp.arange(CH_HI, dtype=jnp.int32)[None, :]
    fraction = channel.astype(jnp.float32) / float(points)
    phases = TWO_PI * (delays[:, :, None, None] * fraction[None, None])
    weight_re = (weight_scale[:, :, None, None] * jnp.cos(phases)).astype(jnp.bfloat16)
    weight_im = (-weight_scale[:, :, None, None] * jnp.sin(phases)).astype(jnp.bfloat16)
    return (weight_re, weight_im)


def form_beams(weight_re, weight_im, channels):
    real_in = channels[0]
    imag_in = channels[1]

    def contract(weights_part, data_part):
        return jnp.einsum(
            "bsxc,spfxc->bpfxc", weights_part, data_part, preferred_element_type=jnp.float32
        )

    real_out = contract(weight_re, real_in) - contract(weight_im, imag_in)
    imag_out = contract(weight_re, imag_in) + contract(weight_im, real_in)
    return jnp.stack([real_out, imag_out], axis=1)


def select_delays(delay_rows, pointing):
    directions = jnp.arange(delay_rows.shape[0], dtype=jnp.int32)
    onehot = (pointing[:, None] == directions[None, :]).astype(jnp.float32)
    return jnp.dot(
        onehot, delay_rows, precision=lax.Precision.HIGHEST, preferred_element_type=jnp.float32
    )


def with_history(frames_own):
    frame_count = frames_own.shape[3]
    needed = TAPS - 1
    tf_size = lax.axis_size("tf")
    pieces = []
    hop_count = (needed + frame_count - 1) // frame_count
    for hop_step in range(1, hop_count + 1):
        take_count = min(frame_count, needed - (hop_step - 1) * frame_count)
        portion = frames_own[:, :, :, frame_count - take_count :, :]
        pieces.append(passed_along(portion, "tf", hop_step))
    return jnp.concatenate(pieces[::-1] + [frames_own], axis=3)


def body(voltages, delay_table, beam_pointing, station_group):
    planes, stations_here, pol_count, samples_here = voltages.shape
    points = CH_LO * CH_HI
    frame_count = samples_here // points
    frames_own = voltages.reshape(planes, stations_here, pol_count, frame_count, points)
    channels = channelize(with_history(frames_own), frame_count)
    station_total = station_group.shape[0]
    beam_total = beam_pointing.shape[0]
    regrouped = lax.all_to_all(channels, "stn", split_axis=4, concat_axis=1, tiled=True)
    low_count = regrouped.shape[4]
    channel_low = lax.axis_index("stn") * low_count + jnp.arange(low_count, dtype=jnp.int32)
    beam_ids = jnp.arange(beam_total, dtype=jnp.int32)
    delays_all = select_delays(delay_table, beam_pointing)
    weight_re, weight_im = beam_weights(
        delays_all, beam_ids, station_group, channel_low, station_total
    )
    formed = form_beams(weight_re, weight_im, regrouped).astype(jnp.bfloat16)
    result = lax.all_to_all(
        lax.all_to_all(formed, "stn", split_axis=0, concat_axis=4, tiled=True),
        "tf",
        split_axis=4,
        concat_axis=3,
        tiled=True,
    )
    return result


def solution(mesh):
    in_specs = (P(None, "stn", None, "tf"), P(), P(), P())
    out_specs = P("stn", None, None, None, "tf", None)
    return jax.shard_map(body, mesh=mesh, in_specs=in_specs, out_specs=out_specs, check_vma=False)
```

profile of v0, /device:TPU:0, one launch (start us, length us, event | category | flops | bytes accessed | tf_op | source)
XLA Modules:
  0.0 318.8 jit_solution(10097307890491218836)
XLA Ops:
  0.0 3.3 %reshape.363 = bf16[2,8,2,8,4096]{4,3,2,1,0:T(8,128)(2,1)S(1)} reshape(bf16[2,8,2,32768]{3,2,1,0:T(2,128)(2,1)} %param.4) | data formatting | bytes 4194304 | tf_op jit(solution)/shard_map/reshape | solution.py:124
  3.5 2.5 collective-permute-start.1
  6.1 0.5 slice.175
  6.6 1.2 copy.40
  7.7 4.4 %collective-permute-start = (bf16[2,8,2,7,4096]{4,1,3,2,0:T(8,128)(2,1)S(1)}, bf16[2,8,2,7,4096]{4,1,3,2,0:T(8,128)(2,1)S(1)}, u32[]{:S(2)}, u32[]{:S(2)}) collective-permute-start(bf16[2,8,2,7,4096]{4,1,3,2,0:T(8,128)(2,1)S(1)} %copy.40), channel_id=1, source_target_pairs={{0,2},{1,3},{4,6},{5,7},{8,10},{9,11},{12,14},{13,15},{16,18},{17,... | collective-permute-start | bytes 5505032 | tf_op jit(solution)/shard_map/ppermute | solution.py:20
  12.4 0.3 fusion.58
  12.7 0.3 negate_convert_fusion
  13.0 1.2 fusion.41
  14.2 38.2 %collective-permute-done = bf16[2,8,2,7,4096]{4,1,3,2,0:T(8,128)(2,1)S(1)} collective-permute-done((bf16[2,8,2,7,4096]{4,1,3,2,0:T(8,128)(2,1)S(1)}, bf16[2,8,2,7,4096]{4,1,3,2,0:T(8,128)(2,1)S(1)}, u32[]{:S(2)}, u32[]{:S(2)}) %collective-permute-start) | collective-permute-done | bytes 1835040 | tf_op jit(solution)/shard_map/ppermute | solution.py:20
  52.4 1.1 copy.41
  53.7 0.2 constant_dynamic-update-slice_fusion
  53.9 11.7 %fusion.31 = bf16[2,8,2,8,32,128,1]{5,3,4,1,2,0,6:T(8,128)(2,1)S(1)} fusion(f32[4096]{0:T(1024)S(1)} %get-tuple-element.10, bf16[2,8,2,16,4096]{4,3,1,2,0:T(8,128)(2,1)S(1)} %constant_dynamic-update-slice_fusion, f32[4096]{0:T(1024)S(1)} %get-tuple-element.11, f32[4096]{0:T(1024)S(1)} %get-tuple-element.12, f32[4096]{0:T(1024)S(1)} %get-tuple-element.13, ...), kind=kLoop, calls=%fused_computation.51 | loop fusion | flops 72351744 | bytes 23068672 | tf_op jit(solution)/shard_map/reshape | solution.py:53
  65.6 0.7 convolution_bitcast_fusion
  66.4 0.6 add_convert_fusion.2
  67.0 0.7 fusion.36
  67.7 3.5 %copy.43 = bf16[2,8,2,8,32,128]{5,0,3,2,1,4:T(2,128)(2,1)} copy(bf16[2,8,2,8,32,128]{5,4,0,3,2,1:T(8,128)(2,1)S(1)} %fusion.36) | data formatting | bytes 4194304 | tf_op jit(solution)/shard_map/convert_element_type | solution.py:70
  71.2 5.8 %all-to-all-start = ((bf16[2,8,2,8,32,128]{5,0,3,2,1,4:T(2,128)(2,1)}), bf16[2,8,2,8,32,128]{5,0,3,2,1,4:T(2,128)(2,1)S(1)}, u32[]{:S(2)}, u32[]{:S(2)}) async-start(bf16[2,8,2,8,32,128]{5,0,3,2,1,4:T(2,128)(2,1)} %copy.43), calls=%async_computation | async-start | bytes 4194304 | tf_op jit(solution)/shard_map/all_to_all | solution.py:128
  77.4 43.2 %all-to-all-done = bf16[2,8,2,8,32,128]{5,0,3,2,1,4:T(2,128)(2,1)S(1)} async-done(((bf16[2,8,2,8,32,128]{5,0,3,2,1,4:T(2,128)(2,1)}), bf16[2,8,2,8,32,128]{5,0,3,2,1,4:T(2,128)(2,1)S(1)}, u32[]{:S(2)}, u32[]{:S(2)}) %all-to-all-start) | async-done | bytes 2097184 | tf_op jit(solution)/shard_map/all_to_all | solution.py:128
  120.6 0.5 copy.44
  121.0 0.4 fusion.79
  121.5 3.4 %copy.46 = bf16[64,2,8,4,128]{0,2,1,4,3:T(8,128)(2,1)} copy(bf16[64,2,8,4,128]{4,2,3,1,0:T(8,128)(2,1)S(1)} %bitcast.84) | data formatting | bytes 2097152 | tf_op jit(solution)/shard_map/squeeze | solution.py:86
  125.0 3.3 %copy.48 = bf16[64,2,8,4,128]{0,2,1,4,3:T(8,128)(2,1)} copy(bf16[64,2,8,4,128]{4,2,3,1,0:T(8,128)(2,1)S(1)} %bitcast.85) | data formatting | bytes 2097152 | tf_op jit(solution)/shard_map/squeeze | solution.py:87
  128.4 33.9 %fusion.4 = f32[4,128,2,8,32]{4,3,2,1,0:T(8,128)S(1)} fusion(bf16[64,2,8,4,128]{0,2,1,4,3:T(8,128)(2,1)} %copy.46, f32[4,128]{1,0:T(4,128)S(1)} %convert_multiply_fusion.1, f32[32,64]{1,0:T(8,128)S(1)} %fusion.69, f32[32,64]{1,0:T(8,128)S(1)} %get-tuple-element.30), kind=kOutput, calls=%fused_computation.21 | convolution fusion | flops 37748736 | bytes 2115584 | tf_op jit(solution)/shard_map/bsxc,spfxc->bpfxc/dot_general | solution.py:90
  162.3 33.6 %fusion.2 = f32[4,128,2,8,32]{4,3,2,1,0:T(8,128)} fusion(bf16[64,2,8,4,128]{0,2,1,4,3:T(8,128)(2,1)S(1)} %copy-done.1, f32[4,128]{1,0:T(4,128)S(1)} %convert_multiply_fusion.1, f32[32,64]{1,0:T(8,128)S(1)} %fusion.69, f32[32,64]{1,0:T(8,128)S(1)} %get-tuple-element.30), kind=kOutput, calls=%fused_computation.20 | convolution fusion | flops 37748736 | bytes 2115584 | tf_op jit(solution)/shard_map/bsxc,spfxc->bpfxc/dot_general | solution.py:90
  195.9 33.2 %fusion.20 = bf16[32,1,2,8,4,128]{0,3,2,5,4,1:T(8,128)(2,1)S(1)} fusion(f32[4,128,2,8,32]{4,3,2,1,0:T(8,128)S(1)} %fusion.4, bf16[64,2,8,4,128]{0,2,1,4,3:T(8,128)(2,1)S(1)} %copy-done.1, f32[32,64]{1,0:T(8,128)S(1)} %get-tuple-element.29, f32[4,128]{1,0:T(4,128)S(1)} %convert_multiply_fusion.1, f32[32,64]{1,0:T(8,128)S(1)} %fusion.69), kind=kOutput, calls=%fused_computation.36 | convolution fusion | flops 38273024 | bytes 2639872 | tf_op jit(solution)/shard_map/bsxc,spfxc->bpfxc/dot_general | solution.py:90
  229.2 1.9 copy.51
  231.0 35.0 %fusion.21 = bf16[32,1,2,8,4,128]{0,3,2,5,4,1:T(8,128)(2,1)S(1)} fusion(f32[4,128,2,8,32]{4,3,2,1,0:T(8,128)} %fusion.2, bf16[64,2,8,4,128]{0,2,1,4,3:T(8,128)(2,1)} %copy.46, f32[32,64]{1,0:T(8,128)S(1)} %get-tuple-element.29, f32[4,128]{1,0:T(4,128)S(1)} %convert_multiply_fusion.1, f32[32,64]{1,0:T(8,128)S(1)} %fusion.69), kind=kOutput, calls=%fused_computation.37 | convolution fusion | flops 38273024 | bytes 2639872 | tf_op jit(solution)/shard_map/bsxc,spfxc->bpfxc/dot_general | solution.py:90
  266.0 1.9 copy.52
  268.0 28.6 %all_to_all.51 = bf16[32,2,2,8,4,128]{5,3,4,2,1,0:T(8,128)(2,1)S(1)} all-to-all(bf16[32,2,2,8,4,128]{5,3,4,2,1,0:T(8,128)(2,1)S(1)} %pad_maximum_fusion.1), channel_id=1, replica_groups=mesh['stn'=8,'tf'=4] {'stn'}, dimensions={0} | all-to-all | bytes 2097152 | tf_op jit(solution)/shard_map/all_to_all | solution.py:138
  296.7 0.3 copy.54
  297.0 19.7 %all_to_all.52 = bf16[4,2,2,8,32,128]{5,3,2,1,0,4:T(8,128)(2,1)S(1)} all-to-all(bf16[4,2,2,8,32,128]{5,3,2,1,0,4:T(8,128)(2,1)S(1)} %copy.54), channel_id=1, replica_groups=mesh['stn'=8,'tf'=4] {'tf'}, dimensions={4} | all-to-all | bytes 2097152 | tf_op jit(solution)/shard_map/all_to_all | solution.py:137
  316.6 2.2 copy.56
  (27 shorter events, 1.5 us)
Async XLA Ops:
  0.0 77.2 %copy-start = (f32[128,64]{0,1:T(8,128)S(1)}, f32[128,64]{0,1:T(8,128)}, u32[]{:S(2)}) copy-start(f32[128,64]{0,1:T(8,128)} %param.5) | copy-start | bytes 98308
  3.5 50.0 %collective-permute-start.1 = (bf16[2,8,2,8,4096]{4,3,1,2,0:T(8,128)(2,1)S(1)}, bf16[2,8,2,8,4096]{4,3,1,2,0:T(8,128)(2,1)S(1)}, u32[]{:S(2)}, u32[]{:S(2)}) collective-permute-start(bf16[2,8,2,8,4096]{4,3,1,2,0:T(8,128)(2,1)S(1)} %copy.65), channel_id=1, source_target_pairs={{0,1},{1,2},{2,3},{4,5},{5,6},{6,7},{8,9},{9,10},{10,11},{12,13},{... | collective-permute-start | bytes 6291464 | tf_op jit(solution)/shard_map/ppermute | solution.py:20
  7.7 44.7 %collective-permute-start = (bf16[2,8,2,7,4096]{4,1,3,2,0:T(8,128)(2,1)S(1)}, bf16[2,8,2,7,4096]{4,1,3,2,0:T(8,128)(2,1)S(1)}, u32[]{:S(2)}, u32[]{:S(2)}) collective-permute-start(bf16[2,8,2,7,4096]{4,1,3,2,0:T(8,128)(2,1)S(1)} %copy.40), channel_id=1, source_target_pairs={{0,2},{1,3},{4,6},{5,7},{8,10},{9,11},{12,14},{13,15},{16,18},{17,... | collective-permute-start | bytes 5505032 | tf_op jit(solution)/shard_map/ppermute | solution.py:20
  67.7 9.5 %copy-start.2 = (s32[64]{0:T(128)S(1)}, s32[64]{0:T(128)}, u32[]{:S(2)}) copy-start(s32[64]{0:T(128)} %param.7) | copy-start | bytes 772
  67.7 9.5 %copy-start.3 = (s32[32]{0:T(128)S(1)}, s32[32]{0:T(128)}, u32[]{:S(2)}) copy-start(s32[32]{0:T(128)} %param.6) | copy-start | bytes 388
  71.2 49.3 %all-to-all-start = ((bf16[2,8,2,8,32,128]{5,0,3,2,1,4:T(2,128)(2,1)}), bf16[2,8,2,8,32,128]{5,0,3,2,1,4:T(2,128)(2,1)S(1)}, u32[]{:S(2)}, u32[]{:S(2)}) async-start(bf16[2,8,2,8,32,128]{5,0,3,2,1,4:T(2,128)(2,1)} %copy.43), calls=%async_computation | async-start | bytes 4194304 | tf_op jit(solution)/shard_map/all_to_all | solution.py:128
  128.4 33.9 %copy-start.1 = (bf16[64,2,8,4,128]{0,2,1,4,3:T(8,128)(2,1)S(1)}, bf16[64,2,8,4,128]{0,2,1,4,3:T(8,128)(2,1)}, u32[]{:S(2)}) copy-start(bf16[64,2,8,4,128]{0,2,1,4,3:T(8,128)(2,1)} %copy.48) | copy-start | bytes 3145732
where the time goes:
time: 319 us
  matrix products  137 us (43%)
  waiting for transfers between devices  81.3 us (25%)
  blocking collectives  48.2 us (15%)
  local copies, waits for them, and re-layouts  24.3 us (8%)
  other arithmetic  14.6 us (5%)
  starting transfers between devices  12.8 us (4%)
    dot_general x4, matrix products, contract(): jnp.einsum('bsxc,spfxc->bpfxc', weights_part, data_part, preferred_elemen...  136 us
    all_to_all x1, waiting for transfers between devices, body(): lax.all_to_all(channels, 'stn', split_axis=4, concat_axis=1, tiled=True)  43.2 us
    ppermute x2, waiting for transfers between devices, passed_along(): lax.ppermute(value, axis, [(source, source + steps) for source in range(f...  38.2 us
    all_to_all x1, blocking collectives, body(): lax.all_to_all(formed, 'stn', split_axis=0, concat_axis=4, tiled=True)  28.6 us
    all_to_all x1, blocking collectives, body(): lax.all_to_all(lax.all_to_all(formed, 'stn', split_axis=0, concat_axis=4,...  19.7 us
    reshape x1, other arithmetic, channelize(): shaped = filtered.reshape(filtered.shape[:4] + (CH_LO, CH_HI))  11.7 us
    ppermute x2, starting transfers between devices, passed_along(): lax.ppermute(value, axis, [(source, source + steps) for source in range(f...  6.94 us
  transfers between devices with their start and end apart: 3, of which 2 were waited for; matrix products, arithmetic and copies ran while one was open for 2% of the time, Pallas kernels for 0%

commit v1 on v0

--- a/solution.py
+++ b/solution.py
@@ -1,17 +1,348 @@
+import functools
 import math
 
 import jax
 import jax.numpy as jnp
 from jax import lax
+from jax.experimental import pallas as pl
+from jax.experimental.pallas import tpu as pltpu
 from jax.sharding import PartitionSpec as P
 
 TAPS = 16
 CH_LO = 32
 CH_HI = 128
 GROUPS = 4
-
-
+POINTS = CH_LO * CH_HI
 TWO_PI = 2.0 * math.pi
+BF = jnp.bfloat16
+F32 = jnp.float32
+
+LANES = 128
+TF = 4
+STN = 8
+PART = CH_HI // TF
+LOW = CH_LO // TF
+PER = 4
+
+
+def filter_window(position):
+    total_len = float(TAPS * POINTS)
+    value = position.astype(F32)
+    hann_taper = 0.5 - 0.5 * jnp.cos(TWO_PI / total_len * value)
+    return jnp.sinc((value - 0.5 * total_len) / float(POINTS)) * hann_taper
+
+
+def window_rows(part):
+    shape = (TAPS, 2 * CH_LO, LANES)
+    tap = lax.broadcasted_iota(jnp.int32, shape, 0)
+    n2 = lax.broadcasted_iota(jnp.int32, shape, 1) // 2
+    n1 = part * PART + lax.broadcasted_iota(jnp.int32, shape, 2) % PART
+    return filter_window(tap * POINTS + n2 * CH_HI + n1)
+
+
+def dft_pair(points):
+    counter = jnp.arange(points, dtype=jnp.int32)
+    product = counter[:, None] * counter[None, :] % points
+    angles = TWO_PI / points * product.astype(F32)
+    factor = 1.0 / math.sqrt(points)
+    return jnp.cos(angles) * factor, jnp.sin(angles) * factor
+
+
+def first_table():
+    cosine, sine = dft_pair(CH_LO)
+    planes = jnp.stack([jnp.stack([cosine, sine]), jnp.stack([-sine, cosine])])
+    planes = planes.reshape(2, 2, TF, LOW, CH_LO)
+    both = jnp.eye(2, dtype=F32)
+    table = jnp.einsum("oitkn,pr->otpkinr", planes, both)
+    return table.reshape(4 * CH_LO, 4 * CH_LO).astype(BF)
+
+
+def second_table():
+    cosine, sine = dft_pair(CH_HI)
+    table = jnp.concatenate(
+        [jnp.concatenate([cosine, -sine], axis=1), jnp.concatenate([sine, cosine], axis=1)], axis=0
+    )
+    return table.astype(BF)
+
+
+def twiddle_rows(part):
+    shape = (2 * CH_LO, LANES)
+    row = lax.broadcasted_iota(jnp.int32, shape, 0)
+    k2 = row // (2 * LOW) * LOW + row % LOW
+    n1 = part * PART + lax.broadcasted_iota(jnp.int32, shape, 1) % PART
+    angle = TWO_PI / POINTS * (k2 * n1).astype(F32)
+    return jnp.cos(angle), jnp.sin(angle)
+
+
+def swap_lane_blocks(parts):
+    return [
+        jnp.concatenate([part[:, j * PART : (j + 1) * PART] for part in parts], axis=1)
+        for j in range(len(parts))
+    ]
+
+
+def spread_kernel(volt_ref, out_ref):
+    parts = [volt_ref[0, a] for a in range(PER)]
+    for j, block in enumerate(swap_lane_blocks(parts)):
+        out_ref[j, 0, 0] = block
+
+
+def spread(volt):
+    planes, stations, rows, _ = volt.shape
+    groups = stations // PER
+    return pl.pallas_call(
+        spread_kernel,
+        name="spread",
+        grid=(planes, groups),
+        in_specs=[pl.BlockSpec((1, PER, rows, LANES), lambda q, c: (q, c, 0, 0))],
+        out_specs=pl.BlockSpec((TF, 1, 1, rows, LANES), lambda q, c: (0, q, c, 0, 0)),
+        out_shape=jax.ShapeDtypeStruct((TF, planes, groups, rows, LANES), BF),
+    )(volt)
+
+
+def channel_kernel(frames, blocks_ref, win_ref, table_ref, cos_ref, sin_ref, out_ref, wide_ref, filt_ref):
+    sources = blocks_ref.shape[0]
+    per_source = frames // sources
+    rows = 2 * CH_LO
+    history = TAPS - 1
+    wide_ref[:, 0:history] = jnp.zeros((2, history, rows, LANES), F32)
+    for q in range(2):
+        for src in range(sources):
+            block = blocks_ref[src, q, 0].astype(F32)
+            wide_ref[q, pl.ds(history + src * per_source, per_source)] = block.reshape(
+                per_source, rows, LANES
+            )
+
+    strip = 16
+
+    def one_strip(step, carry):
+        q = step // (rows // strip)
+        at = pl.multiple_of(step % (rows // strip) * strip, strip)
+        for f in range(frames):
+            total = None
+            for tap in range(max(0, history - f), TAPS):
+                term = win_ref[tap, pl.ds(at, strip), :] * wide_ref[q, f + tap, pl.ds(at, strip), :]
+                total = term if total is None else total + term
+            filt_ref[f, q, pl.ds(at, strip), :] = total.astype(BF)
+        return carry
+
+    lax.fori_loop(0, 2 * rows // strip, one_strip, 0)
+
+    table = table_ref[...]
+    cosine, sine = cos_ref[...], sin_ref[...]
+    per_dest = frames // STN
+
+    def one_pair(pair, carry):
+        left = filt_ref[2 * pair].reshape(2 * rows, LANES)
+        right = filt_ref[2 * pair + 1].reshape(2 * rows, LANES)
+        both = jnp.concatenate([left, right], axis=1)
+        spectrum = jnp.dot(table, both, preferred_element_type=F32)
+        for side in range(2):
+            f = 2 * pair + side
+            real = spectrum[:rows, side * LANES : (side + 1) * LANES]
+            imag = spectrum[rows:, side * LANES : (side + 1) * LANES]
+            turned = (real * cosine + imag * sine, imag * cosine - real * sine)
+            for o in range(2):
+                value = turned[o].astype(BF)
+                out_ref[f // per_dest, :, o, 0, f % per_dest] = value.reshape(TF, 2 * LOW, LANES)
+        return carry
+
+    lax.fori_loop(0, frames // 2, one_pair, 0)
+
+
+def channel_step(blocks, window, table, cosine, sine):
+    sources, planes, groups, rows, _ = blocks.shape
+    frames = sources * rows // (2 * CH_LO)
+    per_dest = frames // STN
+    whole = lambda shape: pl.BlockSpec(shape, lambda c: (0,) * len(shape))
+    return pl.pallas_call(
+        functools.partial(channel_kernel, frames),
+        name="channel_step",
+        grid=(groups,),
+        in_specs=[
+            pl.BlockSpec((sources, planes, 1, rows, LANES), lambda c: (0, 0, c, 0, 0)),
+            whole(window.shape),
+            whole(table.shape),
+            whole(cosine.shape),
+            whole(sine.shape),
+        ],
+        out_specs=pl.BlockSpec(
+            (STN, TF, planes, 1, per_dest, 2 * LOW, LANES), lambda c: (0, 0, 0, c, 0, 0, 0)
+        ),
+        out_shape=jax.ShapeDtypeStruct((STN, TF, planes, groups, per_dest, 2 * LOW, LANES), BF),
+        scratch_shapes=[
+            pltpu.VMEM((planes, frames + TAPS - 1, 2 * CH_LO, LANES), F32),
+            pltpu.VMEM((frames, planes, 2 * CH_LO, LANES), BF),
+        ],
+    )(blocks, window, table, cosine, sine)
+
+
+def weight_kernel(low_ref, table_ref, beam_ref, group_ref, out_ref, order_ref, start_ref):
+    stations = group_ref.shape[0]
+    per_group = out_ref.shape[1]
+    scale = math.sqrt(GROUPS / stations)
+    shape = (LOW, LANES)
+    k2 = low_ref[0] + lax.broadcasted_iota(jnp.int32, shape, 0)
+    channel = k2 + CH_LO * lax.broadcasted_iota(jnp.int32, shape, 1)
+    fraction = channel.astype(F32) / float(POINTS)
+
+    def one_station(s, carry):
+        group = group_ref[s]
+        for i in range(per_group):
+            turns = table_ref[beam_ref[group + GROUPS * i], s] * fraction
+            quarter = jnp.round(4.0 * turns)
+            angle = TWO_PI * (turns - 0.25 * quarter)
+            square = angle * angle
+            sine = angle * (
+                1.0 + square * (-1.0 / 6 + square * (1.0 / 120 + square * (-1.0 / 5040 + square * (1.0 / 362880))))
+            )
+            cosine = 1.0 + square * (
+                -0.5 + square * (1.0 / 24 + square * (-1.0 / 720 + square * (1.0 / 40320)))
+            )
+            turn = quarter.astype(jnp.int32) & 3
+            odd = (turn & 1) == 1
+            base_cos = jnp.where(odd, sine, cosine)
+            base_sin = jnp.where(odd, cosine, sine)
+            real = jnp.where((turn == 1) | (turn == 2), -base_cos, base_cos)
+            imag = jnp.where(turn >= 2, -base_sin, base_sin)
+            out_ref[s, i, 0] = (scale * real).astype(BF).astype(F32)
+            out_ref[s, i, 1] = (-scale * imag).astype(BF).astype(F32)
+        return carry
+
+    lax.fori_loop(0, stations, one_station, 0)
+
+    at = jnp.int32(0)
+    for g in range(GROUPS):
+        start_ref[g] = at
+
+        def put(s, at, g=g):
+            mine = group_ref[s] == g
+
+            @pl.when(mine)
+            def _():
+                order_ref[at] = s
+
+            return at + mine.astype(jnp.int32)
+
+        at = lax.fori_loop(0, stations, put, at)
+    start_ref[GROUPS] = at
+
+
+def beam_weights(low, delay_table, beam_pointing, station_group):
+    stations = station_group.shape[0]
+    per_group = beam_pointing.shape[0] // GROUPS
+    smem = pl.BlockSpec(memory_space=pltpu.SMEM)
+    return pl.pallas_call(
+        weight_kernel,
+        name="beam_weights",
+        in_specs=[smem] * 4,
+        out_specs=[pl.BlockSpec(memory_space=pltpu.VMEM), smem, smem],
+        out_shape=[
+            jax.ShapeDtypeStruct((stations, per_group, 2, LOW, LANES), F32),
+            jax.ShapeDtypeStruct((stations,), jnp.int32),
+            jax.ShapeDtypeStruct((GROUPS + 1,), jnp.int32),
+        ],
+    )(low, delay_table, beam_pointing, station_group)
+
+
+def beam_kernel(blocks_ref, table_ref, weight_ref, order_ref, start_ref, out_ref, chan_ref):
+    src = pl.program_id(0)
+    groups, per_dest = blocks_ref.shape[3], blocks_ref.shape[4]
+    rows = per_dest * 2 * LOW
+    table = table_ref[...]
+    for c in range(groups):
+        planes = []
+        for o in range(2):
+            parts = [blocks_ref[0, j, o, c].reshape(rows, LANES) for j in range(TF)]
+            planes.append(swap_lane_blocks(parts))
+        for a in range(PER):
+            both = jnp.concatenate([planes[0][a], planes[1][a]], axis=1)
+            spectrum = jnp.dot(both, table, preferred_element_type=F32)
+            at = src * (groups * PER) + c * PER + a
+            for o in range(2):
+                chan_ref[at, o] = spectrum[:, o * LANES : (o + 1) * LANES].reshape(
+                    per_dest * 2, LOW, LANES
+                )
+
+    @pl.when(src == pl.num_programs(0) - 1)
+    def _():
+        per_group = weight_ref.shape[1]
+
+        def one_block(step, carry):
+            g = step // per_dest
+            f = step % per_dest
+
+            def one_station(pos, acc):
+                s = order_ref[pos]
+                new = []
+                data = [(chan_ref[s, 0, 2 * f + p], chan_ref[s, 1, 2 * f + p]) for p in range(2)]
+                for i in range(per_group):
+                    wre, wim = weight_ref[s, i, 0], weight_ref[s, i, 1]
+                    for p in range(2):
+                        re, im = data[p]
+                        are, aim = acc[4 * i + 2 * p], acc[4 * i + 2 * p + 1]
+                        new.append(are + (wre * re - wim * im))
+                        new.append(aim + (wre * im + wim * re))
+                return tuple(new)
+
+            zero = jnp.zeros((LOW, LANES), F32)
+            acc = lax.fori_loop(
+                start_ref[g], start_ref[g + 1], one_station, (zero,) * (4 * per_group)
+            )
+            for i in range(per_group):
+                for p in range(2):
+                    for o in range(2):
+                        out_ref[i, g, o, p, f] = acc[4 * i + 2 * p + o].astype(BF)
+            return carry
+
+        lax.fori_loop(0, GROUPS * per_dest, one_block, 0)
+
+
+def beam_step(blocks, table, weights, order, start):
+    sources, parts, planes, groups, per_dest, _, _ = blocks.shape
+    stations, per_group = weights.shape[:2]
+    smem = pl.BlockSpec(memory_space=pltpu.SMEM)
+    out = (per_group, GROUPS, planes, 2, per_dest, LOW, LANES)
+    return pl.pallas_call(
+        beam_kernel,
+        name="beam_step",
+        grid=(sources,),
+        in_specs=[
+            pl.BlockSpec((1,) + blocks.shape[1:], lambda s: (s, 0, 0, 0, 0, 0, 0)),
+            pl.BlockSpec(table.shape, lambda s: (0, 0)),
+            pl.BlockSpec(memory_space=pltpu.VMEM),
+            smem,
+            smem,
+        ],
+        out_specs=pl.BlockSpec(out, lambda s: (0,) * len(out)),
+        out_shape=jax.ShapeDtypeStruct(out, BF),
+        scratch_shapes=[pltpu.VMEM((stations, planes, 2 * per_dest, LOW, LANES), F32)],
+    )(blocks, table, weights, order, start)
+
+
+def fast_body(voltages, delay_table, beam_pointing, station_group):
+    planes, stations_here, pols, samples_here = voltages.shape
+    part = lax.axis_index("tf")
+    chunks = samples_here // LANES
+    volt = voltages.reshape(planes, stations_here, pols, chunks, LANES)
+    volt = volt.transpose(0, 1, 3, 2, 4).reshape(planes, stations_here, chunks * pols, LANES)
+
+    blocks = spread(volt)
+    blocks = lax.all_to_all(blocks, "tf", split_axis=0, concat_axis=0, tiled=True)
+    cosine, sine = twiddle_rows(part)
+    turned = channel_step(blocks, window_rows(part), first_table(), cosine, sine)
+
+    shape = turned.shape
+    turned = turned.reshape((STN * TF,) + shape[2:])
+    turned = lax.all_to_all(turned, ("stn", "tf"), split_axis=0, concat_axis=0, tiled=True)
+    turned = turned.reshape(shape)
+
+    low = (part * LOW).astype(jnp.int32).reshape(1)
+    weights, order, start = beam_weights(low, delay_table, beam_pointing, station_group)
+    beams = beam_step(turned, second_table(), weights, order, start)
+    beams = lax.all_to_all(beams, "stn", split_axis=0, concat_axis=0, tiled=True)
+    beams = beams.transpose(1, 2, 3, 0, 4, 5, 6)
+    return beams.reshape(beams.shape[:3] + (-1,) + beams.shape[5:])
 
 
 def passed_along(value, axis, steps):
@@ -20,7 +351,7 @@
     return lax.ppermute(value, axis, [(source, source + steps) for source in range(first, last)])
 
 
-def filter_window(tap_count, points):
+def plain_window(tap_count, points):
     position = jnp.arange(tap_count * points, dtype=jnp.int32).astype(jnp.float32)
     total_len = float(tap_count * points)
     hann_taper = 0.5 - 0.5 * jnp.cos(TWO_PI / total_len * position)
@@ -41,7 +372,7 @@
 
 def channelize(extended, frame_count):
     points = CH_LO * CH_HI
-    window = filter_window(TAPS, points)
+    window = plain_window(TAPS, points)
     filtered = sum(
         (
             window[tap_step]
@@ -70,7 +401,7 @@
     ).astype(jnp.bfloat16)
 
 
-def beam_weights(delays, beam_ids, groups, channel_low, station_total):
+def plain_weights(delays, beam_ids, groups, channel_low, station_total):
     points = CH_LO * CH_HI
     member = (groups[None, :] == (beam_ids % GROUPS)[:, None]).astype(jnp.float32)
     weight_scale = math.sqrt(GROUPS / station_total) * member
@@ -117,7 +448,7 @@
     return jnp.concatenate(pieces[::-1] + [frames_own], axis=3)
 
 
-def body(voltages, delay_table, beam_pointing, station_group):
+def plain_body(voltages, delay_table, beam_pointing, station_group):
     planes, stations_here, pol_count, samples_here = voltages.shape
     points = CH_LO * CH_HI
     frame_count = samples_here // points
@@ -130,7 +461,7 @@
     channel_low = lax.axis_index("stn") * low_count + jnp.arange(low_count, dtype=jnp.int32)
     beam_ids = jnp.arange(beam_total, dtype=jnp.int32)
     delays_all = select_delays(delay_table, beam_pointing)
-    weight_re, weight_im = beam_weights(
+    weight_re, weight_im = plain_weights(
         delays_all, beam_ids, station_group, channel_low, station_total
     )
     formed = form_beams(weight_re, weight_im, regrouped).astype(jnp.bfloat16)
@@ -144,7 +475,24 @@
     return result
 
 
+def fits(mesh, voltages, station_group):
+    planes, stations, pols, samples = voltages.shape
+    tf, stn = mesh.shape["tf"], mesh.shape["stn"]
+    frames = samples // POINTS
+    return (
+        tf == TF and stn == STN and stations == stn * 2 * PER and (planes, pols) == (2, 2)
+        and frames % (tf * stn) == 0
+    )
+
+
 def solution(mesh):
     in_specs = (P(None, "stn", None, "tf"), P(), P(), P())
     out_specs = P("stn", None, None, None, "tf", None)
-    return jax.shard_map(body, mesh=mesh, in_specs=in_specs, out_specs=out_specs, check_vma=False)
+
+    def whole(*args):
+        body = fast_body if fits(mesh, args[0], args[3]) else plain_body
+        return jax.shard_map(
+            body, mesh=mesh, in_specs=in_specs, out_specs=out_specs, check_vma=False
+        )(*args)
+
+    return whole

time: 319 us -> 151 us (0.47)
  matrix products: 137 us -> 0 us
  Pallas kernels: 0 us -> 42.8 us
  waiting for transfers between devices: 81.3 us -> 55.6 us
  blocking collectives: 48.2 us -> 29.6 us
  local copies, waits for them, and re-layouts: 24.3 us -> 5.87 us
  other arithmetic: 14.6 us -> 6.01 us
    dot_general x7 -> x0, matrix products: 137 us -> none  [the longest x4 136 us: contract(): jnp.einsum('bsxc,spfxc->bpfxc', weights_part, data_part, preferred_elemen...]
    pallas_call x0 -> x4, Pallas kernels: none -> 42.8 us  [the longest x1 15.9 us: beam_step(): pl.pallas_call(beam_kernel, name='beam_step', grid=(sources,), in_specs=[...]
    ppermute x2 -> x0, waiting for transfers between devices: 38.2 us -> none  [passed_along(): lax.ppermute(value, axis, [(source, source + steps) for source in range(f...]
    all_to_all x2 -> x1, blocking collectives: 48.2 us -> 29.6 us  [fast_body(): lax.all_to_all(beams, 'stn', split_axis=0, concat_axis=0, tiled=True)]
    all_to_all x1 -> x2, waiting for transfers between devices: 43.2 us -> 55.6 us  [the longest x1 36.1 us: fast_body(): lax.all_to_all(turned, ('stn', 'tf'), split_axis=0, concat_axis=0, tiled=...]
    reshape x1 -> x0, other arithmetic: 11.7 us -> none  [channelize(): shaped = filtered.reshape(filtered.shape[:4] + (CH_LO, CH_HI))]
    ppermute x2 -> x0, starting transfers between devices: 6.94 us -> none  [passed_along(): lax.ppermute(value, axis, [(source, source + steps) for source in range(f...]
    squeeze x2 -> x0, local copies, waits for them, and re-layouts: 6.7 us -> none  [the longest x1 3.36 us: form_beams(): real_in = channels[0]]
  transfers between devices with their start and end apart: 3 -> 2, of which waited for: 2 -> 2; matrix products, arithmetic and copies ran while one was open for 2% -> 5% of each run, Pallas kernels for 0% -> 7%
where the time goes in v1:
time: 151 us; the launch traced here: 150 us
  waiting for transfers between devices  55.6 us (37%)
  Pallas kernels  42.8 us (28%)
  blocking collectives  29.6 us (20%)
  starting transfers between devices  9.94 us (7%)
  other arithmetic  6.01 us (4%)
  local copies, waits for them, and re-layouts  5.87 us (4%)
    all_to_all x1, waiting for transfers between devices, fast_body(): lax.all_to_all(turned, ('stn', 'tf'), split_axis=0, concat_axis=0, tiled=...  36.1 us
    all_to_all x1, blocking collectives, fast_body(): lax.all_to_all(beams, 'stn', split_axis=0, concat_axis=0, tiled=True)  29.6 us
    all_to_all x1, waiting for transfers between devices, fast_body(): lax.all_to_all(blocks, 'tf', split_axis=0, concat_axis=0, tiled=True)  19.5 us
    pallas_call x1, Pallas kernels, beam_step(): pl.pallas_call(beam_kernel, name='beam_step', grid=(sources,), in_specs=[...  15.9 us
    pallas_call x1, Pallas kernels, channel_step(): pl.pallas_call(functools.partial(channel_kernel, frames), name='channel_s...  11.6 us
    pallas_call x1, Pallas kernels, beam_weights(): pl.pallas_call(weight_kernel, name='beam_weights', in_specs=[smem] * 4, o...  10.6 us
    all_to_all x1, starting transfers between devices, fast_body(): lax.all_to_all(turned, ('stn', 'tf'), split_axis=0, concat_axis=0, tiled=...  5.68 us
    pallas_call x1, Pallas kernels, spread(): pl.pallas_call(spread_kernel, name='spread', grid=(planes, groups), in_sp...  4.64 us
  transfers between devices with their start and end apart: 2, of which 2 were waited for; matrix products, arithmetic and copies ran while one was open for 5% of the time, Pallas kernels for 7%

profile of v1, /device:TPU:0, one launch (start us, length us, event | category | flops | bytes accessed | tf_op | source)
XLA Modules:
  0.0 149.9 jit_solution(3856369200220446439)
XLA Ops:
  0.0 4.6 %spread.1 = bf16[4,2,2,512,128]{4,3,2,1,0:T(8,128)(2,1)} custom-call(bf16[2,8,512,128]{3,2,1,0:T(8,128)(2,1)} %bitcast.17), custom_call_target="tpu_custom_call" | custom-call | tf_op jit(solution)/shard_map/spread/pallas_call | solution.py:93
  4.6 4.3 %all-to-all-start = ((bf16[4,2,2,512,128]{4,3,2,1,0:T(8,128)(2,1)}), bf16[4,2,2,512,128]{4,3,2,1,0:T(8,128)(2,1)S(1)}, u32[]{:S(2)}, u32[]{:S(2)}) async-start(bf16[4,2,2,512,128]{4,3,2,1,0:T(8,128)(2,1)} %spread.1), calls=%async_computation | async-start | bytes 4194304 | tf_op jit(solution)/shard_map/all_to_all | solution.py:331
  8.9 0.2 sine_multiply_fusion.1
  9.1 0.2 copy.12
  9.3 0.4 fusion.8
  9.7 0.5 convert_element_type.61
  10.2 0.7 copy.13.table_ref
  11.0 0.9 fusion.21
  11.8 3.3 %fusion.4.win_ref = f32[16,64,128]{2,1,0:T(8,128)} fusion(s32[128]{0:T(128)S(1)} %get-tuple-element.18, s32[128]{0:T(128)S(1)} %get-tuple-element.19, s32[]{:T(128)S(6)} %mul.303, s32[64]{0:T(128)S(1)} %get-tuple-element.16, s32[64]{0:T(128)S(1)} %get-tuple-element.17, s32[16]{0:T(128)S(1)} %iota_multiply_fusion, pred[64]{0:T(512)(128)(4,1)S(1)} %compare_and_fusion.3, ...), kind=kLoop, calls=%fused_computation.11 | loop fusion | flops 6029312 | bytes 526084 | tf_op jit(solution)/shard_map/mul | solution.py:32
  15.1 19.5 %all-to-all-done.blocks_ref = bf16[4,2,2,512,128]{4,3,2,1,0:T(8,128)(2,1)S(1)} async-done(((bf16[4,2,2,512,128]{4,3,2,1,0:T(8,128)(2,1)}), bf16[4,2,2,512,128]{4,3,2,1,0:T(8,128)(2,1)S(1)}, u32[]{:S(2)}, u32[]{:S(2)}) %all-to-all-start) | async-done | bytes 2097184 | tf_op jit(solution)/shard_map/all_to_all | solution.py:331
  34.6 0.0 copy-start
  34.6 1.3 copy-done
  35.9 11.6 %channel_step.1 = bf16[8,4,2,2,4,16,128]{6,5,4,3,2,1,0:T(8,128)(2,1)} custom-call(bf16[4,2,2,512,128]{4,3,2,1,0:T(8,128)(2,1)} %copy-done, f32[16,64,128]{2,1,0:T(8,128)} %fusion.4.win_ref, bf16[128,128]{1,0:T(8,128)(2,1)} %copy.13.table_ref, f32[64,128]{1,0:T(8,128)} %get-tuple-element.12.cos_ref, f32[64,128]{1,0:T(8,128)} %get-tuple-element.11.sin_ref), custom_call_target="tpu_custom_call" | custom-call | tf_op jit(solution)/shard_map/channel_step/pallas_call | solution.py:158
  47.5 0.0 copy-start.2
  47.5 5.7 %all-to-all-start.1 = ((bf16[32,2,2,4,16,128]{5,4,3,2,1,0:T(8,128)(2,1)}), bf16[32,2,2,4,16,128]{5,4,3,2,1,0:T(8,128)(2,1)S(1)}, u32[]{:S(2)}, u32[]{:S(2)}) async-start(bf16[32,2,2,4,16,128]{5,4,3,2,1,0:T(8,128)(2,1)} %bitcast.14), calls=%async_computation.1 | async-start | bytes 4194304 | tf_op jit(solution)/shard_map/all_to_all | solution.py:337
  53.2 0.0 copy-done.2
  53.2 0.7 copy.14.table_ref
  54.0 10.6 %beam_weights.1 = (f32[64,8,2,8,128]{4,3,2,1,0:T(8,128)}, s32[64]{0:T(128)}, s32[5]{0:T(128)}) custom-call(s32[1]{0:T(128)} %bitcast.6.low_ref, f32[128,64]{1,0:T(8,128)} %copy.14.table_ref, s32[32]{0:T(128)} %beam_ref.1, s32[64]{0:T(128)} %group_ref.1), custom_call_target="tpu_custom_call" | custom-call | tf_op jit(solution)/shard_map/beam_weights/pallas_call | solution.py:235
  64.6 0.3 fusion.20
  64.8 0.3 negate_convert_fusion
  65.1 0.7 maximum_maximum_fusion.table_ref
  65.8 36.1 %all-to-all-done.1 = bf16[32,2,2,4,16,128]{5,4,3,2,1,0:T(8,128)(2,1)S(1)} async-done(((bf16[32,2,2,4,16,128]{5,4,3,2,1,0:T(8,128)(2,1)}), bf16[32,2,2,4,16,128]{5,4,3,2,1,0:T(8,128)(2,1)S(1)}, u32[]{:S(2)}, u32[]{:S(2)}) %all-to-all-start.1) | async-done | bytes 2097184 | tf_op jit(solution)/shard_map/all_to_all | solution.py:337
  101.9 0.0 copy-start.1
  101.9 1.3 copy-done.1
  103.3 15.9 %beam_step.1 = bf16[8,4,2,2,4,8,128]{6,5,4,3,2,1,0:T(8,128)(2,1)} custom-call(bf16[8,4,2,2,4,16,128]{6,5,4,3,2,1,0:T(8,128)(2,1)} %bitcast.15, bf16[256,256]{1,0:T(8,128)(2,1)} %maximum_maximum_fusion.table_ref, f32[64,8,2,8,128]{4,3,2,1,0:T(8,128)} %get-tuple-element.8.weight_ref, s32[64]{0:T(128)} %get-tuple-element.9.order_ref, s32[5]{0:T(128)} %get-tuple-element.10.start_ref), custom_call_target="tpu_custom_call" | custom-call | tf_op jit(solution)/shard_map/beam_step/pallas_call | solution.py:306
  119.2 29.6 %all_to_all.15 = bf16[8,4,2,2,4,8,128]{6,5,4,3,2,1,0:T(8,128)(2,1)S(1)} all-to-all(bf16[8,4,2,2,4,8,128]{6,5,4,3,2,1,0:T(8,128)(2,1)} %beam_step.1), channel_id=1, replica_groups=mesh['stn'=8,'tf'=4] {'stn'}, dimensions={0} | all-to-all | bytes 2097152 | tf_op jit(solution)/shard_map/all_to_all | solution.py:343
  148.8 1.1 copy.15
  (11 shorter events, 0.1 us)
Async XLA Ops:
  4.6 29.9 %all-to-all-start = ((bf16[4,2,2,512,128]{4,3,2,1,0:T(8,128)(2,1)}), bf16[4,2,2,512,128]{4,3,2,1,0:T(8,128)(2,1)S(1)}, u32[]{:S(2)}, u32[]{:S(2)}) async-start(bf16[4,2,2,512,128]{4,3,2,1,0:T(8,128)(2,1)} %spread.1), calls=%async_computation | async-start | bytes 4194304 | tf_op jit(solution)/shard_map/all_to_all | solution.py:331
  34.6 1.3 copy-start
  47.5 5.7 %copy-start.2 = (f32[128,64]{0,1:T(8,128)S(1)}, f32[128,64]{0,1:T(8,128)}, u32[]{:S(2)}) copy-start(f32[128,64]{0,1:T(8,128)} %param.5) | copy-start | bytes 98308
  47.5 54.4 %all-to-all-start.1 = ((bf16[32,2,2,4,16,128]{5,4,3,2,1,0:T(8,128)(2,1)}), bf16[32,2,2,4,16,128]{5,4,3,2,1,0:T(8,128)(2,1)S(1)}, u32[]{:S(2)}, u32[]{:S(2)}) async-start(bf16[32,2,2,4,16,128]{5,4,3,2,1,0:T(8,128)(2,1)} %bitcast.14), calls=%async_computation.1 | async-start | bytes 4194304 | tf_op jit(solution)/shard_map/all_to_all | solution.py:337
  101.9 1.3 copy-start.1

commit v2 on v0

--- a/solution.py
+++ b/solution.py
@@ -1,17 +1,517 @@
+import functools
 import math
 
 import jax
 import jax.numpy as jnp
+import numpy as np
 from jax import lax
+from jax.experimental import pallas as pl
+from jax.experimental.pallas import tpu as pltpu
 from jax.sharding import PartitionSpec as P
+
 
 TAPS = 16
 CH_LO = 32
 CH_HI = 128
 GROUPS = 4
-
-
+POINTS = CH_LO * CH_HI
 TWO_PI = 2.0 * math.pi
+BF = jnp.bfloat16
+F32 = jnp.float32
+
+LANES = 128
+TF = 4
+STN = 8
+PART = CH_HI // TF
+LOW = CH_LO // TF
+PER = 4
+CHUNKS = 2
+
+
+def filter_window(position):
+    total_len = float(TAPS * POINTS)
+    value = position.astype(F32)
+    hann_taper = 0.5 - 0.5 * jnp.cos(TWO_PI / total_len * value)
+    return jnp.sinc((value - 0.5 * total_len) / float(POINTS)) * hann_taper
+
+
+def window_rows(part):
+    shape = (TAPS, 2 * CH_LO, LANES)
+    tap = lax.broadcasted_iota(jnp.int32, shape, 0)
+    n2 = lax.broadcasted_iota(jnp.int32, shape, 1) // 2
+    n1 = part * PART + lax.broadcasted_iota(jnp.int32, shape, 2) % PART
+    return filter_window(tap * POINTS + n2 * CH_HI + n1)
+
+
+def dft_pair(points):
+    counter = np.arange(points)
+    angles = TWO_PI / points * (counter[:, None] * counter[None, :] % points)
+    factor = 1.0 / math.sqrt(points)
+    return np.cos(angles) * factor, np.sin(angles) * factor
+
+
+def first_table():
+    cosine, sine = dft_pair(CH_LO)
+    planes = np.stack([np.stack([cosine, sine]), np.stack([-sine, cosine])])
+    planes = planes.reshape(2, 2, TF, LOW, CH_LO)
+    table = np.einsum("oitkn,pr->otpkinr", planes, np.eye(2))
+    return jnp.asarray(table.reshape(4 * CH_LO, 4 * CH_LO), BF)
+
+
+def second_table():
+    cosine, sine = dft_pair(CH_HI)
+    table = np.block([[cosine, -sine], [sine, cosine]])
+    return jnp.asarray(table, BF)
+
+
+def twiddle_rows(part):
+    shape = (2 * CH_LO, LANES)
+    row = lax.broadcasted_iota(jnp.int32, shape, 0)
+    k2 = row // (2 * LOW) * LOW + row % LOW
+    n1 = part * PART + lax.broadcasted_iota(jnp.int32, shape, 1) % PART
+    angle = TWO_PI / POINTS * (k2 * n1).astype(F32)
+    return jnp.cos(angle), jnp.sin(angle)
+
+
+VMEM = pl.BlockSpec(memory_space=pltpu.VMEM)
+SMEM = pl.BlockSpec(memory_space=pltpu.SMEM)
+HBM = pl.BlockSpec(memory_space=pltpu.HBM)
+
+
+def params(mib):
+    return pltpu.CompilerParams(vmem_limit_bytes=mib << 20)
+
+
+def cost(mib, flops=0):
+    return pl.CostEstimate(flops=flops, bytes_accessed=mib << 20, transcendentals=0)
+
+
+def swap_lane_blocks(parts):
+    lane = lax.broadcasted_iota(jnp.int32, parts[0].shape, 1)
+    upper = lane >= 2 * PART
+    odd = (lane // PART) % 2 == 1
+    turned = [pltpu.roll(part, 2 * PART, 1) for part in parts]
+    half = [
+        jnp.where(upper, turned[2], parts[0]),
+        jnp.where(upper, turned[3], parts[1]),
+        jnp.where(upper, parts[2], turned[0]),
+        jnp.where(upper, parts[3], turned[1]),
+    ]
+    out = []
+    for low, high in ((half[0], half[1]), (half[2], half[3])):
+        out.append(jnp.where(odd, pltpu.roll(high, PART, 1), low))
+        out.append(jnp.where(odd, high, pltpu.roll(low, LANES - PART, 1)))
+    return out
+
+
+def spread_kernel(chunk, me_ref, volt_ref, *refs):
+    outs, (in_ref, sem) = refs[:TF], refs[TF:]
+    planes, _, frames, _, _ = volt_ref.shape
+    reads = [
+        pltpu.make_async_copy(volt_ref.at[q, pl.ds(chunk * PER, PER)], in_ref.at[q], sem.at[q])
+        for q in range(planes)
+    ]
+    for read in reads:
+        read.start()
+    for q in range(planes):
+        reads[q].wait()
+        for me in range(TF):
+
+            @pl.when(me_ref[0] == me)
+            def _(me=me, q=q):
+                def one(f, carry):
+                    parts = [in_ref[q, a, f] for a in range(PER)]
+                    for j, block in enumerate(swap_lane_blocks(parts)):
+                        outs[j ^ me][q, f] = block
+                    return carry
+
+                lax.fori_loop(0, frames, one, 0)
+
+
+def spread(me, volt, chunk):
+    planes, _, frames, rows, _ = volt.shape
+    return pl.pallas_call(
+        functools.partial(spread_kernel, chunk),
+        name="spread",
+        in_specs=[SMEM, HBM],
+        out_specs=[VMEM] * TF,
+        out_shape=[jax.ShapeDtypeStruct((planes, frames, rows, LANES), BF)] * TF,
+        scratch_shapes=[
+            pltpu.VMEM((planes, PER, frames, rows, LANES), BF),
+            pltpu.SemaphoreType.DMA((planes,)),
+        ],
+        compiler_params=params(6),
+        cost_estimate=cost(4),
+    )(me, volt)
+
+
+def channel_kernel(me_ref, *refs):
+    sources = refs[:TF]
+    win_ref, table_ref, cos_ref, sin_ref, out_ref, stage_ref, filt_ref, done_ref, sem = refs[TF:]
+    me = me_ref[0]
+    rows = 2 * CH_LO
+    history = TAPS - 1
+    planes, per_source = sources[0].shape[:2]
+    frames = TF * per_source
+    for d, ref in enumerate(sources):
+        stage_ref[:, pl.ds((me ^ d) * per_source, per_source)] = ref[...]
+
+    strip = 16
+
+    def one_strip(q, step, carry):
+        at = pl.multiple_of(step * strip, strip)
+        data = [stage_ref[q, f, pl.ds(at, strip), :].astype(F32) for f in range(frames)]
+        taps = [win_ref[tap, pl.ds(at, strip), :] for tap in range(TAPS)]
+        for f in range(frames):
+            total = None
+            for tap in range(max(0, history - f), TAPS):
+                term = taps[tap] * data[f + tap - history]
+                total = term if total is None else total + term
+            filt_ref[f, q, pl.ds(at, strip), :] = total.astype(BF)
+        return carry
+
+    for q in range(planes):
+        lax.fori_loop(0, rows // strip, functools.partial(one_strip, q), 0)
+
+    table = table_ref[...]
+    per_dest = frames // STN
+
+    def send(dest):
+        return pltpu.make_async_copy(done_ref.at[dest], out_ref.at[dest], sem.at[dest])
+
+    def one_dest(dest, carry):
+        cosine, sine = cos_ref[...], sin_ref[...]
+        for pair in range(per_dest // 2):
+            f = per_dest * dest + 2 * pair
+            left = filt_ref[f].reshape(2 * rows, LANES)
+            right = filt_ref[f + 1].reshape(2 * rows, LANES)
+            both = jnp.concatenate([left, right], axis=1)
+            spectrum = jnp.dot(table, both, preferred_element_type=F32)
+            for side in range(2):
+                real = spectrum[:rows, side * LANES : (side + 1) * LANES]
+                imag = spectrum[rows:, side * LANES : (side + 1) * LANES]
+                turned = (real * cosine + imag * sine, imag * cosine - real * sine)
+                for o in range(2):
+                    value = turned[o].astype(BF).reshape(TF, 2 * LOW, LANES)
+                    done_ref[dest, :, o, 2 * pair + side] = value
+        send(dest).start()
+        return carry
+
+    lax.fori_loop(0, STN, one_dest, 0, unroll=2)
+    for dest in range(STN):
+        send(dest).wait()
+
+
+def channel_step(me, blocks, window, table, cosine, sine):
+    planes, per_source, rows, _ = blocks[0].shape
+    frames = TF * per_source
+    out = (STN, TF, planes, frames // STN, 2 * LOW, LANES)
+    return pl.pallas_call(
+        channel_kernel,
+        name="channel_step",
+        in_specs=[SMEM] + [VMEM] * (TF + 4),
+        out_specs=HBM,
+        out_shape=jax.ShapeDtypeStruct(out, BF),
+        scratch_shapes=[
+            pltpu.VMEM((planes, frames, rows, LANES), BF),
+            pltpu.VMEM((frames, planes, rows, LANES), BF),
+            pltpu.VMEM(out, BF),
+            pltpu.SemaphoreType.DMA((STN,)),
+        ],
+        compiler_params=params(12),
+        cost_estimate=cost(8, 1 << 29),
+    )(me, *blocks, window, table, cosine, sine)
+
+
+def weight_kernel(chunk, at_ref, table_ref, beam_ref, group_ref, out_ref, order_ref, start_ref):
+    total = group_ref.shape[0]
+    members = out_ref.shape[0] - 1
+    offsets = out_ref.shape[1]
+    scale = math.sqrt(GROUPS / total)
+    shape = (LOW, LANES)
+    k2 = at_ref[0] * LOW + lax.broadcasted_iota(jnp.int32, shape, 0)
+    channel = k2 + CH_LO * lax.broadcasted_iota(jnp.int32, shape, 1)
+    fraction = channel.astype(F32) / float(POINTS)
+
+    def station(member):
+        return (member // PER) * (PER * CHUNKS) + chunk * PER + member % PER
+
+    def one_member(member, carry):
+        s = station(member)
+        group = group_ref[s]
+        for d in range(offsets):
+            beam = group + GROUPS * (at_ref[1] ^ d)
+            turns = table_ref[beam_ref[beam], s] * fraction
+            quarter = jnp.round(4.0 * turns)
+            angle = TWO_PI * (turns - 0.25 * quarter)
+            square = angle * angle
+            sine = angle * (
+                1.0 + square * (-1.0 / 6 + square * (1.0 / 120 + square * (-1.0 / 5040 + square * (1.0 / 362880))))
+            )
+            cosine = 1.0 + square * (
+                -0.5 + square * (1.0 / 24 + square * (-1.0 / 720 + square * (1.0 / 40320)))
+            )
+            turn = quarter.astype(jnp.int32) & 3
+            odd = (turn & 1) == 1
+            base_cos = jnp.where(odd, sine, cosine)
+            base_sin = jnp.where(odd, cosine, sine)
+            real = scale * jnp.where((turn == 1) | (turn == 2), -base_cos, base_cos)
+            imag = -scale * jnp.where(turn >= 2, -base_sin, base_sin)
+            real = real.astype(BF).astype(F32)
+            imag = imag.astype(BF).astype(F32)
+            out_ref[member, d, 0] = real
+            out_ref[member, d, 1] = imag - real
+            out_ref[member, d, 2] = imag + real
+        return carry
+
+    lax.fori_loop(0, members, one_member, 0)
+    out_ref[members] = jnp.zeros(out_ref.shape[1:], F32)
+
+    at = jnp.int32(0)
+    for g in range(GROUPS):
+        start_ref[g] = at // 2
+
+        def put(member, at, g=g):
+            mine = group_ref[station(member)] == g
+
+            @pl.when(mine)
+            def _():
+                order_ref[at] = member
+
+            return at + mine.astype(jnp.int32)
+
+        at = lax.fori_loop(0, members, put, at)
+
+        @pl.when(at % 2 == 1)
+        def _():
+            order_ref[at] = members
+
+        at = at + at % 2
+    start_ref[GROUPS] = at // 2
+
+
+def beam_weights(at, chunk, delay_table, beam_pointing, station_group):
+    members = station_group.shape[0] // CHUNKS
+    offsets = beam_pointing.shape[0] // GROUPS
+    return pl.pallas_call(
+        functools.partial(weight_kernel, chunk),
+        name="beam_weights",
+        in_specs=[SMEM] * 4,
+        out_specs=[VMEM, SMEM, SMEM],
+        out_shape=[
+            jax.ShapeDtypeStruct((members + 1, offsets, 3, LOW, LANES), F32),
+            jax.ShapeDtypeStruct((members + GROUPS,), jnp.int32),
+            jax.ShapeDtypeStruct((GROUPS + 1,), jnp.int32),
+        ],
+        compiler_params=params(8),
+        cost_estimate=cost(8, 1 << 29),
+    )(at, delay_table, beam_pointing, station_group)
+
+
+def transform(blocks_ref, table_ref, chan_ref):
+    sources, _, _, per_dest = blocks_ref.shape[:4]
+    rows = per_dest * 2 * LOW
+    table = table_ref[...]
+    for src in range(sources):
+        planes = []
+        for o in range(2):
+            parts = [blocks_ref[src, j, o].reshape(rows, LANES) for j in range(TF)]
+            planes.append(swap_lane_blocks(parts))
+        for a in range(PER):
+            both = jnp.concatenate([planes[0][a], planes[1][a]], axis=1)
+            spectrum = jnp.dot(both, table, preferred_element_type=F32)
+            for o in range(2):
+                value = spectrum[:, o * LANES : (o + 1) * LANES]
+                chan_ref[src * PER + a, o] = value.reshape(per_dest * 2, LOW, LANES)
+    chan_ref[chan_ref.shape[0] - 1] = jnp.zeros(chan_ref.shape[1:], F32)
+
+
+def form_beams_of(offsets, chan_ref, weight_ref, order_ref, start_ref, put):
+    count = len(offsets)
+    wide = 16 // count
+    blocks = chan_ref.shape[2] // wide
+
+    def one_block(step, carry):
+        g, base = step // blocks, step % blocks * wide
+
+        def one_pair(pair, acc):
+            acc = list(acc)
+            for member in (order_ref[2 * pair], order_ref[2 * pair + 1]):
+                data = []
+                for x in range(wide):
+                    re, im = chan_ref[member, 0, base + x], chan_ref[member, 1, base + x]
+                    data.append((re + im, re, im))
+                for i, d in enumerate(offsets):
+                    for y in range(3):
+                        weight = weight_ref[member, d, y]
+                        for x in range(wide):
+                            at = (i * 3 + y) * wide + x
+                            acc[at] = acc[at] + weight * data[x][y]
+            return tuple(acc)
+
+        zero = jnp.zeros((LOW, LANES), F32)
+        acc = lax.fori_loop(start_ref[g], start_ref[g + 1], one_pair, (zero,) * (3 * count * wide))
+        for i, d in enumerate(offsets):
+            for x in range(wide):
+                both, re, im = (acc[(i * 3 + y) * wide + x] for y in range(3))
+                put(d, g, 0, base + x, both - im)
+                put(d, g, 1, base + x, both + re)
+        return carry
+
+    lax.fori_loop(0, GROUPS * blocks, one_block, 0)
+
+
+def early_kernel(blocks_ref, table_ref, weight_ref, order_ref, start_ref, at_ref, sum_ref, next_ref, chan_ref):
+    next_ref[0], next_ref[1] = at_ref[0], at_ref[1]
+    transform(blocks_ref, table_ref, chan_ref)
+
+    def put(d, g, o, fp, value):
+        sum_ref[d, g, o, fp % 2, fp // 2] = value
+
+    form_beams_of(range(weight_ref.shape[1]), chan_ref, weight_ref, order_ref, start_ref, put)
+
+
+def late_kernel(offsets, fresh, *refs):
+    if fresh:
+        blocks_ref, table_ref, weight_ref, order_ref, start_ref, sum_ref = refs[:6]
+        chan_ref, outs = refs[6], refs[7:]
+        transform(blocks_ref, table_ref, chan_ref)
+    else:
+        chan_ref, weight_ref, order_ref, start_ref, sum_ref = refs[:5]
+        outs = refs[5:]
+
+    def put(d, g, o, fp, value):
+        f, p = fp // 2, fp % 2
+        outs[d - offsets[0]][g, o, p, f] = (value + sum_ref[d, g, o, p, f]).astype(BF)
+
+    form_beams_of(offsets, chan_ref, weight_ref, order_ref, start_ref, put)
+
+
+def beam_shapes(blocks, weights):
+    planes, per_dest = blocks.shape[2:4]
+    one = (GROUPS, planes, 2, per_dest, LOW, LANES)
+    return one, (weights.shape[0], planes, 2 * per_dest, LOW, LANES)
+
+
+def beams_early(blocks, table, weights, order, start, at):
+    one, chan = beam_shapes(blocks, weights)
+    return pl.pallas_call(
+        early_kernel,
+        name="beams_early",
+        in_specs=[VMEM] * 3 + [SMEM] * 3,
+        out_specs=[VMEM, SMEM],
+        out_shape=[
+            jax.ShapeDtypeStruct((weights.shape[1],) + one, F32),
+            jax.ShapeDtypeStruct(at.shape, at.dtype),
+        ],
+        scratch_shapes=[pltpu.VMEM(chan, F32)],
+        compiler_params=params(12),
+        cost_estimate=cost(8, 1 << 29),
+    )(blocks, table, weights, order, start, at)
+
+
+def beams_far(blocks, table, weights, order, start, partial):
+    one, chan = beam_shapes(blocks, weights)
+    offsets = range(weights.shape[1] // 2, weights.shape[1])
+    outs = pl.pallas_call(
+        functools.partial(late_kernel, offsets, True),
+        name="beams_far",
+        in_specs=[VMEM] * 3 + [SMEM] * 2 + [VMEM],
+        out_specs=[VMEM] * (1 + len(offsets)),
+        out_shape=[jax.ShapeDtypeStruct(chan, F32)] + [jax.ShapeDtypeStruct(one, BF)] * len(offsets),
+        compiler_params=params(12),
+        cost_estimate=cost(8, 1 << 29),
+    )(blocks, table, weights, order, start, partial)
+    return outs[0], outs[1:]
+
+
+def beams_near(chan, weights, order, start, partial):
+    offsets = range(weights.shape[1] // 2)
+    return pl.pallas_call(
+        functools.partial(late_kernel, offsets, False),
+        name="beams_near",
+        in_specs=[VMEM] * 2 + [SMEM] * 2 + [VMEM],
+        out_specs=[VMEM] * len(offsets),
+        out_shape=[jax.ShapeDtypeStruct(partial.shape[1:], BF)] * len(offsets),
+        compiler_params=params(12),
+        cost_estimate=cost(8, 1 << 29),
+    )(chan, weights, order, start, partial)
+
+
+def gather_kernel(me_ref, *refs):
+    parts, out_ref, sem = refs[:STN], refs[STN], refs[STN + 1]
+    per_dest = parts[0].shape[3]
+    copies = []
+    for d, part in enumerate(parts):
+        frames = pl.ds((me_ref[0] ^ d) * per_dest, per_dest)
+        copies.append(pltpu.make_async_copy(part, out_ref.at[:, :, :, frames], sem.at[d]))
+    for copy in copies:
+        copy.start()
+    for copy in copies:
+        copy.wait()
+
+
+def gather_frames(me, parts):
+    shape = parts[0].shape
+    shape = shape[:3] + (shape[3] * len(parts),) + shape[4:]
+    return pl.pallas_call(
+        gather_kernel,
+        name="gather_frames",
+        in_specs=[SMEM] + [VMEM] * len(parts),
+        out_specs=pl.BlockSpec(memory_space=pl.ANY),
+        out_shape=jax.ShapeDtypeStruct(shape, BF),
+        scratch_shapes=[pltpu.SemaphoreType.DMA((len(parts),))],
+        compiler_params=params(4),
+    )(me, *parts)
+
+
+def swapped(value, axis, offset):
+    count = lax.axis_size(axis)
+    return lax.ppermute(value, axis, [(i, i ^ offset) for i in range(count)])
+
+
+def fast_body(voltages, delay_table, beam_pointing, station_group):
+    planes, stations_here, pols, samples_here = voltages.shape
+    part, home = lax.axis_index("tf"), lax.axis_index("stn")
+    me = part.astype(jnp.int32).reshape(1)
+    owner = home.astype(jnp.int32).reshape(1)
+    at = jnp.concatenate([me, owner])
+    rows = samples_here // LANES
+    volt = voltages.reshape(planes, stations_here, pols, rows, LANES)
+    volt = volt.transpose(0, 1, 3, 2, 4)
+    volt = volt.reshape(planes, stations_here, rows // CH_LO, CH_LO * pols, LANES)
+    cosine, sine = twiddle_rows(part)
+    window, first, second = window_rows(part), first_table(), second_table()
+
+    blocks = []
+    for chunk in range(CHUNKS):
+        own = spread(me, volt, chunk)
+        row = [own[0]]
+        for d in range(1, TF):
+            row.append(swapped(own[d], "tf", d))
+        blocks.append(row)
+
+    turned = []
+    for chunk in range(CHUNKS):
+        value = channel_step(me, blocks[chunk], window, first, cosine, sine)
+        shape = value.shape
+        value = value.reshape((STN * TF,) + shape[2:])
+        value = lax.all_to_all(value, ("stn", "tf"), split_axis=0, concat_axis=0, tiled=True)
+        turned.append(value.reshape(shape))
+
+    args = (delay_table, beam_pointing, station_group)
+    weights = beam_weights(at, 0, *args)
+    partial, at = beams_early(turned[0], second, *weights, at)
+    weights = beam_weights(at, 1, *args)
+    chan, far = beams_far(turned[1], second, *weights, partial)
+    parts = [None] * STN
+    for i, value in enumerate(far):
+        d = STN // 2 + i
+        parts[d] = swapped(value, "stn", d)
+    near = beams_near(chan, *weights, partial)
+    for d, value in enumerate(near):
+        parts[d] = swapped(value, "stn", d) if d else value
+    return gather_frames(owner, parts)
 
 
 def passed_along(value, axis, steps):
@@ -20,7 +520,7 @@
     return lax.ppermute(value, axis, [(source, source + steps) for source in range(first, last)])
 
 
-def filter_window(tap_count, points):
+def plain_window(tap_count, points):
     position = jnp.arange(tap_count * points, dtype=jnp.int32).astype(jnp.float32)
     total_len = float(tap_count * points)
     hann_taper = 0.5 - 0.5 * jnp.cos(TWO_PI / total_len * position)
@@ -41,7 +541,7 @@
 
 def channelize(extended, frame_count):
     points = CH_LO * CH_HI
-    window = filter_window(TAPS, points)
+    window = plain_window(TAPS, points)
     filtered = sum(
         (
             window[tap_step]
@@ -70,7 +570,7 @@
     ).astype(jnp.bfloat16)
 
 
-def beam_weights(delays, beam_ids, groups, channel_low, station_total):
+def plain_weights(delays, beam_ids, groups, channel_low, station_total):
     points = CH_LO * CH_HI
     member = (groups[None, :] == (beam_ids % GROUPS)[:, None]).astype(jnp.float32)
     weight_scale = math.sqrt(GROUPS / station_total) * member
@@ -107,7 +607,6 @@
 def with_history(frames_own):
     frame_count = frames_own.shape[3]
     needed = TAPS - 1
-    tf_size = lax.axis_size("tf")
     pieces = []
     hop_count = (needed + frame_count - 1) // frame_count
     for hop_step in range(1, hop_count + 1):
@@ -117,7 +616,7 @@
     return jnp.concatenate(pieces[::-1] + [frames_own], axis=3)
 
 
-def body(voltages, delay_table, beam_pointing, station_group):
+def plain_body(voltages, delay_table, beam_pointing, station_group):
     planes, stations_here, pol_count, samples_here = voltages.shape
     points = CH_LO * CH_HI
     frame_count = samples_here // points
@@ -130,7 +629,7 @@
     channel_low = lax.axis_index("stn") * low_count + jnp.arange(low_count, dtype=jnp.int32)
     beam_ids = jnp.arange(beam_total, dtype=jnp.int32)
     delays_all = select_delays(delay_table, beam_pointing)
-    weight_re, weight_im = beam_weights(
+    weight_re, weight_im = plain_weights(
         delays_all, beam_ids, station_group, channel_low, station_total
     )
     formed = form_beams(weight_re, weight_im, regrouped).astype(jnp.bfloat16)
@@ -147,4 +646,12 @@
 def solution(mesh):
     in_specs = (P(None, "stn", None, "tf"), P(), P(), P())
     out_specs = P("stn", None, None, None, "tf", None)
-    return jax.shard_map(body, mesh=mesh, in_specs=in_specs, out_specs=out_specs, check_vma=False)
+
+    def spread_over(body):
+        return jax.shard_map(
+            body, mesh=mesh, in_specs=in_specs, out_specs=out_specs, check_vma=False
+        )
+
+    if mesh.shape["tf"] == TF and mesh.shape["stn"] == STN:
+        return spread_over(fast_body)
+    return spread_over(plain_body)

time: 319 us -> 129 us (0.40)
  matrix products: 137 us -> 0 us
  blocking collectives: 48.2 us -> 0 us
  Pallas kernels: 0 us -> 42.4 us
  waiting for transfers between devices: 81.3 us -> 50.5 us
  local copies, waits for them, and re-layouts: 24.3 us -> 7.25 us
  other arithmetic: 14.6 us -> 2.85 us
  starting transfers between devices: 12.8 us -> 24.4 us
    dot_general x7 -> x0, matrix products: 137 us -> none  [the longest x4 136 us: contract(): jnp.einsum('bsxc,spfxc->bpfxc', weights_part, data_part, preferred_elemen...]
    all_to_all x2 -> x0, blocking collectives: 48.2 us -> none  [the longest x1 28.6 us: body(): lax.all_to_all(formed, 'stn', split_axis=0, concat_axis=4, tiled=True)]
    pallas_call x0 -> x10, Pallas kernels: none -> 42.4 us  [the longest x2 14 us: beam_weights(): pl.pallas_call(functools.partial(weight_kernel, chunk), name='beam_weight...]
    all_to_all x1 -> x2, waiting for transfers between devices: 43.2 us -> 3.99 us  [fast_body(): lax.all_to_all(value, ('stn', 'tf'), split_axis=0, concat_axis=0, tiled=T...]
    reshape x1 -> x0, other arithmetic: 11.7 us -> none  [channelize(): shaped = filtered.reshape(filtered.shape[:4] + (CH_LO, CH_HI))]
    ppermute x2 -> x13, waiting for transfers between devices: 38.2 us -> 46.5 us  [swapped(): return lax.ppermute(value, axis, [(i, i ^ offset) for i in range(count)])]
    ppermute x2 -> x13, starting transfers between devices: 6.94 us -> 14.9 us  [swapped(): return lax.ppermute(value, axis, [(i, i ^ offset) for i in range(count)])]
    unnamed x9 -> x25, local copies, waits for them, and re-layouts: 0.23 us -> 7.25 us
  transfers between devices with their start and end apart: 3 -> 15, of which waited for: 2 -> 9; matrix products, arithmetic and copies ran while one was open for 2% -> 2% of each run, Pallas kernels for 0% -> 21%
where the time goes in v2:
time: 129 us; the launch traced here: 128 us
  waiting for transfers between devices  50.5 us (39%)
  Pallas kernels  42.4 us (33%)
  starting transfers between devices  24.4 us (19%)
  local copies, waits for them, and re-layouts  7.25 us (6%)
  other arithmetic  2.85 us (2%)
    ppermute x13, waiting for transfers between devices, swapped(): return lax.ppermute(value, axis, [(i, i ^ offset) for i in range(count)])  46.5 us
    ppermute x13, starting transfers between devices, swapped(): return lax.ppermute(value, axis, [(i, i ^ offset) for i in range(count)])  14.9 us
    pallas_call x2, Pallas kernels, beam_weights(): pl.pallas_call(functools.partial(weight_kernel, chunk), name='beam_weight...  14 us
    all_to_all x2, starting transfers between devices, fast_body(): lax.all_to_all(value, ('stn', 'tf'), split_axis=0, concat_axis=0, tiled=T...  9.54 us
    pallas_call x2, Pallas kernels, channel_step(): pl.pallas_call(channel_kernel, name='channel_step', in_specs=[SMEM] + [VM...  8.36 us
    unnamed x25, local copies, waits for them, and re-layouts  7.25 us
    pallas_call x1, Pallas kernels, beams_early(): pl.pallas_call(early_kernel, name='beams_early', in_specs=[VMEM] * 3 + [S...  6.61 us
    pallas_call x2, Pallas kernels, spread(): pl.pallas_call(functools.partial(spread_kernel, chunk), name='spread', in...  5.62 us
  transfers between devices with their start and end apart: 15, of which 9 were waited for; matrix products, arithmetic and copies ran while one was open for 2% of the time, Pallas kernels for 21%

profile of v2, /device:TPU:0, one launch (start us, length us, event | category | flops | bytes accessed | tf_op | source)
XLA Modules:
  0.0 127.7 jit_solution(10599580029378718254)
XLA Ops:
  0.0 1.6 %copy-done = bf16[2,8,2,32768]{3,2,1,0:T(2,128)(2,1)S(1)} copy-done((bf16[2,8,2,32768]{3,2,1,0:T(2,128)(2,1)S(1)}, bf16[2,8,2,32768]{3,2,1,0:T(2,128)(2,1)}, u32[]{:S(2)}) %copy-start) | copy-done | bytes 2097176
  1.6 2.8 %spread.3 = (bf16[2,8,64,128]{3,2,1,0:T(8,128)(2,1)S(1)}, bf16[2,8,64,128]{3,2,1,0:T(8,128)(2,1)S(1)}, bf16[2,8,64,128]{3,2,1,0:T(8,128)(2,1)S(1)}, bf16[2,8,64,128]{3,2,1,0:T(8,128)(2,1)S(1)}) custom-call(s32[1]{0:T(128)} %bitcast.1.me_ref, bf16[2,8,8,64,128]{4,3,2,1,0:T(8,128)(2,1)S(1)} %bitcast.11), custom_call_target="tpu_custom_call" | custom-call | bytes 4194304 | tf_op jit(solution)/shard_map/spread/pallas_call | solution.py:133
  5.0 2.6 %collective-permute-start.4 = (bf16[2,8,64,128]{3,2,1,0:T(8,128)(2,1)S(1)}, bf16[2,8,64,128]{3,2,1,0:T(8,128)(2,1)S(1)}, u32[]{:S(2)}, u32[]{:S(2)}) collective-permute-start(bf16[2,8,64,128]{3,2,1,0:T(8,128)(2,1)S(1)} %get-tuple-element.36), channel_id=1, source_target_pairs={{0,2},{1,3},{2,0},{3,1},{4,6},{5,7},{6,4},{7,5},{8,10},{9,11},{10,... | collective-permute-start | bytes 786440 | tf_op jit(solution)/shard_map/ppermute | solution.py:470
  7.6 2.5 %fusion.4.refs_4_ = f32[16,64,128]{2,1,0:T(8,128)S(1)} fusion(s32[128]{0:T(128)S(1)} %get-tuple-element.59, s32[128]{0:T(128)S(1)} %get-tuple-element.60, s32[]{:T(128)S(6)} %mul.100, s32[64]{0:T(128)S(1)} %get-tuple-element.57, s32[64]{0:T(128)S(1)} %get-tuple-element.58, s32[16]{0:T(128)S(1)} %iota_multiply_fusion, pred[64]{0:T(512)(128)(4,1)S(1)} %compare_and_fusion.3, ...), kind=kLoop, calls=%fused_computation.10 | loop fusion | flops 6029312 | bytes 526084 | tf_op jit(solution)/shard_map/mul | solution.py:35
  10.4 4.3 %collective-permute-done.4.refs_2_ = bf16[2,8,64,128]{3,2,1,0:T(8,128)(2,1)S(1)} collective-permute-done((bf16[2,8,64,128]{3,2,1,0:T(8,128)(2,1)S(1)}, bf16[2,8,64,128]{3,2,1,0:T(8,128)(2,1)S(1)}, u32[]{:S(2)}, u32[]{:S(2)}) %collective-permute-start.4) | collective-permute-done | bytes 262176 | tf_op jit(solution)/shard_map/ppermute | solution.py:470
  14.7 5.1 %collective-permute-done.5.refs_3_ = bf16[2,8,64,128]{3,2,1,0:T(8,128)(2,1)S(1)} collective-permute-done((bf16[2,8,64,128]{3,2,1,0:T(8,128)(2,1)S(1)}, bf16[2,8,64,128]{3,2,1,0:T(8,128)(2,1)S(1)}, u32[]{:S(2)}, u32[]{:S(2)}) %collective-permute-start.5) | collective-permute-done | bytes 262176 | tf_op jit(solution)/shard_map/ppermute | solution.py:470
  21.5 4.8 %channel_step.3 = bf16[8,4,2,4,16,128]{5,4,3,2,1,0:T(8,128)(2,1)S(1)} custom-call(s32[1]{0:T(128)} %bitcast.1.me_ref, bf16[2,8,64,128]{3,2,1,0:T(8,128)(2,1)S(1)} %get-tuple-element.34.refs_0_, bf16[2,8,64,128]{3,2,1,0:T(8,128)(2,1)S(1)} %collective-permute-done.3.refs_1_, bf16[2,8,64,128]{3,2,1,0:T(8,128)(2,1)S(1)} %collective-permute-done.4.refs_2_, ...), custom_call_target="tpu_custom_call" | custom-call | flops 536870912 | bytes 8388608 | tf_op jit(solution)/shard_map/channel_step/pallas_call | solution.py:209
  26.3 1.0 copy-done.4
  27.2 5.9 %all-to-all-start.1 = ((bf16[32,2,4,16,128]{4,3,2,1,0:T(8,128)(2,1)}), bf16[32,2,4,16,128]{4,3,2,1,0:T(8,128)(2,1)}, u32[]{:S(2)}, u32[]{:S(2)}) async-start(bf16[32,2,4,16,128]{4,3,2,1,0:T(8,128)(2,1)} %bitcast.13), calls=%async_computation.1 | async-start | bytes 2097152 | tf_op jit(solution)/shard_map/all_to_all | solution.py:499
  33.2 2.8 %spread.2 = (bf16[2,8,64,128]{3,2,1,0:T(8,128)(2,1)S(1)}, bf16[2,8,64,128]{3,2,1,0:T(8,128)(2,1)S(1)}, bf16[2,8,64,128]{3,2,1,0:T(8,128)(2,1)S(1)}, bf16[2,8,64,128]{3,2,1,0:T(8,128)(2,1)S(1)}) custom-call(s32[1]{0:T(128)} %bitcast.1.me_ref, bf16[2,8,8,64,128]{4,3,2,1,0:T(8,128)(2,1)S(1)} %bitcast.12), custom_call_target="tpu_custom_call" | custom-call | bytes 4194304 | tf_op jit(solution)/shard_map/spread/pallas_call | solution.py:133
  36.3 1.6 %collective-permute-start.1 = (bf16[2,8,64,128]{3,2,1,0:T(8,128)(2,1)S(1)}, bf16[2,8,64,128]{3,2,1,0:T(8,128)(2,1)S(1)}, u32[]{:S(2)}, u32[]{:S(2)}) collective-permute-start(bf16[2,8,64,128]{3,2,1,0:T(8,128)(2,1)S(1)} %get-tuple-element.32), channel_id=1, source_target_pairs={{0,2},{1,3},{2,0},{3,1},{4,6},{5,7},{6,4},{7,5},{8,10},{9,11},{10,... | collective-permute-start | bytes 786440 | tf_op jit(solution)/shard_map/ppermute | solution.py:470
  37.9 13.8 %collective-permute-done.1.refs_2_ = bf16[2,8,64,128]{3,2,1,0:T(8,128)(2,1)S(1)} collective-permute-done((bf16[2,8,64,128]{3,2,1,0:T(8,128)(2,1)S(1)}, bf16[2,8,64,128]{3,2,1,0:T(8,128)(2,1)S(1)}, u32[]{:S(2)}, u32[]{:S(2)}) %collective-permute-start.1) | collective-permute-done | bytes 262176 | tf_op jit(solution)/shard_map/ppermute | solution.py:470
  51.8 7.4 %collective-permute-done.2.refs_3_ = bf16[2,8,64,128]{3,2,1,0:T(8,128)(2,1)S(1)} collective-permute-done((bf16[2,8,64,128]{3,2,1,0:T(8,128)(2,1)S(1)}, bf16[2,8,64,128]{3,2,1,0:T(8,128)(2,1)S(1)}, u32[]{:S(2)}, u32[]{:S(2)}) %collective-permute-start.2) | collective-permute-done | bytes 262176 | tf_op jit(solution)/shard_map/ppermute | solution.py:470
  59.1 3.6 %channel_step.2 = bf16[8,4,2,4,16,128]{5,4,3,2,1,0:T(8,128)(2,1)} custom-call(s32[1]{0:T(128)} %bitcast.1.me_ref, bf16[2,8,64,128]{3,2,1,0:T(8,128)(2,1)S(1)} %get-tuple-element.30.refs_0_, bf16[2,8,64,128]{3,2,1,0:T(8,128)(2,1)S(1)} %collective-permute-done.refs_1_, bf16[2,8,64,128]{3,2,1,0:T(8,128)(2,1)S(1)} %collective-permute-done.1.refs_2_, ...), custom_call_target="tpu_custom_call" | custom-call | flops 536870912 | bytes 8388608 | tf_op jit(solution)/shard_map/channel_step/pallas_call | solution.py:209
  62.7 3.6 %all-to-all-start = ((bf16[32,2,4,16,128]{4,3,2,1,0:T(8,128)(2,1)}), bf16[32,2,4,16,128]{4,3,2,1,0:T(8,128)(2,1)}, u32[]{:S(2)}, u32[]{:S(2)}) async-start(bf16[32,2,4,16,128]{4,3,2,1,0:T(8,128)(2,1)} %bitcast.5), calls=%async_computation | async-start | bytes 2097152 | tf_op jit(solution)/shard_map/all_to_all | solution.py:499
  66.6 7.0 %beam_weights.2 = (f32[33,8,3,8,128]{4,3,2,1,0:T(8,128)S(1)}, s32[36]{0:T(128)S(1)}, s32[5]{0:T(128)S(1)}) custom-call(s32[2]{0:T(128)S(1)} %pad_add_fusion.at_ref, f32[128,64]{1,0:T(8,128)S(1)} %copy.8.table_ref, s32[32]{0:T(128)S(1)} %copy-done.9, s32[64]{0:T(128)S(1)} %copy-done.10), custom_call_target="tpu_custom_call" | custom-call | flops 536870912 | bytes 8388608 | tf_op jit(solution)/shard_map/beam_weights/pallas_call | solution.py:296
  73.6 6.6 %beams_early.1 = (f32[8,4,2,2,4,8,128]{6,5,4,3,2,1,0:T(8,128)S(1)}, s32[2]{0:T(128)S(1)}) custom-call(bf16[8,4,2,4,16,128]{5,4,3,2,1,0:T(8,128)(2,1)} %bitcast.10.blocks_ref, bf16[256,256]{1,0:T(8,128)(2,1)S(1)} %copy-done.5, f32[33,8,3,8,128]{4,3,2,1,0:T(8,128)S(1)} %get-tuple-element.38.weight_ref, s32[36]{0:T(128)S(1)} %get-tuple-element.39.order_ref, ...), custom_call_target="tpu_custom_call" | custom-call | flops 536870912 | bytes 8388608 | tf_op jit(solution)/shard_map/beams_early/pallas_call | solution.py:398
  80.2 1.3 %copy-done.2 = f32[8,4,2,2,4,8,128]{6,5,4,3,2,1,0:T(8,128)} copy-done((f32[8,4,2,2,4,8,128]{6,5,4,3,2,1,0:T(8,128)}, f32[8,4,2,2,4,8,128]{6,5,4,3,2,1,0:T(8,128)S(1)}, u32[]{:S(2)}) %copy-start.2) | copy-done | bytes 2097176
  81.5 7.1 %beam_weights.3 = (f32[33,8,3,8,128]{4,3,2,1,0:T(8,128)S(1)}, s32[36]{0:T(128)S(1)}, s32[5]{0:T(128)S(1)}) custom-call(s32[2]{0:T(128)S(1)} %get-tuple-element.41.at_ref, f32[128,64]{1,0:T(8,128)S(1)} %copy.8.table_ref, s32[32]{0:T(128)S(1)} %copy-done.9, s32[64]{0:T(128)S(1)} %copy-done.10), custom_call_target="tpu_custom_call" | custom-call | flops 536870912 | bytes 8388608 | tf_op jit(solution)/shard_map/beam_weights/pallas_call | solution.py:296
  88.6 4.0 %all-to-all-done = bf16[32,2,4,16,128]{4,3,2,1,0:T(8,128)(2,1)} async-done(((bf16[32,2,4,16,128]{4,3,2,1,0:T(8,128)(2,1)}), bf16[32,2,4,16,128]{4,3,2,1,0:T(8,128)(2,1)}, u32[]{:S(2)}, u32[]{:S(2)}) %all-to-all-start) | async-done | bytes 1048608 | tf_op jit(solution)/shard_map/all_to_all | solution.py:499
  92.5 1.6 %copy-done.3 = f32[8,4,2,2,4,8,128]{6,5,4,3,2,1,0:T(8,128)S(1)} copy-done((f32[8,4,2,2,4,8,128]{6,5,4,3,2,1,0:T(8,128)S(1)}, f32[8,4,2,2,4,8,128]{6,5,4,3,2,1,0:T(8,128)}, u32[]{:S(2)}) %copy-start.3) | copy-done | bytes 2097176
  94.1 4.4 %beams_far.1 = (f32[33,2,8,8,128]{4,3,2,1,0:T(8,128)S(1)}, bf16[4,2,2,4,8,128]{5,4,3,2,1,0:T(8,128)(2,1)S(1)}, bf16[4,2,2,4,8,128]{5,4,3,2,1,0:T(8,128)(2,1)S(1)...) custom-call(bf16[8,4,2,4,16,128]{5,4,3,2,1,0:T(8,128)(2,1)} %bitcast.6.refs_0_, ...), custom_call_target="tpu_custom_call" | custom-call | flops 536870912 | bytes 8388608 | tf_op jit(solution)/shard_map/beams_far/pallas_call | solution.py:416
  98.5 2.4 %beams_near.1 = (bf16[4,2,2,4,8,128]{5,4,3,2,1,0:T(8,128)(2,1)S(1)}, bf16[4,2,2,4,8,128]{5,4,3,2,1,0:T(8,128)(2,1)S(1)}, bf16[4,2,2,4,8,128]{5,4,3,2,1,0:T(8,128)(2,1)S(1)}, bf16[4,2,2,4,8,128]{5,4,3,2,1,0:T(8,128)(2,1)S(1)}) custom-call(f32[33,2,8,8,128]{4,3,2,1,0:T(8,128)S(1)} %get-tuple-element.46.refs_0_, ...), custom_call_target="tpu_custom_call" | custom-call | flops 536870912 | bytes 8388608 | tf_op jit(solution)/shard_map/beams_near/pallas_call | solution.py:430
  100.9 1.5 %collective-permute-start.6 = (bf16[4,2,2,4,8,128]{5,4,3,2,1,0:T(8,128)(2,1)S(1)}, bf16[4,2,2,4,8,128]{5,4,3,2,1,0:T(8,128)(2,1)S(1)}, u32[]{:S(2)}, u32[]{:S(2)}) collective-permute-start(bf16[4,2,2,4,8,128]{5,4,3,2,1,0:T(8,128)(2,1)S(1)} %get-tuple-element.48), channel_id=1, source_target_pairs={{0,4},{4,0},{8,12},{12,8},{16,20},{20,16},{24,28},{28,24},{1,5},{5... | collective-permute-start | bytes 393224 | tf_op jit(solution)/shard_map/ppermute | solution.py:470
  103.1 1.4 %collective-permute-start.8 = (bf16[4,2,2,4,8,128]{5,4,3,2,1,0:T(8,128)(2,1)S(1)}, bf16[4,2,2,4,8,128]{5,4,3,2,1,0:T(8,128)(2,1)S(1)}, u32[]{:S(2)}, u32[]{:S(2)}) collective-permute-start(bf16[4,2,2,4,8,128]{5,4,3,2,1,0:T(8,128)(2,1)S(1)} %get-tuple-element.50), channel_id=1, source_target_pairs={{0,12},{4,8},{8,4},{12,0},{16,28},{20,24},{24,20},{28,16},{1,13},{... | collective-permute-start | bytes 393224 | tf_op jit(solution)/shard_map/ppermute | solution.py:470
  105.2 3.1 %collective-permute-start.10 = (bf16[4,2,2,4,8,128]{5,4,3,2,1,0:T(8,128)(2,1)S(1)}, bf16[4,2,2,4,8,128]{5,4,3,2,1,0:T(8,128)(2,1)S(1)}, u32[]{:S(2)}, u32[]{:S(2)}) collective-permute-start(bf16[4,2,2,4,8,128]{5,4,3,2,1,0:T(8,128)(2,1)S(1)} %get-tuple-element.52), channel_id=1, source_target_pairs={{0,20},{4,16},{8,28},{12,24},{16,4},{20,0},{24,12},{28,8},{1,21},{... | collective-permute-start | bytes 393224 | tf_op jit(solution)/shard_map/ppermute | solution.py:470
  108.3 1.5 %collective-permute-start.11 = (bf16[4,2,2,4,8,128]{5,4,3,2,1,0:T(8,128)(2,1)S(1)}, bf16[4,2,2,4,8,128]{5,4,3,2,1,0:T(8,128)(2,1)S(1)}, u32[]{:S(2)}, u32[]{:S(2)}) collective-permute-start(bf16[4,2,2,4,8,128]{5,4,3,2,1,0:T(8,128)(2,1)S(1)} %get-tuple-element.53), channel_id=1, source_target_pairs={{0,24},{4,28},{8,16},{12,20},{16,8},{20,12},{24,0},{28,4},{1,25},{... | collective-permute-start | bytes 393224 | tf_op jit(solution)/shard_map/ppermute | solution.py:470
  109.8 2.2 %collective-permute-done.7.refs_2_ = bf16[4,2,2,4,8,128]{5,4,3,2,1,0:T(8,128)(2,1)S(1)} collective-permute-done((bf16[4,2,2,4,8,128]{5,4,3,2,1,0:T(8,128)(2,1)S(1)}, bf16[4,2,2,4,8,128]{5,4,3,2,1,0:T(8,128)(2,1)S(1)}, u32[]{:S(2)}, u32[]{:S(2)}) %collective-permute-start.7) | collective-permute-done | bytes 131104 | tf_op jit(solution)/shard_map/ppermute | solution.py:470
  112.0 1.0 collective-permute-start.12
  113.3 9.7 %collective-permute-done.9.refs_4_ = bf16[4,2,2,4,8,128]{5,4,3,2,1,0:T(8,128)(2,1)S(1)} collective-permute-done((bf16[4,2,2,4,8,128]{5,4,3,2,1,0:T(8,128)(2,1)S(1)}, bf16[4,2,2,4,8,128]{5,4,3,2,1,0:T(8,128)(2,1)S(1)}, u32[]{:S(2)}, u32[]{:S(2)}) %collective-permute-start.9) | collective-permute-done | bytes 131104 | tf_op jit(solution)/shard_map/ppermute | solution.py:470
  123.0 3.7 %collective-permute-done.10.refs_5_ = bf16[4,2,2,4,8,128]{5,4,3,2,1,0:T(8,128)(2,1)S(1)} collective-permute-done((bf16[4,2,2,4,8,128]{5,4,3,2,1,0:T(8,128)(2,1)S(1)}, bf16[4,2,2,4,8,128]{5,4,3,2,1,0:T(8,128)(2,1)S(1)}, u32[]{:S(2)}, u32[]{:S(2)}) %collective-permute-start.10) | collective-permute-done | bytes 131104 | tf_op jit(solution)/shard_map/ppermute | solution.py:470
  126.7 1.0 gather_frames.1
  (44 shorter events, 4.7 us)
Async XLA Ops:
  0.0 1.6 %copy-start = (bf16[2,8,2,32768]{3,2,1,0:T(2,128)(2,1)S(1)}, bf16[2,8,2,32768]{3,2,1,0:T(2,128)(2,1)}, u32[]{:S(2)}) copy-start(bf16[2,8,2,32768]{3,2,1,0:T(2,128)(2,1)} %param.6) | copy-start | bytes 6291460
  1.6 18.9 %copy-start.8 = (bf16[128,128]{1,0:T(8,128)(2,1)S(1)}, bf16[128,128]{1,0:T(8,128)(2,1)}, u32[]{:S(2)}) copy-start(bf16[128,128]{1,0:T(8,128)(2,1)} %constant.136.clone.refs_5_) | copy-start | bytes 98308
  4.4 6.0 %collective-permute-start.3 = (bf16[2,8,64,128]{3,2,1,0:T(8,128)(2,1)S(1)}, bf16[2,8,64,128]{3,2,1,0:T(8,128)(2,1)S(1)}, u32[]{:S(2)}, u32[]{:S(2)}) collective-permute-start(bf16[2,8,64,128]{3,2,1,0:T(8,128)(2,1)S(1)} %get-tuple-element.35), channel_id=1, source_target_pairs={{0,1},{1,0},{2,3},{3,2},{4,5},{5,4},{6,7},{7,6},{8,9},{9,8},{10,11... | collective-permute-start | bytes 786440 | tf_op jit(solution)/shard_map/ppermute | solution.py:470
  5.0 9.7 %collective-permute-start.4 = (bf16[2,8,64,128]{3,2,1,0:T(8,128)(2,1)S(1)}, bf16[2,8,64,128]{3,2,1,0:T(8,128)(2,1)S(1)}, u32[]{:S(2)}, u32[]{:S(2)}) collective-permute-start(bf16[2,8,64,128]{3,2,1,0:T(8,128)(2,1)S(1)} %get-tuple-element.36), channel_id=1, source_target_pairs={{0,2},{1,3},{2,0},{3,1},{4,6},{5,7},{6,4},{7,5},{8,10},{9,11},{10,... | collective-permute-start | bytes 786440 | tf_op jit(solution)/shard_map/ppermute | solution.py:470
  7.5 12.3 %collective-permute-start.5 = (bf16[2,8,64,128]{3,2,1,0:T(8,128)(2,1)S(1)}, bf16[2,8,64,128]{3,2,1,0:T(8,128)(2,1)S(1)}, u32[]{:S(2)}, u32[]{:S(2)}) collective-permute-start(bf16[2,8,64,128]{3,2,1,0:T(8,128)(2,1)S(1)} %get-tuple-element.37), channel_id=1, source_target_pairs={{0,3},{1,2},{2,1},{3,0},{4,7},{5,6},{6,5},{7,4},{8,11},{9,10},{10,... | collective-permute-start | bytes 786440 | tf_op jit(solution)/shard_map/ppermute | solution.py:470
  19.8 0.7 copy-start.6
  20.5 1.0 copy-start.7
  21.5 11.7 %copy-start.1 = (bf16[2,8,2,32768]{3,2,1,0:T(2,128)(2,1)S(1)}, bf16[2,8,2,32768]{3,2,1,0:T(2,128)(2,1)}, u32[]{:S(2)}) copy-start(bf16[2,8,2,32768]{3,2,1,0:T(2,128)(2,1)} %param.6) | copy-start | bytes 6291460
  26.3 1.0 copy-start.4
  27.2 35.5 %all-to-all-start.1 = ((bf16[32,2,4,16,128]{4,3,2,1,0:T(8,128)(2,1)}), bf16[32,2,4,16,128]{4,3,2,1,0:T(8,128)(2,1)}, u32[]{:S(2)}, u32[]{:S(2)}) async-start(bf16[32,2,4,16,128]{4,3,2,1,0:T(8,128)(2,1)} %bitcast.13), calls=%async_computation.1 | async-start | bytes 2097152 | tf_op jit(solution)/shard_map/all_to_all | solution.py:499
  36.0 1.9 %collective-permute-start = (bf16[2,8,64,128]{3,2,1,0:T(8,128)(2,1)S(1)}, bf16[2,8,64,128]{3,2,1,0:T(8,128)(2,1)S(1)}, u32[]{:S(2)}, u32[]{:S(2)}) collective-permute-start(bf16[2,8,64,128]{3,2,1,0:T(8,128)(2,1)S(1)} %get-tuple-element.31), channel_id=1, source_target_pairs={{0,1},{1,0},{2,3},{3,2},{4,5},{5,4},{6,7},{7,6},{8,9},{9,8},{10,11... | collective-permute-start | bytes 786440 | tf_op jit(solution)/shard_map/ppermute | solution.py:470
  36.3 15.5 %collective-permute-start.1 = (bf16[2,8,64,128]{3,2,1,0:T(8,128)(2,1)S(1)}, bf16[2,8,64,128]{3,2,1,0:T(8,128)(2,1)S(1)}, u32[]{:S(2)}, u32[]{:S(2)}) collective-permute-start(bf16[2,8,64,128]{3,2,1,0:T(8,128)(2,1)S(1)} %get-tuple-element.32), channel_id=1, source_target_pairs={{0,2},{1,3},{2,0},{3,1},{4,6},{5,7},{6,4},{7,5},{8,10},{9,11},{10,... | collective-permute-start | bytes 786440 | tf_op jit(solution)/shard_map/ppermute | solution.py:470
  37.9 21.2 %collective-permute-start.2 = (bf16[2,8,64,128]{3,2,1,0:T(8,128)(2,1)S(1)}, bf16[2,8,64,128]{3,2,1,0:T(8,128)(2,1)S(1)}, u32[]{:S(2)}, u32[]{:S(2)}) collective-permute-start(bf16[2,8,64,128]{3,2,1,0:T(8,128)(2,1)S(1)} %get-tuple-element.33), channel_id=1, source_target_pairs={{0,3},{1,2},{2,1},{3,0},{4,7},{5,6},{6,5},{7,4},{8,11},{9,10},{10,... | collective-permute-start | bytes 786440 | tf_op jit(solution)/shard_map/ppermute | solution.py:470
  59.1 7.2 %copy-start.11 = (f32[128,64]{0,1:T(8,128)S(1)}, f32[128,64]{0,1:T(8,128)}, u32[]{:S(2)}) copy-start(f32[128,64]{0,1:T(8,128)} %param.7) | copy-start | bytes 98308
  59.1 7.4 %copy-start.9 = (s32[32]{0:T(128)S(1)}, s32[32]{0:T(128)}, u32[]{:S(2)}) copy-start(s32[32]{0:T(128)} %beam_ref.3) | copy-start | bytes 388
  59.1 7.4 %copy-start.10 = (s32[64]{0:T(128)S(1)}, s32[64]{0:T(128)}, u32[]{:S(2)}) copy-start(s32[64]{0:T(128)} %group_ref.3) | copy-start | bytes 772
  62.7 10.8 %copy-start.5 = (bf16[256,256]{1,0:T(8,128)(2,1)S(1)}, bf16[256,256]{1,0:T(8,128)(2,1)}, u32[]{:S(2)}) copy-start(bf16[256,256]{1,0:T(8,128)(2,1)} %constant.137.clone.table_ref.refs_1_) | copy-start | bytes 393220
  62.7 29.8 %all-to-all-start = ((bf16[32,2,4,16,128]{4,3,2,1,0:T(8,128)(2,1)}), bf16[32,2,4,16,128]{4,3,2,1,0:T(8,128)(2,1)}, u32[]{:S(2)}, u32[]{:S(2)}) async-start(bf16[32,2,4,16,128]{4,3,2,1,0:T(8,128)(2,1)} %bitcast.5), calls=%async_computation | async-start | bytes 2097152 | tf_op jit(solution)/shard_map/all_to_all | solution.py:499
  80.2 1.3 %copy-start.2 = (f32[8,4,2,2,4,8,128]{6,5,4,3,2,1,0:T(8,128)}, f32[8,4,2,2,4,8,128]{6,5,4,3,2,1,0:T(8,128)S(1)}, u32[]{:S(2)}) copy-start(f32[8,4,2,2,4,8,128]{6,5,4,3,2,1,0:T(8,128)S(1)} %get-tuple-element.45.refs_5_.refs_4_) | copy-start | bytes 6291460
  92.5 1.6 %copy-start.3 = (f32[8,4,2,2,4,8,128]{6,5,4,3,2,1,0:T(8,128)S(1)}, f32[8,4,2,2,4,8,128]{6,5,4,3,2,1,0:T(8,128)}, u32[]{:S(2)}) copy-start(f32[8,4,2,2,4,8,128]{6,5,4,3,2,1,0:T(8,128)} %copy-done.2) | copy-start | bytes 6291460
  100.9 7.4 %collective-permute-start.6 = (bf16[4,2,2,4,8,128]{5,4,3,2,1,0:T(8,128)(2,1)S(1)}, bf16[4,2,2,4,8,128]{5,4,3,2,1,0:T(8,128)(2,1)S(1)}, u32[]{:S(2)}, u32[]{:S(2)}) collective-permute-start(bf16[4,2,2,4,8,128]{5,4,3,2,1,0:T(8,128)(2,1)S(1)} %get-tuple-element.48), channel_id=1, source_target_pairs={{0,4},{4,0},{8,12},{12,8},{16,20},{20,16},{24,28},{28,24},{1,5},{5... | collective-permute-start | bytes 393224 | tf_op jit(solution)/shard_map/ppermute | solution.py:470
  102.5 9.5 %collective-permute-start.7 = (bf16[4,2,2,4,8,128]{5,4,3,2,1,0:T(8,128)(2,1)S(1)}, bf16[4,2,2,4,8,128]{5,4,3,2,1,0:T(8,128)(2,1)S(1)}, u32[]{:S(2)}, u32[]{:S(2)}) collective-permute-start(bf16[4,2,2,4,8,128]{5,4,3,2,1,0:T(8,128)(2,1)S(1)} %get-tuple-element.49), channel_id=1, source_target_pairs={{0,8},{4,12},{8,0},{12,4},{16,24},{20,28},{24,16},{28,20},{1,9},{5... | collective-permute-start | bytes 393224 | tf_op jit(solution)/shard_map/ppermute | solution.py:470
  103.1 10.2 %collective-permute-start.8 = (bf16[4,2,2,4,8,128]{5,4,3,2,1,0:T(8,128)(2,1)S(1)}, bf16[4,2,2,4,8,128]{5,4,3,2,1,0:T(8,128)(2,1)S(1)}, u32[]{:S(2)}, u32[]{:S(2)}) collective-permute-start(bf16[4,2,2,4,8,128]{5,4,3,2,1,0:T(8,128)(2,1)S(1)} %get-tuple-element.50), channel_id=1, source_target_pairs={{0,12},{4,8},{8,4},{12,0},{16,28},{20,24},{24,20},{28,16},{1,13},{... | collective-permute-start | bytes 393224 | tf_op jit(solution)/shard_map/ppermute | solution.py:470
  104.5 18.5 %collective-permute-start.9 = (bf16[4,2,2,4,8,128]{5,4,3,2,1,0:T(8,128)(2,1)S(1)}, bf16[4,2,2,4,8,128]{5,4,3,2,1,0:T(8,128)(2,1)S(1)}, u32[]{:S(2)}, u32[]{:S(2)}) collective-permute-start(bf16[4,2,2,4,8,128]{5,4,3,2,1,0:T(8,128)(2,1)S(1)} %get-tuple-element.51), channel_id=1, source_target_pairs={{0,16},{4,20},{8,24},{12,28},{16,0},{20,4},{24,8},{28,12},{1,17},{... | collective-permute-start | bytes 393224 | tf_op jit(solution)/shard_map/ppermute | solution.py:470
  105.2 21.5 %collective-permute-start.10 = (bf16[4,2,2,4,8,128]{5,4,3,2,1,0:T(8,128)(2,1)S(1)}, bf16[4,2,2,4,8,128]{5,4,3,2,1,0:T(8,128)(2,1)S(1)}, u32[]{:S(2)}, u32[]{:S(2)}) collective-permute-start(bf16[4,2,2,4,8,128]{5,4,3,2,1,0:T(8,128)(2,1)S(1)} %get-tuple-element.52), channel_id=1, source_target_pairs={{0,20},{4,16},{8,28},{12,24},{16,4},{20,0},{24,12},{28,8},{1,21},{... | collective-permute-start | bytes 393224 | tf_op jit(solution)/shard_map/ppermute | solution.py:470
  108.3 18.4 %collective-permute-start.11 = (bf16[4,2,2,4,8,128]{5,4,3,2,1,0:T(8,128)(2,1)S(1)}, bf16[4,2,2,4,8,128]{5,4,3,2,1,0:T(8,128)(2,1)S(1)}, u32[]{:S(2)}, u32[]{:S(2)}) collective-permute-start(bf16[4,2,2,4,8,128]{5,4,3,2,1,0:T(8,128)(2,1)S(1)} %get-tuple-element.53), channel_id=1, source_target_pairs={{0,24},{4,28},{8,16},{12,20},{16,8},{20,12},{24,0},{28,4},{1,25},{... | collective-permute-start | bytes 393224 | tf_op jit(solution)/shard_map/ppermute | solution.py:470
  112.0 14.7 %collective-permute-start.12 = (bf16[4,2,2,4,8,128]{5,4,3,2,1,0:T(8,128)(2,1)S(1)}, bf16[4,2,2,4,8,128]{5,4,3,2,1,0:T(8,128)(2,1)S(1)}, u32[]{:S(2)}, u32[]{:S(2)}) collective-permute-start(bf16[4,2,2,4,8,128]{5,4,3,2,1,0:T(8,128)(2,1)S(1)} %get-tuple-element.54), channel_id=1, source_target_pairs={{0,28},{4,24},{8,20},{12,16},{16,12},{20,8},{24,4},{28,0},{1,29},{... | collective-permute-start | bytes 393224 | tf_op jit(solution)/shard_map/ppermute | solution.py:470

commit v3 on v2

--- a/solution.py
+++ b/solution.py
@@ -55,20 +55,20 @@
     planes = np.stack([np.stack([cosine, sine]), np.stack([-sine, cosine])])
     planes = planes.reshape(2, 2, TF, LOW, CH_LO)
     table = np.einsum("oitkn,pr->otpkinr", planes, np.eye(2))
-    return jnp.asarray(table.reshape(4 * CH_LO, 4 * CH_LO), BF)
+    return jnp.asarray(table.reshape(2, TF, 2 * LOW, 4 * CH_LO), BF)
 
 
 def second_table():
     cosine, sine = dft_pair(CH_HI)
     table = np.block([[cosine, -sine], [sine, cosine]])
-    return jnp.asarray(table, BF)
+    return jnp.asarray(table.reshape(2, TF, PART, 2 * CH_HI), BF)
 
 
 def twiddle_rows(part):
-    shape = (2 * CH_LO, LANES)
-    row = lax.broadcasted_iota(jnp.int32, shape, 0)
-    k2 = row // (2 * LOW) * LOW + row % LOW
-    n1 = part * PART + lax.broadcasted_iota(jnp.int32, shape, 1) % PART
+    shape = (TF, 2 * LOW, LANES)
+    k2 = lax.broadcasted_iota(jnp.int32, shape, 0) * LOW
+    k2 = k2 + lax.broadcasted_iota(jnp.int32, shape, 1) % LOW
+    n1 = part * PART + lax.broadcasted_iota(jnp.int32, shape, 2) % PART
     angle = TWO_PI / POINTS * (k2 * n1).astype(F32)
     return jnp.cos(angle), jnp.sin(angle)
 
@@ -104,28 +104,20 @@
     return out
 
 
-def spread_kernel(chunk, me_ref, volt_ref, *refs):
-    outs, (in_ref, sem) = refs[:TF], refs[TF:]
-    planes, _, frames, _, _ = volt_ref.shape
-    reads = [
-        pltpu.make_async_copy(volt_ref.at[q, pl.ds(chunk * PER, PER)], in_ref.at[q], sem.at[q])
-        for q in range(planes)
-    ]
-    for read in reads:
-        read.start()
-    for q in range(planes):
-        reads[q].wait()
-        for me in range(TF):
-
-            @pl.when(me_ref[0] == me)
-            def _(me=me, q=q):
-                def one(f, carry):
-                    parts = [in_ref[q, a, f] for a in range(PER)]
-                    for j, block in enumerate(swap_lane_blocks(parts)):
-                        outs[j ^ me][q, f] = block
-                    return carry
-
-                lax.fori_loop(0, frames, one, 0)
+def spread_kernel(chunk, me_ref, volt_ref, *outs):
+    planes, _, frames = volt_ref.shape[:3]
+    for me in range(TF):
+
+        @pl.when(me_ref[0] == me)
+        def _(me=me):
+            def one(step, carry):
+                q, f = step // frames, step % frames
+                parts = [volt_ref[q, chunk * PER + a, f] for a in range(PER)]
+                for j, block in enumerate(swap_lane_blocks(parts)):
+                    outs[j ^ me][q, f] = block
+                return carry
+
+            lax.fori_loop(0, planes * frames, one, 0, unroll=2)
 
 
 def spread(me, volt, chunk):
@@ -133,21 +125,18 @@
     return pl.pallas_call(
         functools.partial(spread_kernel, chunk),
         name="spread",
-        in_specs=[SMEM, HBM],
+        in_specs=[SMEM, VMEM],
         out_specs=[VMEM] * TF,
         out_shape=[jax.ShapeDtypeStruct((planes, frames, rows, LANES), BF)] * TF,
-        scratch_shapes=[
-            pltpu.VMEM((planes, PER, frames, rows, LANES), BF),
-            pltpu.SemaphoreType.DMA((planes,)),
-        ],
-        compiler_params=params(6),
+        compiler_params=params(2),
         cost_estimate=cost(4),
     )(me, volt)
 
 
-def channel_kernel(me_ref, *refs):
+def channel_kernel(split, me_ref, *refs):
     sources = refs[:TF]
-    win_ref, table_ref, cos_ref, sin_ref, out_ref, stage_ref, filt_ref, done_ref, sem = refs[TF:]
+    win_ref, table_ref, cos_ref, sin_ref = refs[TF : TF + 4]
+    stage_ref, filt_ref = refs[-2:] if split else refs[-4:-2]
     me = me_ref[0]
     rows = 2 * CH_LO
     history = TAPS - 1
@@ -173,14 +162,20 @@
     for q in range(planes):
         lax.fori_loop(0, rows // strip, functools.partial(one_strip, q), 0)
 
-    table = table_ref[...]
+    ranges = [(me ^ t) if split else t for t in range(TF)]
+    table = jnp.concatenate([table_ref[o, t] for o in range(planes) for t in ranges], axis=0)
     per_dest = frames // STN
-
-    def send(dest):
-        return pltpu.make_async_copy(done_ref.at[dest], out_ref.at[dest], sem.at[dest])
+    if split:
+        outs = refs[TF + 4 : TF + 4 + TF]
+    else:
+        out_ref, done_ref, sem = refs[TF + 4], refs[-2], refs[-1]
+
+        def send(dest):
+            return pltpu.make_async_copy(done_ref.at[dest], out_ref.at[dest], sem.at[dest])
 
     def one_dest(dest, carry):
-        cosine, sine = cos_ref[...], sin_ref[...]
+        cosine = jnp.concatenate([cos_ref[t] for t in ranges], axis=0)
+        sine = jnp.concatenate([sin_ref[t] for t in ranges], axis=0)
         for pair in range(per_dest // 2):
             f = per_dest * dest + 2 * pair
             left = filt_ref[f].reshape(2 * rows, LANES)
@@ -193,31 +188,43 @@
                 turned = (real * cosine + imag * sine, imag * cosine - real * sine)
                 for o in range(2):
                     value = turned[o].astype(BF).reshape(TF, 2 * LOW, LANES)
-                    done_ref[dest, :, o, 2 * pair + side] = value
-        send(dest).start()
+                    if split:
+                        for d in range(TF):
+                            outs[d][dest, o, 2 * pair + side] = value[d]
+                    else:
+                        done_ref[dest, :, o, 2 * pair + side] = value
+        if not split:
+            send(dest).start()
         return carry
 
     lax.fori_loop(0, STN, one_dest, 0, unroll=2)
-    for dest in range(STN):
-        send(dest).wait()
-
-
-def channel_step(me, blocks, window, table, cosine, sine):
+    if not split:
+        for dest in range(STN):
+            send(dest).wait()
+
+
+def channel_step(me, blocks, window, table, cosine, sine, split):
     planes, per_source, rows, _ = blocks[0].shape
     frames = TF * per_source
-    out = (STN, TF, planes, frames // STN, 2 * LOW, LANES)
+    tail = (planes, frames // STN, 2 * LOW, LANES)
+    scratch = [
+        pltpu.VMEM((planes, frames, rows, LANES), BF),
+        pltpu.VMEM((frames, planes, rows, LANES), BF),
+    ]
+    if split:
+        out_shape = [jax.ShapeDtypeStruct((STN,) + tail, BF)] * TF
+        out_specs = [VMEM] * TF
+    else:
+        out = (STN, TF) + tail
+        out_shape, out_specs = jax.ShapeDtypeStruct(out, BF), HBM
+        scratch += [pltpu.VMEM(out, BF), pltpu.SemaphoreType.DMA((STN,))]
     return pl.pallas_call(
-        channel_kernel,
+        functools.partial(channel_kernel, split),
         name="channel_step",
         in_specs=[SMEM] + [VMEM] * (TF + 4),
-        out_specs=HBM,
-        out_shape=jax.ShapeDtypeStruct(out, BF),
-        scratch_shapes=[
-            pltpu.VMEM((planes, frames, rows, LANES), BF),
-            pltpu.VMEM((frames, planes, rows, LANES), BF),
-            pltpu.VMEM(out, BF),
-            pltpu.SemaphoreType.DMA((STN,)),
-        ],
+        out_specs=out_specs,
+        out_shape=out_shape,
+        scratch_shapes=scratch,
         compiler_params=params(12),
         cost_estimate=cost(8, 1 << 29),
     )(me, *blocks, window, table, cosine, sine)
@@ -234,7 +241,10 @@
     fraction = channel.astype(F32) / float(POINTS)
 
     def station(member):
-        return (member // PER) * (PER * CHUNKS) + chunk * PER + member % PER
+        source = member // PER
+        if chunk:
+            source = source ^ at_ref[1]
+        return source * (PER * CHUNKS) + chunk * PER + member % PER
 
     def one_member(member, carry):
         s = station(member)
@@ -308,22 +318,47 @@
     )(at, delay_table, beam_pointing, station_group)
 
 
-def transform(blocks_ref, table_ref, chan_ref):
-    sources, _, _, per_dest = blocks_ref.shape[:4]
-    rows = per_dest * 2 * LOW
-    table = table_ref[...]
-    for src in range(sources):
-        planes = []
+def transform(parts_of, table, put):
+    planes = [swap_lane_blocks(parts_of(o)) for o in range(2)]
+    for a in range(PER):
+        both = jnp.concatenate([planes[0][a], planes[1][a]], axis=1)
+        spectrum = jnp.dot(both, table, preferred_element_type=F32)
         for o in range(2):
-            parts = [blocks_ref[src, j, o].reshape(rows, LANES) for j in range(TF)]
-            planes.append(swap_lane_blocks(parts))
-        for a in range(PER):
-            both = jnp.concatenate([planes[0][a], planes[1][a]], axis=1)
-            spectrum = jnp.dot(both, table, preferred_element_type=F32)
-            for o in range(2):
-                value = spectrum[:, o * LANES : (o + 1) * LANES]
-                chan_ref[src * PER + a, o] = value.reshape(per_dest * 2, LOW, LANES)
-    chan_ref[chan_ref.shape[0] - 1] = jnp.zeros(chan_ref.shape[1:], F32)
+            put(a, o, spectrum[:, o * LANES : (o + 1) * LANES])
+
+
+def table_of(table_ref, parts):
+    return jnp.concatenate([table_ref[q, j] for q in range(2) for j in parts], axis=0)
+
+
+def middle_kernel(at_ref, *refs):
+    blocks, table_ref, outs = refs[:TF], refs[TF], refs[TF + 1 :]
+    me, owner = at_ref[0], at_ref[1]
+    per_dest = blocks[0].shape[2]
+    table = table_of(table_ref, [me ^ d for d in range(TF)])
+    for e, out in enumerate(outs):
+
+        def parts_of(o, e=e):
+            return [block[owner ^ e, o].reshape(per_dest * 2 * LOW, LANES) for block in blocks]
+
+        def put(a, o, value, out=out):
+            out[a, o] = value.astype(BF)
+
+        transform(parts_of, table, put)
+
+
+def middle_step(at, blocks, table):
+    _, planes, per_dest, _, _ = blocks[0].shape
+    out = (PER, planes, per_dest * 2 * LOW, LANES)
+    return pl.pallas_call(
+        middle_kernel,
+        name="middle_step",
+        in_specs=[SMEM] + [VMEM] * (TF + 1),
+        out_specs=[VMEM] * STN,
+        out_shape=[jax.ShapeDtypeStruct(out, BF)] * STN,
+        compiler_params=params(4),
+        cost_estimate=cost(4, 1 << 28),
+    )(at, *blocks, table)
 
 
 def form_beams_of(offsets, chan_ref, weight_ref, order_ref, start_ref, put):
@@ -361,81 +396,89 @@
     lax.fori_loop(0, GROUPS * blocks, one_block, 0)
 
 
-def early_kernel(blocks_ref, table_ref, weight_ref, order_ref, start_ref, at_ref, sum_ref, next_ref, chan_ref):
-    next_ref[0], next_ref[1] = at_ref[0], at_ref[1]
-    transform(blocks_ref, table_ref, chan_ref)
-
-    def put(d, g, o, fp, value):
+def early_kernel(blocks_ref, table_ref, weight_ref, order_ref, start_ref, sum_hbm, chan_ref, sum_ref, sem):
+    sources, _, _, per_dest = blocks_ref.shape[:4]
+    table = table_of(table_ref, range(TF))
+    for src in range(sources):
+
+        def parts_of(o, src=src):
+            return [blocks_ref[src, j, o].reshape(per_dest * 2 * LOW, LANES) for j in range(TF)]
+
+        def put(a, o, value, src=src):
+            chan_ref[src * PER + a, o] = value.reshape(per_dest * 2, LOW, LANES)
+
+        transform(parts_of, table, put)
+    chan_ref[chan_ref.shape[0] - 1] = jnp.zeros(chan_ref.shape[1:], F32)
+
+    def keep(d, g, o, fp, value):
         sum_ref[d, g, o, fp % 2, fp // 2] = value
 
-    form_beams_of(range(weight_ref.shape[1]), chan_ref, weight_ref, order_ref, start_ref, put)
-
-
-def late_kernel(offsets, fresh, *refs):
+    form_beams_of(range(weight_ref.shape[1]), chan_ref, weight_ref, order_ref, start_ref, keep)
+    write = pltpu.make_async_copy(sum_ref, sum_hbm, sem)
+    write.start()
+    write.wait()
+
+
+def late_kernel(offsets, fresh, weight_ref, order_ref, start_ref, sum_hbm, *refs):
+    sum_ref, sem = refs[-2:]
+    read = pltpu.make_async_copy(sum_hbm.at[pl.ds(offsets[0], len(offsets))], sum_ref, sem)
+    read.start()
     if fresh:
-        blocks_ref, table_ref, weight_ref, order_ref, start_ref, sum_ref = refs[:6]
-        chan_ref, outs = refs[6], refs[7:]
-        transform(blocks_ref, table_ref, chan_ref)
+        blocks, chan_ref, outs = refs[:STN], refs[STN], refs[STN + 1 : -2]
+        members, planes, both = chan_ref.shape[:3]
+        for e, block in enumerate(blocks):
+            value = block[...].astype(F32)
+            chan_ref[pl.ds(e * PER, PER)] = value.reshape(PER, planes, both, LOW, LANES)
+        chan_ref[members - 1] = jnp.zeros(chan_ref.shape[1:], F32)
     else:
-        chan_ref, weight_ref, order_ref, start_ref, sum_ref = refs[:5]
-        outs = refs[5:]
+        chan_ref, outs = refs[0], refs[1:-2]
+    read.wait()
 
     def put(d, g, o, fp, value):
         f, p = fp // 2, fp % 2
-        outs[d - offsets[0]][g, o, p, f] = (value + sum_ref[d, g, o, p, f]).astype(BF)
+        at = d - offsets[0]
+        outs[at][g, o, p, f] = (value + sum_ref[at, g, o, p, f]).astype(BF)
 
     form_beams_of(offsets, chan_ref, weight_ref, order_ref, start_ref, put)
 
 
-def beam_shapes(blocks, weights):
+def beams_early(blocks, table, weights, order, start):
     planes, per_dest = blocks.shape[2:4]
-    one = (GROUPS, planes, 2, per_dest, LOW, LANES)
-    return one, (weights.shape[0], planes, 2 * per_dest, LOW, LANES)
-
-
-def beams_early(blocks, table, weights, order, start, at):
-    one, chan = beam_shapes(blocks, weights)
+    out = (weights.shape[1], GROUPS, planes, 2, per_dest, LOW, LANES)
     return pl.pallas_call(
         early_kernel,
         name="beams_early",
-        in_specs=[VMEM] * 3 + [SMEM] * 3,
-        out_specs=[VMEM, SMEM],
-        out_shape=[
-            jax.ShapeDtypeStruct((weights.shape[1],) + one, F32),
-            jax.ShapeDtypeStruct(at.shape, at.dtype),
+        in_specs=[VMEM] * 3 + [SMEM] * 2,
+        out_specs=HBM,
+        out_shape=jax.ShapeDtypeStruct(out, F32),
+        scratch_shapes=[
+            pltpu.VMEM((weights.shape[0], planes, 2 * per_dest, LOW, LANES), F32),
+            pltpu.VMEM(out, F32),
+            pltpu.SemaphoreType.DMA,
         ],
-        scratch_shapes=[pltpu.VMEM(chan, F32)],
         compiler_params=params(12),
         cost_estimate=cost(8, 1 << 29),
-    )(blocks, table, weights, order, start, at)
-
-
-def beams_far(blocks, table, weights, order, start, partial):
-    one, chan = beam_shapes(blocks, weights)
-    offsets = range(weights.shape[1] // 2, weights.shape[1])
-    outs = pl.pallas_call(
-        functools.partial(late_kernel, offsets, True),
-        name="beams_far",
-        in_specs=[VMEM] * 3 + [SMEM] * 2 + [VMEM],
-        out_specs=[VMEM] * (1 + len(offsets)),
-        out_shape=[jax.ShapeDtypeStruct(chan, F32)] + [jax.ShapeDtypeStruct(one, BF)] * len(offsets),
+    )(blocks, table, weights, order, start)
+
+
+def beams_late(offsets, blocks, weights, order, start, partial):
+    fresh = isinstance(blocks, list)
+    more = blocks if fresh else [blocks]
+    one = partial.shape[1:]
+    out_shape = [jax.ShapeDtypeStruct(one, BF)] * len(offsets)
+    if fresh:
+        chan = (weights.shape[0], one[1], one[2] * one[3], LOW, LANES)
+        out_shape = [jax.ShapeDtypeStruct(chan, F32)] + out_shape
+    return pl.pallas_call(
+        functools.partial(late_kernel, offsets, fresh),
+        name="beams_late",
+        in_specs=[VMEM, SMEM, SMEM, HBM] + [VMEM] * len(more),
+        out_specs=[VMEM] * len(out_shape),
+        out_shape=out_shape,
+        scratch_shapes=[pltpu.VMEM((len(offsets),) + one, F32), pltpu.SemaphoreType.DMA],
         compiler_params=params(12),
         cost_estimate=cost(8, 1 << 29),
-    )(blocks, table, weights, order, start, partial)
-    return outs[0], outs[1:]
-
-
-def beams_near(chan, weights, order, start, partial):
-    offsets = range(weights.shape[1] // 2)
-    return pl.pallas_call(
-        functools.partial(late_kernel, offsets, False),
-        name="beams_near",
-        in_specs=[VMEM] * 2 + [SMEM] * 2 + [VMEM],
-        out_specs=[VMEM] * len(offsets),
-        out_shape=[jax.ShapeDtypeStruct(partial.shape[1:], BF)] * len(offsets),
-        compiler_params=params(12),
-        cost_estimate=cost(8, 1 << 29),
-    )(chan, weights, order, start, partial)
+    )(weights, order, start, partial, *more)
 
 
 def gather_kernel(me_ref, *refs):
@@ -491,24 +534,31 @@
             row.append(swapped(own[d], "tf", d))
         blocks.append(row)
 
-    turned = []
-    for chunk in range(CHUNKS):
-        value = channel_step(me, blocks[chunk], window, first, cosine, sine)
-        shape = value.shape
-        value = value.reshape((STN * TF,) + shape[2:])
-        value = lax.all_to_all(value, ("stn", "tf"), split_axis=0, concat_axis=0, tiled=True)
-        turned.append(value.reshape(shape))
+    value = channel_step(me, blocks[0], window, first, cosine, sine, False)
+    shape = value.shape
+    value = value.reshape((STN * TF,) + shape[2:])
+    value = lax.all_to_all(value, ("stn", "tf"), split_axis=0, concat_axis=0, tiled=True)
+    turned = value.reshape(shape)
+
+    own = channel_step(me, blocks[1], window, first, cosine, sine, True)
+    row = [own[0]]
+    for d in range(1, TF):
+        row.append(swapped(own[d], "tf", d))
+    own = middle_step(at, row, second)
+    late = [own[0]]
+    for e in range(1, STN):
+        late.append(swapped(own[e], "stn", e))
 
     args = (delay_table, beam_pointing, station_group)
     weights = beam_weights(at, 0, *args)
-    partial, at = beams_early(turned[0], second, *weights, at)
+    partial = beams_early(turned, second, *weights)
     weights = beam_weights(at, 1, *args)
-    chan, far = beams_far(turned[1], second, *weights, partial)
+    chan, *far = beams_late(range(STN // 2, STN), late, *weights, partial)
     parts = [None] * STN
     for i, value in enumerate(far):
         d = STN // 2 + i
         parts[d] = swapped(value, "stn", d)
-    near = beams_near(chan, *weights, partial)
+    near = beams_late(range(STN // 2), chan, *weights, partial)
     for d, value in enumerate(near):
         parts[d] = swapped(value, "stn", d) if d else value
     return gather_frames(owner, parts)

time: 129 us -> 145 us (1.12)
  starting transfers between devices: 24.4 us -> 37 us
  waiting for transfers between devices: 50.5 us -> 55.5 us
  Pallas kernels: 42.4 us -> 39.2 us
  local copies, waits for them, and re-layouts: 7.25 us -> 9.69 us
    ppermute x13 -> x23, starting transfers between devices: 14.9 us -> 31.1 us  [swapped(): return lax.ppermute(value, axis, [(i, i ^ offset) for i in range(count)])]
    ppermute x13 -> x23, waiting for transfers between devices: 46.5 us -> 55.5 us  [swapped(): return lax.ppermute(value, axis, [(i, i ^ offset) for i in range(count)])]
    all_to_all x2 -> x1, waiting for transfers between devices: 3.99 us -> 0.01 us  [fast_body(): lax.all_to_all(value, ('stn', 'tf'), split_axis=0, concat_axis=0, tiled=T...]
    all_to_all x2 -> x1, starting transfers between devices: 9.54 us -> 5.93 us  [fast_body(): lax.all_to_all(value, ('stn', 'tf'), split_axis=0, concat_axis=0, tiled=T...]
    pallas_call x2, Pallas kernels: 5.62 us -> 3.16 us  [spread(): pl.pallas_call(functools.partial(spread_kernel, chunk), name='spread', in...]
    unnamed x25 -> x35, local copies, waits for them, and re-layouts: 7.25 us -> 9.69 us
    pallas_call x4 -> x5, Pallas kernels: 15.1 us -> 14.6 us  [the longest x2 6.39 us: channel_step(): pl.pallas_call(functools.partial(channel_kernel, split), name='channel_st...]
  transfers between devices with their start and end apart: 15 -> 24, of which waited for: 9 -> 8; matrix products, arithmetic and copies ran while one was open for 2% -> 2% of each run, Pallas kernels for 21% -> 19%
where the time goes in v3:
time: 145 us
  waiting for transfers between devices  55.5 us (38%)
  Pallas kernels  39.2 us (27%)
  starting transfers between devices  37 us (26%)
  local copies, waits for them, and re-layouts  9.69 us (7%)
  other arithmetic  2.81 us (2%)
    ppermute x23, waiting for transfers between devices, swapped(): return lax.ppermute(value, axis, [(i, i ^ offset) for i in range(count)])  55.5 us
    ppermute x23, starting transfers between devices, swapped(): return lax.ppermute(value, axis, [(i, i ^ offset) for i in range(count)])  31.1 us
    pallas_call x2, Pallas kernels, beam_weights(): pl.pallas_call(functools.partial(weight_kernel, chunk), name='beam_weight...  14.1 us
    unnamed x35, local copies, waits for them, and re-layouts  9.69 us
    pallas_call x2, Pallas kernels, channel_step(): pl.pallas_call(functools.partial(channel_kernel, split), name='channel_st...  6.39 us
    pallas_call x1, Pallas kernels, beams_early(): pl.pallas_call(early_kernel, name='beams_early', in_specs=[VMEM] * 3 + [S...  6.24 us
    all_to_all x1, starting transfers between devices, fast_body(): lax.all_to_all(value, ('stn', 'tf'), split_axis=0, concat_axis=0, tiled=T...  5.93 us
    pallas_call x2, Pallas kernels, beams_late(): pl.pallas_call(functools.partial(late_kernel, offsets, fresh), name='beam...  5.81 us
  transfers between devices with their start and end apart: 24, of which 8 were waited for; matrix products, arithmetic and copies ran while one was open for 2% of the time, Pallas kernels for 19%

profile of v3, /device:TPU:0, one launch (start us, length us, event | category | flops | bytes accessed | tf_op | source)
XLA Modules:
  0.0 144.5 jit_solution(16506264180028719006)
XLA Ops:
  0.0 1.6 %copy-done = bf16[2,8,2,32768]{3,2,1,0:T(2,128)(2,1)S(1)} copy-done((bf16[2,8,2,32768]{3,2,1,0:T(2,128)(2,1)S(1)}, bf16[2,8,2,32768]{3,2,1,0:T(2,128)(2,1)}, u32[]{:S(2)}) %copy-start) | copy-done | bytes 2097176
  1.6 1.6 %spread.2 = (bf16[2,8,64,128]{3,2,1,0:T(8,128)(2,1)S(1)}, bf16[2,8,64,128]{3,2,1,0:T(8,128)(2,1)S(1)}, bf16[2,8,64,128]{3,2,1,0:T(8,128)(2,1)S(1)}, bf16[2,8,64,128]{3,2,1,0:T(8,128)(2,1)S(1)}) custom-call(s32[1]{0:T(128)} %bitcast.1.me_ref, bf16[2,8,8,64,128]{4,3,2,1,0:T(8,128)(2,1)S(1)} %bitcast.9), custom_call_target="tpu_custom_call" | custom-call | bytes 4194304 | tf_op jit(solution)/shard_map/spread/pallas_call | solution.py:125
  3.7 2.6 %collective-permute-start.1 = (bf16[2,8,64,128]{3,2,1,0:T(8,128)(2,1)S(1)}, bf16[2,8,64,128]{3,2,1,0:T(8,128)(2,1)S(1)}, u32[]{:S(2)}, u32[]{:S(2)}) collective-permute-start(bf16[2,8,64,128]{3,2,1,0:T(8,128)(2,1)S(1)} %get-tuple-element.45), channel_id=1, source_target_pairs={{0,2},{1,3},{2,0},{3,1},{4,6},{5,7},{6,4},{7,5},{8,10},{9,11},{10,... | collective-permute-start | bytes 786440 | tf_op jit(solution)/shard_map/ppermute | solution.py:513
  6.4 2.5 %fusion.4.refs_4_ = f32[16,64,128]{2,1,0:T(8,128)S(1)} fusion(s32[128]{0:T(128)S(1)} %get-tuple-element.79, s32[128]{0:T(128)S(1)} %get-tuple-element.80, s32[]{:T(128)S(6)} %mul.101, s32[64]{0:T(128)S(1)} %get-tuple-element.77, s32[64]{0:T(128)S(1)} %get-tuple-element.78, s32[16]{0:T(128)S(1)} %iota_multiply_fusion.1, ...), kind=kLoop, calls=%fused_computation.10 | loop fusion | flops 6029312 | bytes 526084 | tf_op jit(solution)/shard_map/mul | solution.py:35
  9.1 4.3 %collective-permute-done.1.refs_2_ = bf16[2,8,64,128]{3,2,1,0:T(8,128)(2,1)S(1)} collective-permute-done((bf16[2,8,64,128]{3,2,1,0:T(8,128)(2,1)S(1)}, bf16[2,8,64,128]{3,2,1,0:T(8,128)(2,1)S(1)}, u32[]{:S(2)}, u32[]{:S(2)}) %collective-permute-start.1) | collective-permute-done | bytes 262176 | tf_op jit(solution)/shard_map/ppermute | solution.py:513
  13.5 5.1 %collective-permute-done.2.refs_3_ = bf16[2,8,64,128]{3,2,1,0:T(8,128)(2,1)S(1)} collective-permute-done((bf16[2,8,64,128]{3,2,1,0:T(8,128)(2,1)S(1)}, bf16[2,8,64,128]{3,2,1,0:T(8,128)(2,1)S(1)}, u32[]{:S(2)}, u32[]{:S(2)}) %collective-permute-start.2) | collective-permute-done | bytes 262176 | tf_op jit(solution)/shard_map/ppermute | solution.py:513
  20.2 3.6 %channel_step.2 = bf16[8,4,2,4,16,128]{5,4,3,2,1,0:T(8,128)(2,1)} custom-call(s32[1]{0:T(128)} %bitcast.1.me_ref, bf16[2,8,64,128]{3,2,1,0:T(8,128)(2,1)S(1)} %get-tuple-element.43.refs_0_, bf16[2,8,64,128]{3,2,1,0:T(8,128)(2,1)S(1)} %collective-permute-done.refs_1_, bf16[2,8,64,128]{3,2,1,0:T(8,128)(2,1)S(1)} %collective-permute-done.1.refs_2_, ...), custom_call_target="tpu_custom_call" | custom-call | flops 536870912 | bytes 8388608 | tf_op jit(solution)/shard_map/channel_step/pallas_call | solution.py:221
  23.8 5.9 %all-to-all-start = ((bf16[32,2,4,16,128]{4,3,2,1,0:T(8,128)(2,1)}), bf16[32,2,4,16,128]{4,3,2,1,0:T(8,128)(2,1)}, u32[]{:S(2)}, u32[]{:S(2)}) async-start(bf16[32,2,4,16,128]{4,3,2,1,0:T(8,128)(2,1)} %bitcast.5), calls=%async_computation | async-start | bytes 2097152 | tf_op jit(solution)/shard_map/all_to_all | solution.py:540
  29.7 1.6 %spread.3 = (bf16[2,8,64,128]{3,2,1,0:T(8,128)(2,1)S(1)}, bf16[2,8,64,128]{3,2,1,0:T(8,128)(2,1)S(1)}, bf16[2,8,64,128]{3,2,1,0:T(8,128)(2,1)S(1)}, bf16[2,8,64,128]{3,2,1,0:T(8,128)(2,1)S(1)}) custom-call(s32[1]{0:T(128)} %bitcast.1.me_ref, bf16[2,8,8,64,128]{4,3,2,1,0:T(8,128)(2,1)S(1)} %bitcast.10), custom_call_target="tpu_custom_call" | custom-call | bytes 4194304 | tf_op jit(solution)/shard_map/spread/pallas_call | solution.py:125
  31.6 1.6 %collective-permute-start.4 = (bf16[2,8,64,128]{3,2,1,0:T(8,128)(2,1)S(1)}, bf16[2,8,64,128]{3,2,1,0:T(8,128)(2,1)S(1)}, u32[]{:S(2)}, u32[]{:S(2)}) collective-permute-start(bf16[2,8,64,128]{3,2,1,0:T(8,128)(2,1)S(1)} %get-tuple-element.52), channel_id=1, source_target_pairs={{0,2},{1,3},{2,0},{3,1},{4,6},{5,7},{6,4},{7,5},{8,10},{9,11},{10,... | collective-permute-start | bytes 786440 | tf_op jit(solution)/shard_map/ppermute | solution.py:513
  33.3 14.8 %collective-permute-done.4.refs_2_ = bf16[2,8,64,128]{3,2,1,0:T(8,128)(2,1)S(1)} collective-permute-done((bf16[2,8,64,128]{3,2,1,0:T(8,128)(2,1)S(1)}, bf16[2,8,64,128]{3,2,1,0:T(8,128)(2,1)S(1)}, u32[]{:S(2)}, u32[]{:S(2)}) %collective-permute-start.4) | collective-permute-done | bytes 262176 | tf_op jit(solution)/shard_map/ppermute | solution.py:513
  48.1 6.6 %collective-permute-done.5.refs_3_ = bf16[2,8,64,128]{3,2,1,0:T(8,128)(2,1)S(1)} collective-permute-done((bf16[2,8,64,128]{3,2,1,0:T(8,128)(2,1)S(1)}, bf16[2,8,64,128]{3,2,1,0:T(8,128)(2,1)S(1)}, u32[]{:S(2)}, u32[]{:S(2)}) %collective-permute-start.5) | collective-permute-done | bytes 262176 | tf_op jit(solution)/shard_map/ppermute | solution.py:513
  54.7 2.8 %channel_step.3 = (bf16[8,2,4,16,128]{4,3,2,1,0:T(8,128)(2,1)S(1)}, bf16[8,2,4,16,128]{4,3,2,1,0:T(8,128)(2,1)S(1)}, bf16[8,2,4,16,128]{4,3,2,1,0:T(8,128)(2,1)S(1)}, bf16[8,2,4,16,128]{4,3,2,1,0:T(8,128)(2,1)S(1)}) custom-call(s32[1]{0:T(128)} %bitcast.1.me_ref, bf16[2,8,64,128]{3,2,1,0:T(8,128)(2,1)S(1)} %get-tuple-element.50.refs_0_, ...), custom_call_target="tpu_custom_call" | custom-call | flops 536870912 | bytes 8388608 | tf_op jit(solution)/shard_map/channel_step/pallas_call | solution.py:221
  59.5 7.5 %collective-permute-done.7.refs_2_ = bf16[8,2,4,16,128]{4,3,2,1,0:T(8,128)(2,1)S(1)} collective-permute-done((bf16[8,2,4,16,128]{4,3,2,1,0:T(8,128)(2,1)S(1)}, bf16[8,2,4,16,128]{4,3,2,1,0:T(8,128)(2,1)S(1)}, u32[]{:S(2)}, u32[]{:S(2)}) %collective-permute-start.7) | collective-permute-done | bytes 262176 | tf_op jit(solution)/shard_map/ppermute | solution.py:513
  67.0 4.2 %collective-permute-done.8.refs_3_ = bf16[8,2,4,16,128]{4,3,2,1,0:T(8,128)(2,1)S(1)} collective-permute-done((bf16[8,2,4,16,128]{4,3,2,1,0:T(8,128)(2,1)S(1)}, bf16[8,2,4,16,128]{4,3,2,1,0:T(8,128)(2,1)S(1)}, u32[]{:S(2)}, u32[]{:S(2)}) %collective-permute-start.8) | collective-permute-done | bytes 262176 | tf_op jit(solution)/shard_map/ppermute | solution.py:513
  71.2 2.4 %middle_step.1 = (bf16[4,2,64,128]{3,2,1,0:T(8,128)(2,1)S(1)}, bf16[4,2,64,128]{3,2,1,0:T(8,128)(2,1)S(1)}, bf16[4,2,64,128]{3,2,1,0:T(8,128)(2,1)S(1)}, bf16[4,...) custom-call(s32[2]{0:T(128)S(1)} %pad_add_fusion.at_ref, ...), custom_call_target="tpu_custom_call" | custom-call | flops 268435456 | bytes 4194304 | tf_op jit(solution)/shard_map/middle_step/pallas_call | solution.py:353
  74.3 1.9 %collective-permute-start.10 = (bf16[4,2,64,128]{3,2,1,0:T(8,128)(2,1)S(1)}, bf16[4,2,64,128]{3,2,1,0:T(8,128)(2,1)S(1)}, u32[]{:S(2)}, u32[]{:S(2)}) collective-permute-start(bf16[4,2,64,128]{3,2,1,0:T(8,128)(2,1)S(1)} %get-tuple-element.60), channel_id=1, source_target_pairs={{0,8},{4,12},{8,0},{12,4},{16,24},{20,28},{24,16},{28,20},{1,9},{5... | collective-permute-start | bytes 393224 | tf_op jit(solution)/shard_map/ppermute | solution.py:513
  77.3 2.5 %collective-permute-start.12 = (bf16[4,2,64,128]{3,2,1,0:T(8,128)(2,1)}, bf16[4,2,64,128]{3,2,1,0:T(8,128)(2,1)}, u32[]{:S(2)}, u32[]{:S(2)}) collective-permute-start(bf16[4,2,64,128]{3,2,1,0:T(8,128)(2,1)} %get-tuple-element.62), channel_id=1, source_target_pairs={{0,16},{4,20},{8,24},{12,28},{16,0},{20,4},{24,8},{28,12},{1,17},{... | collective-permute-start | bytes 393224 | tf_op jit(solution)/shard_map/ppermute | solution.py:513
  81.7 3.6 %collective-permute-start.14 = (bf16[4,2,64,128]{3,2,1,0:T(8,128)(2,1)}, bf16[4,2,64,128]{3,2,1,0:T(8,128)(2,1)}, u32[]{:S(2)}, u32[]{:S(2)}) collective-permute-start(bf16[4,2,64,128]{3,2,1,0:T(8,128)(2,1)} %get-tuple-element.64), channel_id=1, source_target_pairs={{0,24},{4,28},{8,16},{12,20},{16,8},{20,12},{24,0},{28,4},{1,25},{... | collective-permute-start | bytes 393224 | tf_op jit(solution)/shard_map/ppermute | solution.py:513
  86.3 7.0 %beam_weights.3 = (f32[33,8,3,8,128]{4,3,2,1,0:T(8,128)S(1)}, s32[36]{0:T(128)S(1)}, s32[5]{0:T(128)S(1)}) custom-call(s32[2]{0:T(128)S(1)} %pad_add_fusion.at_ref, f32[128,64]{1,0:T(8,128)S(1)} %copy.7.table_ref, s32[32]{0:T(128)S(1)} %copy-done.14, s32[64]{0:T(128)S(1)} %copy-done.15), custom_call_target="tpu_custom_call" | custom-call | flops 536870912 | bytes 8388608 | tf_op jit(solution)/shard_map/beam_weights/pallas_call | solution.py:306
  93.3 1.7 %copy-done.2 = f32[33,8,3,8,128]{4,3,2,1,0:T(8,128)} copy-done((f32[33,8,3,8,128]{4,3,2,1,0:T(8,128)}, f32[33,8,3,8,128]{4,3,2,1,0:T(8,128)S(1)}, u32[]{:S(2)}) %copy-start.2) | copy-done | bytes 3244056
  96.4 7.1 %beam_weights.2 = (f32[33,8,3,8,128]{4,3,2,1,0:T(8,128)S(1)}, s32[36]{0:T(128)S(1)}, s32[5]{0:T(128)S(1)}) custom-call(s32[2]{0:T(128)S(1)} %pad_add_fusion.at_ref, f32[128,64]{1,0:T(8,128)S(1)} %copy-done.12, s32[32]{0:T(128)S(1)} %copy-done.14, s32[64]{0:T(128)S(1)} %copy-done.15), custom_call_target="tpu_custom_call" | custom-call | flops 536870912 | bytes 8388608 | tf_op jit(solution)/shard_map/beam_weights/pallas_call | solution.py:306
  103.5 1.9 %copy-done.3 = f32[33,8,3,8,128]{4,3,2,1,0:T(8,128)S(1)} copy-done((f32[33,8,3,8,128]{4,3,2,1,0:T(8,128)S(1)}, f32[33,8,3,8,128]{4,3,2,1,0:T(8,128)}, u32[]{:S(2)}) %copy-start.3) | copy-done | bytes 3244056
  105.4 6.2 %beams_early.1.sum_hbm = f32[8,4,2,2,4,8,128]{6,5,4,3,2,1,0:T(8,128)S(1)} custom-call(bf16[8,4,2,4,16,128]{5,4,3,2,1,0:T(8,128)(2,1)} %bitcast.6.blocks_ref, bf16[2,4,32,256]{3,2,1,0:T(8,128)(2,1)S(1)} %copy-done.4, f32[33,8,3,8,128]{4,3,2,1,0:T(8,128)S(1)} %copy-done.3, s32[36]{0:T(128)S(1)} %get-tuple-element.48.order_ref, s32[5]{0:T(128)S(1)} %get-tuple-element.49.start_ref), custom_call_target="tpu_custom_call" | custom-call | flops 536870912 | bytes 8388608 | tf_op jit(solution)/shard_map/beams_early/pallas_call | solution.py:448
  111.8 3.3 %beams_late.2 = (f32[33,2,8,8,128]{4,3,2,1,0:T(8,128)S(1)}, bf16[4,2,2,4,8,128]{5,4,3,2,1,0:T(8,128)(2,1)S(1)}, bf16[4,2,2,4,8,128]{5,4,3,2,1,0:T(8,128)(2,1)S(1...) custom-call(f32[33,8,3,8,128]{4,3,2,1,0:T(8,128)S(1)} %get-tuple-element.40.weight_ref, ...), custom_call_target="tpu_custom_call" | custom-call | flops 536870912 | bytes 8388608 | tf_op jit(solution)/shard_map/beams_late/pallas_call | solution.py:472
  115.1 2.5 %beams_late.3 = (bf16[4,2,2,4,8,128]{5,4,3,2,1,0:T(8,128)(2,1)S(1)}, bf16[4,2,2,4,8,128]{5,4,3,2,1,0:T(8,128)(2,1)S(1)}, bf16[4,2,2,4,8,128]{5,4,3,2,1,0:T(8,128)(2,1)S(1)}, bf16[4,2,2,4,8,128]{5,4,3,2,1,0:T(8,128)(2,1)S(1)}) custom-call(f32[33,8,3,8,128]{4,3,2,1,0:T(8,128)S(1)} %get-tuple-element.40.weight_ref, s32[36]{0:T(128)S(1)} %get-tuple-element.41.order_ref, ...), custom_call_target="tpu_custom_call" | custom-call | flops 536870912 | bytes 8388608 | tf_op jit(solution)/shard_map/beams_late/pallas_call | solution.py:472
  117.6 3.7 %collective-permute-start.16 = (bf16[4,2,2,4,8,128]{5,4,3,2,1,0:T(8,128)(2,1)S(1)}, bf16[4,2,2,4,8,128]{5,4,3,2,1,0:T(8,128)(2,1)S(1)}, u32[]{:S(2)}, u32[]{:S(2)}) collective-permute-start(bf16[4,2,2,4,8,128]{5,4,3,2,1,0:T(8,128)(2,1)S(1)} %get-tuple-element.68), channel_id=1, source_target_pairs={{0,4},{4,0},{8,12},{12,8},{16,20},{20,16},{24,28},{28,24},{1,5},{5... | collective-permute-start | bytes 393224 | tf_op jit(solution)/shard_map/ppermute | solution.py:513
  121.3 1.5 %collective-permute-start.18 = (bf16[4,2,2,4,8,128]{5,4,3,2,1,0:T(8,128)(2,1)S(1)}, bf16[4,2,2,4,8,128]{5,4,3,2,1,0:T(8,128)(2,1)S(1)}, u32[]{:S(2)}, u32[]{:S(2)}) collective-permute-start(bf16[4,2,2,4,8,128]{5,4,3,2,1,0:T(8,128)(2,1)S(1)} %get-tuple-element.70), channel_id=1, source_target_pairs={{0,12},{4,8},{8,4},{12,0},{16,28},{20,24},{24,20},{28,16},{1,13},{... | collective-permute-start | bytes 393224 | tf_op jit(solution)/shard_map/ppermute | solution.py:513
  123.2 3.9 %collective-permute-start.20 = (bf16[4,2,2,4,8,128]{5,4,3,2,1,0:T(8,128)(2,1)S(1)}, bf16[4,2,2,4,8,128]{5,4,3,2,1,0:T(8,128)(2,1)S(1)}, u32[]{:S(2)}, u32[]{:S(2)}) collective-permute-start(bf16[4,2,2,4,8,128]{5,4,3,2,1,0:T(8,128)(2,1)S(1)} %get-tuple-element.72), channel_id=1, source_target_pairs={{0,20},{4,16},{8,28},{12,24},{16,4},{20,0},{24,12},{28,8},{1,21},{... | collective-permute-start | bytes 393224 | tf_op jit(solution)/shard_map/ppermute | solution.py:513
  128.5 2.0 %collective-permute-start.22 = (bf16[4,2,2,4,8,128]{5,4,3,2,1,0:T(8,128)(2,1)S(1)}, bf16[4,2,2,4,8,128]{5,4,3,2,1,0:T(8,128)(2,1)S(1)}, u32[]{:S(2)}, u32[]{:S(2)}) collective-permute-start(bf16[4,2,2,4,8,128]{5,4,3,2,1,0:T(8,128)(2,1)S(1)} %get-tuple-element.74), channel_id=1, source_target_pairs={{0,28},{4,24},{8,20},{12,16},{16,12},{20,8},{24,4},{28,0},{1,29},{... | collective-permute-start | bytes 393224 | tf_op jit(solution)/shard_map/ppermute | solution.py:513
  130.5 9.6 %collective-permute-done.19.refs_4_ = bf16[4,2,2,4,8,128]{5,4,3,2,1,0:T(8,128)(2,1)S(1)} collective-permute-done((bf16[4,2,2,4,8,128]{5,4,3,2,1,0:T(8,128)(2,1)S(1)}, bf16[4,2,2,4,8,128]{5,4,3,2,1,0:T(8,128)(2,1)S(1)}, u32[]{:S(2)}, u32[]{:S(2)}) %collective-permute-start.19) | collective-permute-done | bytes 131104 | tf_op jit(solution)/shard_map/ppermute | solution.py:513
  140.1 3.4 %collective-permute-done.20.refs_5_ = bf16[4,2,2,4,8,128]{5,4,3,2,1,0:T(8,128)(2,1)S(1)} collective-permute-done((bf16[4,2,2,4,8,128]{5,4,3,2,1,0:T(8,128)(2,1)S(1)}, bf16[4,2,2,4,8,128]{5,4,3,2,1,0:T(8,128)(2,1)S(1)}, u32[]{:S(2)}, u32[]{:S(2)}) %collective-permute-start.20) | collective-permute-done | bytes 131104 | tf_op jit(solution)/shard_map/ppermute | solution.py:513
  (73 shorter events, 13.6 us)
Async XLA Ops:
  1.6 17.7 %copy-start.13 = (bf16[2,4,16,128]{3,2,1,0:T(8,128)(2,1)S(1)}, bf16[2,4,16,128]{3,2,1,0:T(8,128)(2,1)}, u32[]{:S(2)}) copy-start(bf16[2,4,16,128]{3,2,1,0:T(8,128)(2,1)} %constant.119.clone.refs_5_) | copy-start | bytes 98308
  3.2 5.9 %collective-permute-start = (bf16[2,8,64,128]{3,2,1,0:T(8,128)(2,1)S(1)}, bf16[2,8,64,128]{3,2,1,0:T(8,128)(2,1)S(1)}, u32[]{:S(2)}, u32[]{:S(2)}) collective-permute-start(bf16[2,8,64,128]{3,2,1,0:T(8,128)(2,1)S(1)} %get-tuple-element.44), channel_id=1, source_target_pairs={{0,1},{1,0},{2,3},{3,2},{4,5},{5,4},{6,7},{7,6},{8,9},{9,8},{10,11... | collective-permute-start | bytes 786440 | tf_op jit(solution)/shard_map/ppermute | solution.py:513
  3.7 9.7 %collective-permute-start.1 = (bf16[2,8,64,128]{3,2,1,0:T(8,128)(2,1)S(1)}, bf16[2,8,64,128]{3,2,1,0:T(8,128)(2,1)S(1)}, u32[]{:S(2)}, u32[]{:S(2)}) collective-permute-start(bf16[2,8,64,128]{3,2,1,0:T(8,128)(2,1)S(1)} %get-tuple-element.45), channel_id=1, source_target_pairs={{0,2},{1,3},{2,0},{3,1},{4,6},{5,7},{6,4},{7,5},{8,10},{9,11},{10,... | collective-permute-start | bytes 786440 | tf_op jit(solution)/shard_map/ppermute | solution.py:513
  6.3 12.3 %collective-permute-start.2 = (bf16[2,8,64,128]{3,2,1,0:T(8,128)(2,1)S(1)}, bf16[2,8,64,128]{3,2,1,0:T(8,128)(2,1)S(1)}, u32[]{:S(2)}, u32[]{:S(2)}) collective-permute-start(bf16[2,8,64,128]{3,2,1,0:T(8,128)(2,1)S(1)} %get-tuple-element.46), channel_id=1, source_target_pairs={{0,3},{1,2},{2,1},{3,0},{4,7},{5,6},{6,5},{7,4},{8,11},{9,10},{10,... | collective-permute-start | bytes 786440 | tf_op jit(solution)/shard_map/ppermute | solution.py:513
  20.2 9.5 %copy-start.1 = (bf16[2,8,2,32768]{3,2,1,0:T(2,128)(2,1)S(1)}, bf16[2,8,2,32768]{3,2,1,0:T(2,128)(2,1)}, u32[]{:S(2)}) copy-start(bf16[2,8,2,32768]{3,2,1,0:T(2,128)(2,1)} %param.6) | copy-start | bytes 6291460
  23.8 79.7 %all-to-all-start = ((bf16[32,2,4,16,128]{4,3,2,1,0:T(8,128)(2,1)}), bf16[32,2,4,16,128]{4,3,2,1,0:T(8,128)(2,1)}, u32[]{:S(2)}, u32[]{:S(2)}) async-start(bf16[32,2,4,16,128]{4,3,2,1,0:T(8,128)(2,1)} %bitcast.5), calls=%async_computation | async-start | bytes 2097152 | tf_op jit(solution)/shard_map/all_to_all | solution.py:540
  29.7 41.5 %copy-start.4 = (bf16[2,4,32,256]{3,2,1,0:T(8,128)(2,1)S(1)}, bf16[2,4,32,256]{3,2,1,0:T(8,128)(2,1)}, u32[]{:S(2)}) copy-start(bf16[2,4,32,256]{3,2,1,0:T(8,128)(2,1)} %constant.120.clone.table_ref.refs_4_) | copy-start | bytes 393220
  29.7 46.6 %copy-start.16 = (f32[128,64]{0,1:T(8,128)S(1)}, f32[128,64]{0,1:T(8,128)}, u32[]{:S(2)}) copy-start(f32[128,64]{0,1:T(8,128)} %param.7) | copy-start | bytes 98308
  31.3 54.9 %copy-start.14 = (s32[32]{0:T(128)S(1)}, s32[32]{0:T(128)}, u32[]{:S(2)}) copy-start(s32[32]{0:T(128)} %beam_ref.3) | copy-start | bytes 388
  31.4 54.9 %copy-start.15 = (s32[64]{0:T(128)S(1)}, s32[64]{0:T(128)}, u32[]{:S(2)}) copy-start(s32[64]{0:T(128)} %group_ref.3) | copy-start | bytes 772
  31.4 1.9 %collective-permute-start.3 = (bf16[2,8,64,128]{3,2,1,0:T(8,128)(2,1)S(1)}, bf16[2,8,64,128]{3,2,1,0:T(8,128)(2,1)S(1)}, u32[]{:S(2)}, u32[]{:S(2)}) collective-permute-start(bf16[2,8,64,128]{3,2,1,0:T(8,128)(2,1)S(1)} %get-tuple-element.51), channel_id=1, source_target_pairs={{0,1},{1,0},{2,3},{3,2},{4,5},{5,4},{6,7},{7,6},{8,9},{9,8},{10,11... | collective-permute-start | bytes 786440 | tf_op jit(solution)/shard_map/ppermute | solution.py:513
  31.6 16.4 %collective-permute-start.4 = (bf16[2,8,64,128]{3,2,1,0:T(8,128)(2,1)S(1)}, bf16[2,8,64,128]{3,2,1,0:T(8,128)(2,1)S(1)}, u32[]{:S(2)}, u32[]{:S(2)}) collective-permute-start(bf16[2,8,64,128]{3,2,1,0:T(8,128)(2,1)S(1)} %get-tuple-element.52), channel_id=1, source_target_pairs={{0,2},{1,3},{2,0},{3,1},{4,6},{5,7},{6,4},{7,5},{8,10},{9,11},{10,... | collective-permute-start | bytes 786440 | tf_op jit(solution)/shard_map/ppermute | solution.py:513
  33.2 21.4 %collective-permute-start.5 = (bf16[2,8,64,128]{3,2,1,0:T(8,128)(2,1)S(1)}, bf16[2,8,64,128]{3,2,1,0:T(8,128)(2,1)S(1)}, u32[]{:S(2)}, u32[]{:S(2)}) collective-permute-start(bf16[2,8,64,128]{3,2,1,0:T(8,128)(2,1)S(1)} %get-tuple-element.53), channel_id=1, source_target_pairs={{0,3},{1,2},{2,1},{3,0},{4,7},{5,6},{6,5},{7,4},{8,11},{9,10},{10,... | collective-permute-start | bytes 786440 | tf_op jit(solution)/shard_map/ppermute | solution.py:513
  57.5 2.0 %collective-permute-start.6 = (bf16[8,2,4,16,128]{4,3,2,1,0:T(8,128)(2,1)S(1)}, bf16[8,2,4,16,128]{4,3,2,1,0:T(8,128)(2,1)S(1)}, u32[]{:S(2)}, u32[]{:S(2)}) collective-permute-start(bf16[8,2,4,16,128]{4,3,2,1,0:T(8,128)(2,1)S(1)} %get-tuple-element.55), channel_id=1, source_target_pairs={{0,1},{1,0},{2,3},{3,2},{4,5},{5,4},{6,7},{7,6},{8,9},{9,8},{10,11... | collective-permute-start | bytes 786440 | tf_op jit(solution)/shard_map/ppermute | solution.py:513
  57.8 9.2 %collective-permute-start.7 = (bf16[8,2,4,16,128]{4,3,2,1,0:T(8,128)(2,1)S(1)}, bf16[8,2,4,16,128]{4,3,2,1,0:T(8,128)(2,1)S(1)}, u32[]{:S(2)}, u32[]{:S(2)}) collective-permute-start(bf16[8,2,4,16,128]{4,3,2,1,0:T(8,128)(2,1)S(1)} %get-tuple-element.56), channel_id=1, source_target_pairs={{0,2},{1,3},{2,0},{3,1},{4,6},{5,7},{6,4},{7,5},{8,10},{9,11},{10,... | collective-permute-start | bytes 786440 | tf_op jit(solution)/shard_map/ppermute | solution.py:513
  59.3 12.0 %collective-permute-start.8 = (bf16[8,2,4,16,128]{4,3,2,1,0:T(8,128)(2,1)S(1)}, bf16[8,2,4,16,128]{4,3,2,1,0:T(8,128)(2,1)S(1)}, u32[]{:S(2)}, u32[]{:S(2)}) collective-permute-start(bf16[8,2,4,16,128]{4,3,2,1,0:T(8,128)(2,1)S(1)} %get-tuple-element.57), channel_id=1, source_target_pairs={{0,3},{1,2},{2,1},{3,0},{4,7},{5,6},{6,5},{7,4},{8,11},{9,10},{10,... | collective-permute-start | bytes 786440 | tf_op jit(solution)/shard_map/ppermute | solution.py:513
  73.7 7.4 %collective-permute-start.9 = (bf16[4,2,64,128]{3,2,1,0:T(8,128)(2,1)S(1)}, bf16[4,2,64,128]{3,2,1,0:T(8,128)(2,1)S(1)}, u32[]{:S(2)}, u32[]{:S(2)}) collective-permute-start(bf16[4,2,64,128]{3,2,1,0:T(8,128)(2,1)S(1)} %get-tuple-element.59), channel_id=1, source_target_pairs={{0,4},{4,0},{8,12},{12,8},{16,20},{20,16},{24,28},{28,24},{1,5},{5... | collective-permute-start | bytes 393224 | tf_op jit(solution)/shard_map/ppermute | solution.py:513
  74.3 11.0 %collective-permute-start.10 = (bf16[4,2,64,128]{3,2,1,0:T(8,128)(2,1)S(1)}, bf16[4,2,64,128]{3,2,1,0:T(8,128)(2,1)S(1)}, u32[]{:S(2)}, u32[]{:S(2)}) collective-permute-start(bf16[4,2,64,128]{3,2,1,0:T(8,128)(2,1)S(1)} %get-tuple-element.60), channel_id=1, source_target_pairs={{0,8},{4,12},{8,0},{12,4},{16,24},{20,28},{24,16},{28,20},{1,9},{5... | collective-permute-start | bytes 393224 | tf_op jit(solution)/shard_map/ppermute | solution.py:513
  76.4 35.3 %collective-permute-start.11 = (bf16[4,2,64,128]{3,2,1,0:T(8,128)(2,1)}, bf16[4,2,64,128]{3,2,1,0:T(8,128)(2,1)}, u32[]{:S(2)}, u32[]{:S(2)}) collective-permute-start(bf16[4,2,64,128]{3,2,1,0:T(8,128)(2,1)} %get-tuple-element.61), channel_id=1, source_target_pairs={{0,12},{4,8},{8,4},{12,0},{16,28},{20,24},{24,20},{28,16},{1,13},{... | collective-permute-start | bytes 393224 | tf_op jit(solution)/shard_map/ppermute | solution.py:513
  77.3 34.4 %collective-permute-start.12 = (bf16[4,2,64,128]{3,2,1,0:T(8,128)(2,1)}, bf16[4,2,64,128]{3,2,1,0:T(8,128)(2,1)}, u32[]{:S(2)}, u32[]{:S(2)}) collective-permute-start(bf16[4,2,64,128]{3,2,1,0:T(8,128)(2,1)} %get-tuple-element.62), channel_id=1, source_target_pairs={{0,16},{4,20},{8,24},{12,28},{16,0},{20,4},{24,8},{28,12},{1,17},{... | collective-permute-start | bytes 393224 | tf_op jit(solution)/shard_map/ppermute | solution.py:513
  79.8 31.9 %collective-permute-start.13 = (bf16[4,2,64,128]{3,2,1,0:T(8,128)(2,1)}, bf16[4,2,64,128]{3,2,1,0:T(8,128)(2,1)}, u32[]{:S(2)}, u32[]{:S(2)}) collective-permute-start(bf16[4,2,64,128]{3,2,1,0:T(8,128)(2,1)} %get-tuple-element.63), channel_id=1, source_target_pairs={{0,20},{4,16},{8,28},{12,24},{16,4},{20,0},{24,12},{28,8},{1,21},{... | collective-permute-start | bytes 393224 | tf_op jit(solution)/shard_map/ppermute | solution.py:513
  81.7 30.0 %collective-permute-start.14 = (bf16[4,2,64,128]{3,2,1,0:T(8,128)(2,1)}, bf16[4,2,64,128]{3,2,1,0:T(8,128)(2,1)}, u32[]{:S(2)}, u32[]{:S(2)}) collective-permute-start(bf16[4,2,64,128]{3,2,1,0:T(8,128)(2,1)} %get-tuple-element.64), channel_id=1, source_target_pairs={{0,24},{4,28},{8,16},{12,20},{16,8},{20,12},{24,0},{28,4},{1,25},{... | collective-permute-start | bytes 393224 | tf_op jit(solution)/shard_map/ppermute | solution.py:513
  86.0 25.8 %collective-permute-start.15 = (bf16[4,2,64,128]{3,2,1,0:T(8,128)(2,1)}, bf16[4,2,64,128]{3,2,1,0:T(8,128)(2,1)}, u32[]{:S(2)}, u32[]{:S(2)}) collective-permute-start(bf16[4,2,64,128]{3,2,1,0:T(8,128)(2,1)} %get-tuple-element.65), channel_id=1, source_target_pairs={{0,28},{4,24},{8,20},{12,16},{16,12},{20,8},{24,4},{28,0},{1,29},{... | collective-permute-start | bytes 393224 | tf_op jit(solution)/shard_map/ppermute | solution.py:513
  105.4 6.3 %copy-start.8 = (bf16[4,2,64,128]{3,2,1,0:T(8,128)(2,1)S(1)}, bf16[4,2,64,128]{3,2,1,0:T(8,128)(2,1)}, u32[]{:S(2)}) copy-start(bf16[4,2,64,128]{3,2,1,0:T(8,128)(2,1)} %copy-done.7) | copy-start | bytes 393220
  105.4 6.3 %copy-start.10 = (bf16[4,2,64,128]{3,2,1,0:T(8,128)(2,1)S(1)}, bf16[4,2,64,128]{3,2,1,0:T(8,128)(2,1)}, u32[]{:S(2)}) copy-start(bf16[4,2,64,128]{3,2,1,0:T(8,128)(2,1)} %copy-done.9) | copy-start | bytes 393220
  117.6 9.6 %collective-permute-start.16 = (bf16[4,2,2,4,8,128]{5,4,3,2,1,0:T(8,128)(2,1)S(1)}, bf16[4,2,2,4,8,128]{5,4,3,2,1,0:T(8,128)(2,1)S(1)}, u32[]{:S(2)}, u32[]{:S(2)}) collective-permute-start(bf16[4,2,2,4,8,128]{5,4,3,2,1,0:T(8,128)(2,1)S(1)} %get-tuple-element.68), channel_id=1, source_target_pairs={{0,4},{4,0},{8,12},{12,8},{16,20},{20,16},{24,28},{28,24},{1,5},{5... | collective-permute-start | bytes 393224 | tf_op jit(solution)/shard_map/ppermute | solution.py:513
  121.3 7.2 %collective-permute-start.17 = (bf16[4,2,2,4,8,128]{5,4,3,2,1,0:T(8,128)(2,1)S(1)}, bf16[4,2,2,4,8,128]{5,4,3,2,1,0:T(8,128)(2,1)S(1)}, u32[]{:S(2)}, u32[]{:S(2)}) collective-permute-start(bf16[4,2,2,4,8,128]{5,4,3,2,1,0:T(8,128)(2,1)S(1)} %get-tuple-element.69), channel_id=1, source_target_pairs={{0,8},{4,12},{8,0},{12,4},{16,24},{20,28},{24,16},{28,20},{1,9},{5... | collective-permute-start | bytes 393224 | tf_op jit(solution)/shard_map/ppermute | solution.py:513
  121.3 9.2 %collective-permute-start.18 = (bf16[4,2,2,4,8,128]{5,4,3,2,1,0:T(8,128)(2,1)S(1)}, bf16[4,2,2,4,8,128]{5,4,3,2,1,0:T(8,128)(2,1)S(1)}, u32[]{:S(2)}, u32[]{:S(2)}) collective-permute-start(bf16[4,2,2,4,8,128]{5,4,3,2,1,0:T(8,128)(2,1)S(1)} %get-tuple-element.70), channel_id=1, source_target_pairs={{0,12},{4,8},{8,4},{12,0},{16,28},{20,24},{24,20},{28,16},{1,13},{... | collective-permute-start | bytes 393224 | tf_op jit(solution)/shard_map/ppermute | solution.py:513
  122.9 17.2 %collective-permute-start.19 = (bf16[4,2,2,4,8,128]{5,4,3,2,1,0:T(8,128)(2,1)S(1)}, bf16[4,2,2,4,8,128]{5,4,3,2,1,0:T(8,128)(2,1)S(1)}, u32[]{:S(2)}, u32[]{:S(2)}) collective-permute-start(bf16[4,2,2,4,8,128]{5,4,3,2,1,0:T(8,128)(2,1)S(1)} %get-tuple-element.71), channel_id=1, source_target_pairs={{0,16},{4,20},{8,24},{12,28},{16,0},{20,4},{24,8},{28,12},{1,17},{... | collective-permute-start | bytes 393224 | tf_op jit(solution)/shard_map/ppermute | solution.py:513
  123.2 20.2 %collective-permute-start.20 = (bf16[4,2,2,4,8,128]{5,4,3,2,1,0:T(8,128)(2,1)S(1)}, bf16[4,2,2,4,8,128]{5,4,3,2,1,0:T(8,128)(2,1)S(1)}, u32[]{:S(2)}, u32[]{:S(2)}) collective-permute-start(bf16[4,2,2,4,8,128]{5,4,3,2,1,0:T(8,128)(2,1)S(1)} %get-tuple-element.72), channel_id=1, source_target_pairs={{0,20},{4,16},{8,28},{12,24},{16,4},{20,0},{24,12},{28,8},{1,21},{... | collective-permute-start | bytes 393224 | tf_op jit(solution)/shard_map/ppermute | solution.py:513
  127.2 16.3 %collective-permute-start.21 = (bf16[4,2,2,4,8,128]{5,4,3,2,1,0:T(8,128)(2,1)S(1)}, bf16[4,2,2,4,8,128]{5,4,3,2,1,0:T(8,128)(2,1)S(1)}, u32[]{:S(2)}, u32[]{:S(2)}) collective-permute-start(bf16[4,2,2,4,8,128]{5,4,3,2,1,0:T(8,128)(2,1)S(1)} %get-tuple-element.73), channel_id=1, source_target_pairs={{0,24},{4,28},{8,16},{12,20},{16,8},{20,12},{24,0},{28,4},{1,25},{... | collective-permute-start | bytes 393224 | tf_op jit(solution)/shard_map/ppermute | solution.py:513
  128.5 15.0 %collective-permute-start.22 = (bf16[4,2,2,4,8,128]{5,4,3,2,1,0:T(8,128)(2,1)S(1)}, bf16[4,2,2,4,8,128]{5,4,3,2,1,0:T(8,128)(2,1)S(1)}, u32[]{:S(2)}, u32[]{:S(2)}) collective-permute-start(bf16[4,2,2,4,8,128]{5,4,3,2,1,0:T(8,128)(2,1)S(1)} %get-tuple-element.74), channel_id=1, source_target_pairs={{0,28},{4,24},{8,20},{12,16},{16,12},{20,8},{24,4},{28,0},{1,29},{... | collective-permute-start | bytes 393224 | tf_op jit(solution)/shard_map/ppermute | solution.py:513
  (9 other events, 9.6 us)

commit v4 on v3

--- a/solution.py
+++ b/solution.py
@@ -22,6 +22,15 @@
 LANES = 128
 TF = 4
 STN = 8
+HALF = STN // 2
+UNROLL = 8
+ROUNDS = ((2, 3, 4, 5), (0, 1, 6, 7))
+
+
+def offset_in(chosen, place):
+    return place + 4 * (place // 2) if chosen else place + 2
+
+
 PART = CH_HI // TF
 LOW = CH_LO // TF
 PER = 4
@@ -104,20 +113,34 @@
     return out
 
 
-def spread_kernel(chunk, me_ref, volt_ref, *outs):
+def spread_kernel(chunk, me_ref, volt_ref, *refs):
+    outs, (in_ref, sem) = refs[:TF], refs[TF:]
     planes, _, frames = volt_ref.shape[:3]
-    for me in range(TF):
-
-        @pl.when(me_ref[0] == me)
-        def _(me=me):
-            def one(step, carry):
-                q, f = step // frames, step % frames
-                parts = [volt_ref[q, chunk * PER + a, f] for a in range(PER)]
-                for j, block in enumerate(swap_lane_blocks(parts)):
-                    outs[j ^ me][q, f] = block
-                return carry
-
-            lax.fori_loop(0, planes * frames, one, 0, unroll=2)
+    half = frames // 2
+    steps = [(q, part) for q in range(planes) for part in range(2)]
+    reads = [
+        pltpu.make_async_copy(
+            volt_ref.at[q, pl.ds(chunk * PER, PER), pl.ds(part * half, half)],
+            in_ref.at[q, :, pl.ds(part * half, half)],
+            sem.at[q, part],
+        )
+        for q, part in steps
+    ]
+    for read in reads:
+        read.start()
+    for (q, part), read in zip(steps, reads):
+        read.wait()
+        for me in range(TF):
+
+            @pl.when(me_ref[0] == me)
+            def _(me=me, q=q, part=part):
+                def one(f, carry):
+                    parts = [in_ref[q, a, f] for a in range(PER)]
+                    for j, block in enumerate(swap_lane_blocks(parts)):
+                        outs[j ^ me][q, f] = block
+                    return carry
+
+                lax.fori_loop(part * half, (part + 1) * half, one, 0, unroll=2)
 
 
 def spread(me, volt, chunk):
@@ -125,19 +148,23 @@
     return pl.pallas_call(
         functools.partial(spread_kernel, chunk),
         name="spread",
-        in_specs=[SMEM, VMEM],
+        in_specs=[SMEM, HBM],
         out_specs=[VMEM] * TF,
         out_shape=[jax.ShapeDtypeStruct((planes, frames, rows, LANES), BF)] * TF,
-        compiler_params=params(2),
+        scratch_shapes=[
+            pltpu.VMEM((planes, PER, frames, rows, LANES), BF),
+            pltpu.SemaphoreType.DMA((planes, 2)),
+        ],
+        compiler_params=params(4),
         cost_estimate=cost(4),
-    )(me, volt)
-
-
-def channel_kernel(split, me_ref, *refs):
+    )(me, pltpu.with_memory_space_constraint(volt, pltpu.HBM))
+
+
+def channel_kernel(split, at_ref, *refs):
     sources = refs[:TF]
     win_ref, table_ref, cos_ref, sin_ref = refs[TF : TF + 4]
     stage_ref, filt_ref = refs[-2:] if split else refs[-4:-2]
-    me = me_ref[0]
+    me, owner = at_ref[0], at_ref[1]
     rows = 2 * CH_LO
     history = TAPS - 1
     planes, per_source = sources[0].shape[:2]
@@ -166,14 +193,15 @@
     table = jnp.concatenate([table_ref[o, t] for o in range(planes) for t in ranges], axis=0)
     per_dest = frames // STN
     if split:
-        outs = refs[TF + 4 : TF + 4 + TF]
+        outs = refs[TF + 4 : TF + 4 + 2 * TF]
     else:
         out_ref, done_ref, sem = refs[TF + 4], refs[-2], refs[-1]
 
         def send(dest):
             return pltpu.make_async_copy(done_ref.at[dest], out_ref.at[dest], sem.at[dest])
 
-    def one_dest(dest, carry):
+    def one_dest(chosen, step, carry):
+        dest = owner ^ offset_in(chosen, step) if split else step
         cosine = jnp.concatenate([cos_ref[t] for t in ranges], axis=0)
         sine = jnp.concatenate([sin_ref[t] for t in ranges], axis=0)
         for pair in range(per_dest // 2):
@@ -190,20 +218,23 @@
                     value = turned[o].astype(BF).reshape(TF, 2 * LOW, LANES)
                     if split:
                         for d in range(TF):
-                            outs[d][dest, o, 2 * pair + side] = value[d]
+                            outs[chosen * TF + d][step, o, 2 * pair + side] = value[d]
                     else:
                         done_ref[dest, :, o, 2 * pair + side] = value
         if not split:
             send(dest).start()
         return carry
 
-    lax.fori_loop(0, STN, one_dest, 0, unroll=2)
-    if not split:
+    if split:
+        for chosen in range(2):
+            lax.fori_loop(0, HALF, functools.partial(one_dest, chosen), 0, unroll=2)
+    else:
+        lax.fori_loop(0, STN, functools.partial(one_dest, 0), 0, unroll=2)
         for dest in range(STN):
             send(dest).wait()
 
 
-def channel_step(me, blocks, window, table, cosine, sine, split):
+def channel_step(at, blocks, window, table, cosine, sine, split):
     planes, per_source, rows, _ = blocks[0].shape
     frames = TF * per_source
     tail = (planes, frames // STN, 2 * LOW, LANES)
@@ -212,8 +243,8 @@
         pltpu.VMEM((frames, planes, rows, LANES), BF),
     ]
     if split:
-        out_shape = [jax.ShapeDtypeStruct((STN,) + tail, BF)] * TF
-        out_specs = [VMEM] * TF
+        out_shape = [jax.ShapeDtypeStruct((HALF,) + tail, BF)] * (2 * TF)
+        out_specs = [VMEM] * (2 * TF)
     else:
         out = (STN, TF) + tail
         out_shape, out_specs = jax.ShapeDtypeStruct(out, BF), HBM
@@ -227,92 +258,98 @@
         scratch_shapes=scratch,
         compiler_params=params(12),
         cost_estimate=cost(8, 1 << 29),
-    )(me, *blocks, window, table, cosine, sine)
-
-
-def weight_kernel(chunk, at_ref, table_ref, beam_ref, group_ref, out_ref, order_ref, start_ref):
+    )(at, *blocks, window, table, cosine, sine)
+
+
+def turned_by(turns):
+    quarter = jnp.round(4.0 * turns)
+    angle = TWO_PI * (turns - 0.25 * quarter)
+    square = angle * angle
+    sine = angle * (
+        1.0 + square * (-1.0 / 6 + square * (1.0 / 120 + square * (-1.0 / 5040 + square * (1.0 / 362880))))
+    )
+    cosine = 1.0 + square * (
+        -0.5 + square * (1.0 / 24 + square * (-1.0 / 720 + square * (1.0 / 40320)))
+    )
+    turn = quarter.astype(jnp.int32) & 3
+    odd = (turn & 1) == 1
+    base_cos = jnp.where(odd, sine, cosine)
+    base_sin = jnp.where(odd, cosine, sine)
+    real = jnp.where((turn == 1) | (turn == 2), -base_cos, base_cos)
+    return real, jnp.where(turn >= 2, -base_sin, base_sin)
+
+
+def weight_kernel(chunk, offset_of, at_ref, table_ref, beam_ref, group_ref, out_ref, order_ref, count_ref, row_ref):
     total = group_ref.shape[0]
     members = out_ref.shape[0] - 1
     offsets = out_ref.shape[1]
     scale = math.sqrt(GROUPS / total)
     shape = (LOW, LANES)
-    k2 = at_ref[0] * LOW + lax.broadcasted_iota(jnp.int32, shape, 0)
-    channel = k2 + CH_LO * lax.broadcasted_iota(jnp.int32, shape, 1)
-    fraction = channel.astype(F32) / float(POINTS)
-
-    def station(member):
-        source = member // PER
-        if chunk:
-            source = source ^ at_ref[1]
-        return source * (PER * CHUNKS) + chunk * PER + member % PER
-
-    def one_member(member, carry):
-        s = station(member)
+    sublane = lax.broadcasted_iota(jnp.int32, shape, 0)
+    lane = lax.broadcasted_iota(jnp.int32, shape, 1)
+    high = (at_ref[0] * LOW + CH_LO * lane).astype(F32) / float(POINTS)
+    low = sublane.astype(F32) / float(POINTS)
+    for g in range(GROUPS):
+        count_ref[g] = 0
+
+    def some_members(step, carry):
+        for slot in range(UNROLL):
+            one_member(step * UNROLL + slot, slot)
+        return carry
+
+    def one_member(member, slot):
+        source = offset_of(member // PER, at_ref[1])
+        s = source * (PER * CHUNKS) + chunk * PER + member % PER
         group = group_ref[s]
+        at = count_ref[group]
+        order_ref[group, at] = member
+        order_ref[group, at + 1] = members
+        count_ref[group] = at + 1
+
+        down = jnp.zeros(shape, F32)
+        across = jnp.zeros(shape, F32)
         for d in range(offsets):
             beam = group + GROUPS * (at_ref[1] ^ d)
-            turns = table_ref[beam_ref[beam], s] * fraction
-            quarter = jnp.round(4.0 * turns)
-            angle = TWO_PI * (turns - 0.25 * quarter)
-            square = angle * angle
-            sine = angle * (
-                1.0 + square * (-1.0 / 6 + square * (1.0 / 120 + square * (-1.0 / 5040 + square * (1.0 / 362880))))
-            )
-            cosine = 1.0 + square * (
-                -0.5 + square * (1.0 / 24 + square * (-1.0 / 720 + square * (1.0 / 40320)))
-            )
-            turn = quarter.astype(jnp.int32) & 3
-            odd = (turn & 1) == 1
-            base_cos = jnp.where(odd, sine, cosine)
-            base_sin = jnp.where(odd, cosine, sine)
-            real = scale * jnp.where((turn == 1) | (turn == 2), -base_cos, base_cos)
-            imag = -scale * jnp.where(turn >= 2, -base_sin, base_sin)
-            real = real.astype(BF).astype(F32)
-            imag = imag.astype(BF).astype(F32)
-            out_ref[member, d, 0] = real
-            out_ref[member, d, 1] = imag - real
-            out_ref[member, d, 2] = imag + real
-        return carry
-
-    lax.fori_loop(0, members, one_member, 0)
-    out_ref[members] = jnp.zeros(out_ref.shape[1:], F32)
-
-    at = jnp.int32(0)
-    for g in range(GROUPS):
-        start_ref[g] = at // 2
-
-        def put(member, at, g=g):
-            mine = group_ref[station(member)] == g
-
-            @pl.when(mine)
-            def _():
-                order_ref[at] = member
-
-            return at + mine.astype(jnp.int32)
-
-        at = lax.fori_loop(0, members, put, at)
-
-        @pl.when(at % 2 == 1)
-        def _():
-            order_ref[at] = members
-
-        at = at + at % 2
-    start_ref[GROUPS] = at // 2
-
-
-def beam_weights(at, chunk, delay_table, beam_pointing, station_group):
-    members = station_group.shape[0] // CHUNKS
+            delay = table_ref[beam_ref[beam], s]
+            down = jnp.where(sublane == d, delay, down)
+            across = jnp.where(lane == d, delay, across)
+        real, imag = turned_by(down * high)
+        row_ref[slot, 0] = scale * real
+        row_ref[slot, 1] = -scale * imag
+        real, imag = turned_by(across * low)
+        imag = -imag
+        for d in range(offsets):
+            high_re = row_ref[slot, 0, pl.ds(d, 1), :]
+            high_im = row_ref[slot, 1, pl.ds(d, 1), :]
+            low_re = jnp.broadcast_to(real[:, d : d + 1], shape)
+            low_im = jnp.broadcast_to(imag[:, d : d + 1], shape)
+            out_ref[member, d, 0] = (high_re * low_re - high_im * low_im).astype(BF)
+            out_ref[member, d, 1] = (high_re * low_im + high_im * low_re).astype(BF)
+
+    out_ref[members] = jnp.zeros(out_ref.shape[1:], BF)
+    lax.fori_loop(0, members // UNROLL, some_members, 0)
+
+
+def beam_weights(at, chosen, delay_table, beam_pointing, station_group):
+    chunk = 0 if chosen is None else 1
+    members = (HALF if chunk else STN) * PER
+
+    def offset_of(place, owner):
+        return place if chosen is None else offset_in(chosen, place) ^ owner
+
     offsets = beam_pointing.shape[0] // GROUPS
+    out = (members + 1, offsets, 2, LOW, LANES)
     return pl.pallas_call(
-        functools.partial(weight_kernel, chunk),
+        functools.partial(weight_kernel, chunk, offset_of),
         name="beam_weights",
         in_specs=[SMEM] * 4,
         out_specs=[VMEM, SMEM, SMEM],
         out_shape=[
-            jax.ShapeDtypeStruct((members + 1, offsets, 3, LOW, LANES), F32),
-            jax.ShapeDtypeStruct((members + GROUPS,), jnp.int32),
-            jax.ShapeDtypeStruct((GROUPS + 1,), jnp.int32),
+            jax.ShapeDtypeStruct(out, BF),
+            jax.ShapeDtypeStruct((GROUPS, members + 2), jnp.int32),
+            jax.ShapeDtypeStruct((GROUPS,), jnp.int32),
         ],
+        scratch_shapes=[pltpu.VMEM((UNROLL, 2, LOW, LANES), F32)],
         compiler_params=params(8),
         cost_estimate=cost(8, 1 << 29),
     )(at, delay_table, beam_pointing, station_group)
@@ -333,13 +370,13 @@
 
 def middle_kernel(at_ref, *refs):
     blocks, table_ref, outs = refs[:TF], refs[TF], refs[TF + 1 :]
-    me, owner = at_ref[0], at_ref[1]
+    me = at_ref[0]
     per_dest = blocks[0].shape[2]
     table = table_of(table_ref, [me ^ d for d in range(TF)])
-    for e, out in enumerate(outs):
-
-        def parts_of(o, e=e):
-            return [block[owner ^ e, o].reshape(per_dest * 2 * LOW, LANES) for block in blocks]
+    for place, out in enumerate(outs):
+
+        def parts_of(o, place=place):
+            return [block[place, o].reshape(per_dest * 2 * LOW, LANES) for block in blocks]
 
         def put(a, o, value, out=out):
             out[a, o] = value.astype(BF)
@@ -354,38 +391,51 @@
         middle_kernel,
         name="middle_step",
         in_specs=[SMEM] + [VMEM] * (TF + 1),
-        out_specs=[VMEM] * STN,
-        out_shape=[jax.ShapeDtypeStruct(out, BF)] * STN,
+        out_specs=[VMEM] * HALF,
+        out_shape=[jax.ShapeDtypeStruct(out, BF)] * HALF,
         compiler_params=params(4),
         cost_estimate=cost(4, 1 << 28),
     )(at, *blocks, table)
 
 
-def form_beams_of(offsets, chan_ref, weight_ref, order_ref, start_ref, put):
+def spread_weights(offsets, weight_ref, wide_ref):
+    def one(member, carry):
+        for i, d in enumerate(offsets):
+            real, imag = weight_ref[member, d, 0].astype(F32), weight_ref[member, d, 1].astype(F32)
+            wide_ref[member, i, 0] = real
+            wide_ref[member, i, 1] = imag - real
+            wide_ref[member, i, 2] = imag + real
+        return carry
+
+    lax.fori_loop(0, weight_ref.shape[0], one, 0, unroll=4)
+
+
+def form_beams_of(offsets, chan_ref, wide_ref, order_ref, count_ref, put, ready=lambda g: None):
     count = len(offsets)
     wide = 16 // count
     blocks = chan_ref.shape[2] // wide
 
-    def one_block(step, carry):
-        g, base = step // blocks, step % blocks * wide
+    def one_block(g, step, carry):
+        base = step * wide
 
         def one_pair(pair, acc):
             acc = list(acc)
-            for member in (order_ref[2 * pair], order_ref[2 * pair + 1]):
+            for member in (order_ref[g, 2 * pair], order_ref[g, 2 * pair + 1]):
                 data = []
                 for x in range(wide):
                     re, im = chan_ref[member, 0, base + x], chan_ref[member, 1, base + x]
                     data.append((re + im, re, im))
                 for i, d in enumerate(offsets):
                     for y in range(3):
-                        weight = weight_ref[member, d, y]
+                        weight = wide_ref[member, i, y]
                         for x in range(wide):
                             at = (i * 3 + y) * wide + x
                             acc[at] = acc[at] + weight * data[x][y]
             return tuple(acc)
 
         zero = jnp.zeros((LOW, LANES), F32)
-        acc = lax.fori_loop(start_ref[g], start_ref[g + 1], one_pair, (zero,) * (3 * count * wide))
+        pairs = (count_ref[g] + 1) // 2
+        acc = lax.fori_loop(0, pairs, one_pair, (zero,) * (3 * count * wide))
         for i, d in enumerate(offsets):
             for x in range(wide):
                 both, re, im = (acc[(i * 3 + y) * wide + x] for y in range(3))
@@ -393,10 +443,14 @@
                 put(d, g, 1, base + x, both + re)
         return carry
 
-    lax.fori_loop(0, GROUPS * blocks, one_block, 0)
-
-
-def early_kernel(blocks_ref, table_ref, weight_ref, order_ref, start_ref, sum_hbm, chan_ref, sum_ref, sem):
+    for g in range(GROUPS):
+        ready(g)
+        lax.fori_loop(0, blocks, functools.partial(one_block, g), 0)
+
+
+def early_kernel(blocks_ref, table_ref, weight_ref, order_ref, count_ref, sum_hbm, chan_ref, sum_ref, wide_ref, sem):
+    offsets = range(weight_ref.shape[1])
+    spread_weights(offsets, weight_ref, wide_ref)
     sources, _, _, per_dest = blocks_ref.shape[:4]
     table = table_of(table_ref, range(TF))
     for src in range(sources):
@@ -410,39 +464,52 @@
         transform(parts_of, table, put)
     chan_ref[chan_ref.shape[0] - 1] = jnp.zeros(chan_ref.shape[1:], F32)
 
+
     def keep(d, g, o, fp, value):
         sum_ref[d, g, o, fp % 2, fp // 2] = value
 
-    form_beams_of(range(weight_ref.shape[1]), chan_ref, weight_ref, order_ref, start_ref, keep)
+    form_beams_of(offsets, chan_ref, wide_ref, order_ref, count_ref, keep)
     write = pltpu.make_async_copy(sum_ref, sum_hbm, sem)
     write.start()
     write.wait()
 
 
-def late_kernel(offsets, fresh, weight_ref, order_ref, start_ref, sum_hbm, *refs):
-    sum_ref, sem = refs[-2:]
-    read = pltpu.make_async_copy(sum_hbm.at[pl.ds(offsets[0], len(offsets))], sum_ref, sem)
-    read.start()
-    if fresh:
-        blocks, chan_ref, outs = refs[:STN], refs[STN], refs[STN + 1 : -2]
-        members, planes, both = chan_ref.shape[:3]
-        for e, block in enumerate(blocks):
-            value = block[...].astype(F32)
-            chan_ref[pl.ds(e * PER, PER)] = value.reshape(PER, planes, both, LOW, LANES)
-        chan_ref[members - 1] = jnp.zeros(chan_ref.shape[1:], F32)
-    else:
-        chan_ref, outs = refs[0], refs[1:-2]
-    read.wait()
+def late_kernel(last, weight_ref, order_ref, count_ref, sum_hbm, *refs):
+    sum_ref, wide_ref, chan_ref, sem = refs[-4:]
+    sources = chan_ref.shape[0] // PER
+    blocks, outs = refs[:sources], refs[sources:-4]
+    reads = [
+        pltpu.make_async_copy(sum_hbm.at[:, g], sum_ref.at[:, g], sem.at[g]) for g in range(GROUPS)
+    ]
+    for read in reads:
+        read.start()
+    offsets = range(weight_ref.shape[1])
+    spread_weights(offsets, weight_ref, wide_ref)
+    members, planes, both = chan_ref.shape[:3]
+    for place, block in enumerate(blocks):
+        value = block[...].astype(F32)
+        chan_ref[pl.ds(place * PER, PER)] = value.reshape(PER, planes, both, LOW, LANES)
+    chan_ref[members - 1] = jnp.zeros(chan_ref.shape[1:], F32)
+
+    def ready(g):
+        reads[g].wait()
 
     def put(d, g, o, fp, value):
         f, p = fp // 2, fp % 2
-        at = d - offsets[0]
-        outs[at][g, o, p, f] = (value + sum_ref[at, g, o, p, f]).astype(BF)
-
-    form_beams_of(offsets, chan_ref, weight_ref, order_ref, start_ref, put)
-
-
-def beams_early(blocks, table, weights, order, start):
+        value = value + sum_ref[d, g, o, p, f]
+        if last:
+            outs[d][g, o, p, f] = value.astype(BF)
+        else:
+            sum_ref[d, g, o, p, f] = value
+
+    form_beams_of(offsets, chan_ref, wide_ref, order_ref, count_ref, put, ready)
+    if not last:
+        write = pltpu.make_async_copy(sum_ref, outs[0], sem.at[0])
+        write.start()
+        write.wait()
+
+
+def beams_early(blocks, table, weights, order, count):
     planes, per_dest = blocks.shape[2:4]
     out = (weights.shape[1], GROUPS, planes, 2, per_dest, LOW, LANES)
     return pl.pallas_call(
@@ -454,31 +521,36 @@
         scratch_shapes=[
             pltpu.VMEM((weights.shape[0], planes, 2 * per_dest, LOW, LANES), F32),
             pltpu.VMEM(out, F32),
+            pltpu.VMEM(weights.shape[:2] + (3, LOW, LANES), F32),
             pltpu.SemaphoreType.DMA,
         ],
         compiler_params=params(12),
         cost_estimate=cost(8, 1 << 29),
-    )(blocks, table, weights, order, start)
-
-
-def beams_late(offsets, blocks, weights, order, start, partial):
-    fresh = isinstance(blocks, list)
-    more = blocks if fresh else [blocks]
+    )(blocks, table, weights, order, count)
+
+
+def beams_late(last, blocks, weights, order, count, partial):
     one = partial.shape[1:]
-    out_shape = [jax.ShapeDtypeStruct(one, BF)] * len(offsets)
-    if fresh:
-        chan = (weights.shape[0], one[1], one[2] * one[3], LOW, LANES)
-        out_shape = [jax.ShapeDtypeStruct(chan, F32)] + out_shape
+    members = weights.shape[0]
+    if last:
+        out_shape, out_specs = [jax.ShapeDtypeStruct(one, BF)] * partial.shape[0], [VMEM] * partial.shape[0]
+    else:
+        out_shape, out_specs = jax.ShapeDtypeStruct(partial.shape, F32), HBM
     return pl.pallas_call(
-        functools.partial(late_kernel, offsets, fresh),
+        functools.partial(late_kernel, last),
         name="beams_late",
-        in_specs=[VMEM, SMEM, SMEM, HBM] + [VMEM] * len(more),
-        out_specs=[VMEM] * len(out_shape),
+        in_specs=[VMEM, SMEM, SMEM, HBM] + [VMEM] * len(blocks),
+        out_specs=out_specs,
         out_shape=out_shape,
-        scratch_shapes=[pltpu.VMEM((len(offsets),) + one, F32), pltpu.SemaphoreType.DMA],
+        scratch_shapes=[
+            pltpu.VMEM(partial.shape, F32),
+            pltpu.VMEM((members, partial.shape[0], 3, LOW, LANES), F32),
+            pltpu.VMEM((members, one[1], one[2] * one[3], LOW, LANES), F32),
+            pltpu.SemaphoreType.DMA((GROUPS,)),
+        ],
         compiler_params=params(12),
         cost_estimate=cost(8, 1 << 29),
-    )(weights, order, start, partial, *more)
+    )(weights, order, count, partial, *blocks)
 
 
 def gather_kernel(me_ref, *refs):
@@ -534,33 +606,31 @@
             row.append(swapped(own[d], "tf", d))
         blocks.append(row)
 
-    value = channel_step(me, blocks[0], window, first, cosine, sine, False)
+    value = channel_step(at, blocks[0], window, first, cosine, sine, False)
     shape = value.shape
     value = value.reshape((STN * TF,) + shape[2:])
     value = lax.all_to_all(value, ("stn", "tf"), split_axis=0, concat_axis=0, tiled=True)
     turned = value.reshape(shape)
 
-    own = channel_step(me, blocks[1], window, first, cosine, sine, True)
-    row = [own[0]]
-    for d in range(1, TF):
-        row.append(swapped(own[d], "tf", d))
-    own = middle_step(at, row, second)
-    late = [own[0]]
-    for e in range(1, STN):
-        late.append(swapped(own[e], "stn", e))
+    own = channel_step(at, blocks[1], window, first, cosine, sine, True)
+    late = [None] * STN
+    for chosen, offsets in enumerate(ROUNDS):
+        row = [own[chosen * TF]]
+        for d in range(1, TF):
+            row.append(swapped(own[chosen * TF + d], "tf", d))
+        sent = middle_step(at, row, second)
+        for e, value in zip(offsets, sent):
+            late[e] = swapped(value, "stn", e) if e else value
 
     args = (delay_table, beam_pointing, station_group)
+    weights = beam_weights(at, None, *args)
+    partial = beams_early(turned, second, *weights)
     weights = beam_weights(at, 0, *args)
-    partial = beams_early(turned, second, *weights)
+    partial = beams_late(False, [late[e] for e in ROUNDS[0]], *weights, partial)
     weights = beam_weights(at, 1, *args)
-    chan, *far = beams_late(range(STN // 2, STN), late, *weights, partial)
-    parts = [None] * STN
-    for i, value in enumerate(far):
-        d = STN // 2 + i
-        parts[d] = swapped(value, "stn", d)
-    near = beams_late(range(STN // 2), chan, *weights, partial)
-    for d, value in enumerate(near):
-        parts[d] = swapped(value, "stn", d) if d else value
+    parts = list(beams_late(True, [late[e] for e in ROUNDS[1]], *weights, partial))
+    for d in range(1, STN):
+        parts[d] = swapped(parts[d], "stn", d)
     return gather_frames(owner, parts)
 
 

time: 145 us -> 137 us (0.945)
  waiting for transfers between devices: 55.5 us -> 48.7 us
  local copies, waits for them, and re-layouts: 9.69 us -> 5.37 us
  Pallas kernels: 39.2 us -> 41.4 us
    ppermute x23 -> x26, waiting for transfers between devices: 55.5 us -> 48.7 us  [swapped(): return lax.ppermute(value, axis, [(i, i ^ offset) for i in range(count)])]
    unnamed x35, local copies, waits for them, and re-layouts: 9.69 us -> 5.37 us
    pallas_call x4 -> x5, Pallas kernels: 19.9 us -> 17.5 us  [the longest x3 9.71 us: beam_weights(): pl.pallas_call(functools.partial(weight_kernel, chunk, offset_of), name='...]
    pallas_call x2, Pallas kernels: 3.16 us -> 5.48 us  [spread(): pl.pallas_call(functools.partial(spread_kernel, chunk), name='spread', in...]
    pallas_call x1 -> x2, Pallas kernels: 2.43 us -> 4.17 us  [middle_step(): pl.pallas_call(middle_kernel, name='middle_step', in_specs=[SMEM] + [VMEM...]
    ppermute x23 -> x26, starting transfers between devices: 31.1 us -> 31.8 us  [swapped(): return lax.ppermute(value, axis, [(i, i ^ offset) for i in range(count)])]
  transfers between devices with their start and end apart: 24 -> 27, of which waited for: 8 -> 9; matrix products, arithmetic and copies ran while one was open for 2% -> 2% of each run, Pallas kernels for 19% -> 22%
where the time goes in v4:
time: 137 us; the launch traced here: 136 us
  waiting for transfers between devices  48.7 us (36%)
  Pallas kernels  41.4 us (30%)
  starting transfers between devices  37.6 us (27%)
  local copies, waits for them, and re-layouts  5.37 us (4%)
  other arithmetic  2.81 us (2%)
    ppermute x26, waiting for transfers between devices, swapped(): return lax.ppermute(value, axis, [(i, i ^ offset) for i in range(count)])  48.7 us
    ppermute x26, starting transfers between devices, swapped(): return lax.ppermute(value, axis, [(i, i ^ offset) for i in range(count)])  31.8 us
    pallas_call x3, Pallas kernels, beam_weights(): pl.pallas_call(functools.partial(weight_kernel, chunk, offset_of), name='...  9.71 us
    pallas_call x2, Pallas kernels, beams_late(): pl.pallas_call(functools.partial(late_kernel, last), name='beams_late', i...  7.82 us
    pallas_call x2, Pallas kernels, channel_step(): pl.pallas_call(functools.partial(channel_kernel, split), name='channel_st...  7.48 us
    all_to_all x1, starting transfers between devices, fast_body(): lax.all_to_all(value, ('stn', 'tf'), split_axis=0, concat_axis=0, tiled=T...  5.8 us
    pallas_call x1, Pallas kernels, beams_early(): pl.pallas_call(early_kernel, name='beams_early', in_specs=[VMEM] * 3 + [S...  5.7 us
    pallas_call x2, Pallas kernels, spread(): pl.pallas_call(functools.partial(spread_kernel, chunk), name='spread', in...  5.48 us
  transfers between devices with their start and end apart: 27, of which 9 were waited for; matrix products, arithmetic and copies ran while one was open for 2% of the time, Pallas kernels for 22%

profile of v4, /device:TPU:0, one launch (start us, length us, event | category | flops | bytes accessed | tf_op | source)
XLA Modules:
  0.0 136.3 jit_solution(5975865181762539852)
XLA Ops:
  0.0 2.6 %spread.2 = (bf16[2,8,64,128]{3,2,1,0:T(8,128)(2,1)S(1)}, bf16[2,8,64,128]{3,2,1,0:T(8,128)(2,1)S(1)}, bf16[2,8,64,128]{3,2,1,0:T(8,128)(2,1)S(1)}, bf16[2,8,64,128]{3,2,1,0:T(8,128)(2,1)S(1)}) custom-call(s32[1]{0:T(128)} %bitcast.1.me_ref, bf16[2,8,8,64,128]{4,3,2,1,0:T(8,128)(2,1)} %bitcast.10), custom_call_target="tpu_custom_call" | custom-call | bytes 4194304 | tf_op jit(solution)/shard_map/spread/pallas_call | solution.py:148
  3.2 2.6 %collective-permute-start.1 = (bf16[2,8,64,128]{3,2,1,0:T(8,128)(2,1)S(1)}, bf16[2,8,64,128]{3,2,1,0:T(8,128)(2,1)S(1)}, u32[]{:S(2)}, u32[]{:S(2)}) collective-permute-start(bf16[2,8,64,128]{3,2,1,0:T(8,128)(2,1)S(1)} %get-tuple-element.54), channel_id=1, source_target_pairs={{0,2},{1,3},{2,0},{3,1},{4,6},{5,7},{6,4},{7,5},{8,10},{9,11},{10,... | collective-permute-start | bytes 786440 | tf_op jit(solution)/shard_map/ppermute | solution.py:585
  5.9 2.5 %fusion.4.refs_4_ = f32[16,64,128]{2,1,0:T(8,128)S(1)} fusion(s32[128]{0:T(128)S(1)} %get-tuple-element.91, s32[128]{0:T(128)S(1)} %get-tuple-element.92, s32[]{:T(128)S(6)} %mul.101, s32[64]{0:T(128)S(1)} %get-tuple-element.89, s32[64]{0:T(128)S(1)} %get-tuple-element.90, s32[16]{0:T(128)S(1)} %iota_multiply_fusion.1, ...), kind=kLoop, calls=%fused_computation.10 | loop fusion | flops 6029312 | bytes 526084 | tf_op jit(solution)/shard_map/mul | solution.py:44
  8.7 4.2 %collective-permute-done.1.refs_2_ = bf16[2,8,64,128]{3,2,1,0:T(8,128)(2,1)S(1)} collective-permute-done((bf16[2,8,64,128]{3,2,1,0:T(8,128)(2,1)S(1)}, bf16[2,8,64,128]{3,2,1,0:T(8,128)(2,1)S(1)}, u32[]{:S(2)}, u32[]{:S(2)}) %collective-permute-start.1) | collective-permute-done | bytes 262176 | tf_op jit(solution)/shard_map/ppermute | solution.py:585
  12.9 5.1 %collective-permute-done.2.refs_3_ = bf16[2,8,64,128]{3,2,1,0:T(8,128)(2,1)S(1)} collective-permute-done((bf16[2,8,64,128]{3,2,1,0:T(8,128)(2,1)S(1)}, bf16[2,8,64,128]{3,2,1,0:T(8,128)(2,1)S(1)}, u32[]{:S(2)}, u32[]{:S(2)}) %collective-permute-start.2) | collective-permute-done | bytes 262176 | tf_op jit(solution)/shard_map/ppermute | solution.py:585
  18.0 4.1 %channel_step.2 = bf16[8,4,2,4,16,128]{5,4,3,2,1,0:T(8,128)(2,1)} custom-call(s32[2]{0:T(128)S(1)} %pad_add_fusion.at_ref, bf16[2,8,64,128]{3,2,1,0:T(8,128)(2,1)S(1)} %get-tuple-element.52.refs_0_, bf16[2,8,64,128]{3,2,1,0:T(8,128)(2,1)S(1)} %collective-permute-done.refs_1_, bf16[2,8,64,128]{3,2,1,0:T(8,128)(2,1)S(1)} %collective-permute-done.1.refs_2_, ...), custom_call_target="tpu_custom_call" | custom-call | flops 536870912 | bytes 8388608 | tf_op jit(solution)/shard_map/channel_step/pallas_call | solution.py:252
  22.1 5.8 %all-to-all-start = ((bf16[32,2,4,16,128]{4,3,2,1,0:T(8,128)(2,1)}), bf16[32,2,4,16,128]{4,3,2,1,0:T(8,128)(2,1)S(1)}, u32[]{:S(2)}, u32[]{:S(2)}) async-start(bf16[32,2,4,16,128]{4,3,2,1,0:T(8,128)(2,1)} %bitcast.5), calls=%async_computation | async-start | bytes 2097152 | tf_op jit(solution)/shard_map/all_to_all | solution.py:612
  28.0 2.9 %spread.3 = (bf16[2,8,64,128]{3,2,1,0:T(8,128)(2,1)S(1)}, bf16[2,8,64,128]{3,2,1,0:T(8,128)(2,1)S(1)}, bf16[2,8,64,128]{3,2,1,0:T(8,128)(2,1)S(1)}, bf16[2,8,64,128]{3,2,1,0:T(8,128)(2,1)S(1)}) custom-call(s32[1]{0:T(128)} %bitcast.1.me_ref, bf16[2,8,8,64,128]{4,3,2,1,0:T(8,128)(2,1)} %bitcast.11), custom_call_target="tpu_custom_call" | custom-call | bytes 4194304 | tf_op jit(solution)/shard_map/spread/pallas_call | solution.py:148
  31.2 1.6 %collective-permute-start.4 = (bf16[2,8,64,128]{3,2,1,0:T(8,128)(2,1)S(1)}, bf16[2,8,64,128]{3,2,1,0:T(8,128)(2,1)S(1)}, u32[]{:S(2)}, u32[]{:S(2)}) collective-permute-start(bf16[2,8,64,128]{3,2,1,0:T(8,128)(2,1)S(1)} %get-tuple-element.61), channel_id=1, source_target_pairs={{0,2},{1,3},{2,0},{3,1},{4,6},{5,7},{6,4},{7,5},{8,10},{9,11},{10,... | collective-permute-start | bytes 786440 | tf_op jit(solution)/shard_map/ppermute | solution.py:585
  32.8 13.9 %collective-permute-done.4.refs_2_ = bf16[2,8,64,128]{3,2,1,0:T(8,128)(2,1)S(1)} collective-permute-done((bf16[2,8,64,128]{3,2,1,0:T(8,128)(2,1)S(1)}, bf16[2,8,64,128]{3,2,1,0:T(8,128)(2,1)S(1)}, u32[]{:S(2)}, u32[]{:S(2)}) %collective-permute-start.4) | collective-permute-done | bytes 262176 | tf_op jit(solution)/shard_map/ppermute | solution.py:585
  46.6 7.4 %collective-permute-done.5.refs_3_ = bf16[2,8,64,128]{3,2,1,0:T(8,128)(2,1)S(1)} collective-permute-done((bf16[2,8,64,128]{3,2,1,0:T(8,128)(2,1)S(1)}, bf16[2,8,64,128]{3,2,1,0:T(8,128)(2,1)S(1)}, u32[]{:S(2)}, u32[]{:S(2)}) %collective-permute-start.5) | collective-permute-done | bytes 262176 | tf_op jit(solution)/shard_map/ppermute | solution.py:585
  54.0 3.4 %channel_step.3 = (bf16[4,2,4,16,128]{4,3,2,1,0:T(8,128)(2,1)S(1)}, bf16[4,2,4,16,128]{4,3,2,1,0:T(8,128)(2,1)S(1)}, bf16[4,2,4,16,128]{4,3,2,1,0:T(8,128)(2,1)S...) custom-call(s32[2]{0:T(128)S(1)} %pad_add_fusion.at_ref, ...), custom_call_target="tpu_custom_call" | custom-call | flops 536870912 | bytes 8388608 | tf_op jit(solution)/shard_map/channel_step/pallas_call | solution.py:252
  61.2 2.8 %collective-permute-done.7.refs_2_ = bf16[4,2,4,16,128]{4,3,2,1,0:T(8,128)(2,1)S(1)} collective-permute-done((bf16[4,2,4,16,128]{4,3,2,1,0:T(8,128)(2,1)S(1)}, bf16[4,2,4,16,128]{4,3,2,1,0:T(8,128)(2,1)S(1)}, u32[]{:S(2)}, u32[]{:S(2)}) %collective-permute-start.7) | collective-permute-done | bytes 131104 | tf_op jit(solution)/shard_map/ppermute | solution.py:585
  64.0 1.7 %collective-permute-done.8.refs_3_ = bf16[4,2,4,16,128]{4,3,2,1,0:T(8,128)(2,1)S(1)} collective-permute-done((bf16[4,2,4,16,128]{4,3,2,1,0:T(8,128)(2,1)S(1)}, bf16[4,2,4,16,128]{4,3,2,1,0:T(8,128)(2,1)S(1)}, u32[]{:S(2)}, u32[]{:S(2)}) %collective-permute-start.8) | collective-permute-done | bytes 131104 | tf_op jit(solution)/shard_map/ppermute | solution.py:585
  65.6 1.9 %middle_step.2 = (bf16[4,2,64,128]{3,2,1,0:T(8,128)(2,1)}, bf16[4,2,64,128]{3,2,1,0:T(8,128)(2,1)}, bf16[4,2,64,128]{3,2,1,0:T(8,128)(2,1)}, bf16[4,2,64,128]{3,2,1,0:T(8,128)(2,1)}) custom-call(s32[2]{0:T(128)S(1)} %pad_add_fusion.at_ref, bf16[4,2,4,16,128]{4,3,2,1,0:T(8,128)(2,1)S(1)} %get-tuple-element.63.refs_0_, ...), custom_call_target="tpu_custom_call" | custom-call | flops 268435456 | bytes 4194304 | tf_op jit(solution)/shard_map/middle_step/pallas_call | solution.py:390
  68.4 2.7 %collective-permute-start.11 = (bf16[4,2,64,128]{3,2,1,0:T(8,128)(2,1)}, bf16[4,2,64,128]{3,2,1,0:T(8,128)(2,1)S(1)}, u32[]{:S(2)}, u32[]{:S(2)}) collective-permute-start(bf16[4,2,64,128]{3,2,1,0:T(8,128)(2,1)} %get-tuple-element.69), channel_id=1, source_target_pairs={{0,16},{4,20},{8,24},{12,28},{16,0},{20,4},{24,8},{28,12},{1,17},{... | collective-permute-start | bytes 393224 | tf_op jit(solution)/shard_map/ppermute | solution.py:585
  71.3 3.8 %beam_weights.5 = (bf16[33,8,2,8,128]{4,3,2,1,0:T(8,128)(2,1)S(1)}, s32[4,34]{1,0:T(4,128)S(1)}, s32[4]{0:T(128)S(1)}) custom-call(s32[2]{0:T(128)S(1)} %pad_add_fusion.at_ref, f32[128,64]{1,0:T(8,128)S(1)} %copy.7.table_ref, s32[32]{0:T(128)S(1)} %copy-done.12, s32[64]{0:T(128)S(1)} %copy-done.13), custom_call_target="tpu_custom_call" | custom-call | flops 536870912 | bytes 8388608 | tf_op jit(solution)/shard_map/beam_weights/pallas_call | solution.py:342
  78.6 2.9 %beam_weights.4 = (bf16[17,8,2,8,128]{4,3,2,1,0:T(8,128)(2,1)S(1)}, s32[4,18]{1,0:T(4,128)S(1)}, s32[4]{0:T(128)S(1)}) custom-call(s32[2]{0:T(128)S(1)} %pad_add_fusion.at_ref, f32[128,64]{1,0:T(8,128)S(1)} %copy.7.table_ref, s32[32]{0:T(128)S(1)} %copy-done.12, s32[64]{0:T(128)S(1)} %copy-done.13), custom_call_target="tpu_custom_call" | custom-call | flops 536870912 | bytes 8388608 | tf_op jit(solution)/shard_map/beam_weights/pallas_call | solution.py:342
  83.4 2.3 %middle_step.3 = (bf16[4,2,64,128]{3,2,1,0:T(8,128)(2,1)S(1)}, bf16[4,2,64,128]{3,2,1,0:T(8,128)(2,1)}, bf16[4,2,64,128]{3,2,1,0:T(8,128)(2,1)}, bf16[4,2,64,128]{3,2,1,0:T(8,128)(2,1)}) custom-call(s32[2]{0:T(128)S(1)} %pad_add_fusion.at_ref, bf16[4,2,4,16,128]{4,3,2,1,0:T(8,128)(2,1)S(1)} %copy-done.15, bf16[4,2,4,16,128]{4,3,2,1,0:T(8,128)(2,1)S(1)} %copy-done.9, ...), custom_call_target="tpu_custom_call" | custom-call | flops 268435456 | bytes 4194304 | tf_op jit(solution)/shard_map/middle_step/pallas_call | solution.py:390
  87.5 2.4 %collective-permute-start.17 = (bf16[4,2,64,128]{3,2,1,0:T(8,128)(2,1)}, bf16[4,2,64,128]{3,2,1,0:T(8,128)(2,1)}, u32[]{:S(2)}, u32[]{:S(2)}) collective-permute-start(bf16[4,2,64,128]{3,2,1,0:T(8,128)(2,1)} %get-tuple-element.77), channel_id=1, source_target_pairs={{0,24},{4,28},{8,16},{12,20},{16,8},{20,12},{24,0},{28,4},{1,25},{... | collective-permute-start | bytes 393224 | tf_op jit(solution)/shard_map/ppermute | solution.py:585
  90.5 1.7 %collective-permute-start.18 = (bf16[4,2,64,128]{3,2,1,0:T(8,128)(2,1)}, bf16[4,2,64,128]{3,2,1,0:T(8,128)(2,1)}, u32[]{:S(2)}, u32[]{:S(2)}) collective-permute-start(bf16[4,2,64,128]{3,2,1,0:T(8,128)(2,1)} %get-tuple-element.78), channel_id=1, source_target_pairs={{0,28},{4,24},{8,20},{12,16},{16,12},{20,8},{24,4},{28,0},{1,29},{... | collective-permute-start | bytes 393224 | tf_op jit(solution)/shard_map/ppermute | solution.py:585
  93.1 3.0 %beam_weights.3 = (bf16[17,8,2,8,128]{4,3,2,1,0:T(8,128)(2,1)S(1)}, s32[4,18]{1,0:T(4,128)S(1)}, s32[4]{0:T(128)S(1)}) custom-call(s32[2]{0:T(128)S(1)} %pad_add_fusion.at_ref, f32[128,64]{1,0:T(8,128)S(1)} %copy-done.6, s32[32]{0:T(128)S(1)} %copy-done.12, s32[64]{0:T(128)S(1)} %copy-done.13), custom_call_target="tpu_custom_call" | custom-call | flops 536870912 | bytes 8388608 | tf_op jit(solution)/shard_map/beam_weights/pallas_call | solution.py:342
  96.1 5.7 %beams_early.1.sum_hbm = f32[8,4,2,2,4,8,128]{6,5,4,3,2,1,0:T(8,128)S(1)} custom-call(bf16[8,4,2,4,16,128]{5,4,3,2,1,0:T(8,128)(2,1)S(1)} %bitcast.9, bf16[2,4,32,256]{3,2,1,0:T(8,128)(2,1)S(1)} %copy-done, bf16[33,8,2,8,128]{4,3,2,1,0:T(8,128)(2,1)S(1)} %get-tuple-element.56.weight_ref, s32[4,34]{1,0:T(4,128)S(1)} %get-tuple-element.57.order_ref, ...), custom_call_target="tpu_custom_call" | custom-call | flops 536870912 | bytes 8388608 | tf_op jit(solution)/shard_map/beams_early/pallas_call | solution.py:515
  101.9 4.1 %beams_late.2.sum_hbm = f32[8,4,2,2,4,8,128]{6,5,4,3,2,1,0:T(8,128)S(1)} custom-call(bf16[17,8,2,8,128]{4,3,2,1,0:T(8,128)(2,1)S(1)} %get-tuple-element.49.weight_ref, s32[4,18]{1,0:T(4,128)S(1)} %get-tuple-element.50.order_ref, s32[4]{0:T(128)S(1)} %get-tuple-element.51.count_ref, f32[8,4,2,2,4,8,128]{6,5,4,3,2,1,0:T(8,128)S(1)} %beams_early.1.sum_hbm, ...), custom_call_target="tpu_custom_call" | custom-call | flops 536870912 | bytes 8388608 | tf_op jit(solution)/shard_map/beams_late/pallas_call | solution.py:539
  106.0 3.7 %beams_late.3 = (bf16[4,2,2,4,8,128]{5,4,3,2,1,0:T(8,128)(2,1)S(1)}, bf16[4,2,2,4,8,128]{5,4,3,2,1,0:T(8,128)(2,1)S(1)}, bf16[4,2,2,4,8,128]{5,4,3,2,1,0:T(8,128...) custom-call(bf16[17,8,2,8,128]{4,3,2,1,0:T(8,128)(2,1)S(1)} %get-tup, ...), custom_call_target="tpu_custom_call" | custom-call | flops 536870912 | bytes 8388608 | tf_op jit(solution)/shard_map/beams_late/pallas_call | solution.py:539
  109.7 1.3 collective-permute-start.19
  111.0 2.3 %collective-permute-start.21 = (bf16[4,2,2,4,8,128]{5,4,3,2,1,0:T(8,128)(2,1)S(1)}, bf16[4,2,2,4,8,128]{5,4,3,2,1,0:T(8,128)(2,1)S(1)}, u32[]{:S(2)}, u32[]{:S(2)}) collective-permute-start(bf16[4,2,2,4,8,128]{5,4,3,2,1,0:T(8,128)(2,1)S(1)} %get-tuple-element.82), channel_id=1, source_target_pairs={{0,12},{4,8},{8,4},{12,0},{16,28},{20,24},{24,20},{28,16},{1,13},{... | collective-permute-start | bytes 393224 | tf_op jit(solution)/shard_map/ppermute | solution.py:585
  114.6 2.3 %collective-permute-start.23 = (bf16[4,2,2,4,8,128]{5,4,3,2,1,0:T(8,128)(2,1)S(1)}, bf16[4,2,2,4,8,128]{5,4,3,2,1,0:T(8,128)(2,1)S(1)}, u32[]{:S(2)}, u32[]{:S(2)}) collective-permute-start(bf16[4,2,2,4,8,128]{5,4,3,2,1,0:T(8,128)(2,1)S(1)} %get-tuple-element.84), channel_id=1, source_target_pairs={{0,20},{4,16},{8,28},{12,24},{16,4},{20,0},{24,12},{28,8},{1,21},{... | collective-permute-start | bytes 393224 | tf_op jit(solution)/shard_map/ppermute | solution.py:585
  116.9 2.4 %collective-permute-start.24 = (bf16[4,2,2,4,8,128]{5,4,3,2,1,0:T(8,128)(2,1)S(1)}, bf16[4,2,2,4,8,128]{5,4,3,2,1,0:T(8,128)(2,1)S(1)}, u32[]{:S(2)}, u32[]{:S(2)}) collective-permute-start(bf16[4,2,2,4,8,128]{5,4,3,2,1,0:T(8,128)(2,1)S(1)} %get-tuple-element.85), channel_id=1, source_target_pairs={{0,24},{4,28},{8,16},{12,20},{16,8},{20,12},{24,0},{28,4},{1,25},{... | collective-permute-start | bytes 393224 | tf_op jit(solution)/shard_map/ppermute | solution.py:585
  120.1 2.2 %collective-permute-start.25 = (bf16[4,2,2,4,8,128]{5,4,3,2,1,0:T(8,128)(2,1)S(1)}, bf16[4,2,2,4,8,128]{5,4,3,2,1,0:T(8,128)(2,1)S(1)}, u32[]{:S(2)}, u32[]{:S(2)}) collective-permute-start(bf16[4,2,2,4,8,128]{5,4,3,2,1,0:T(8,128)(2,1)S(1)} %get-tuple-element.86), channel_id=1, source_target_pairs={{0,28},{4,24},{8,20},{12,16},{16,12},{20,8},{24,4},{28,0},{1,29},{... | collective-permute-start | bytes 393224 | tf_op jit(solution)/shard_map/ppermute | solution.py:585
  122.4 9.4 %collective-permute-done.22.refs_4_ = bf16[4,2,2,4,8,128]{5,4,3,2,1,0:T(8,128)(2,1)S(1)} collective-permute-done((bf16[4,2,2,4,8,128]{5,4,3,2,1,0:T(8,128)(2,1)S(1)}, bf16[4,2,2,4,8,128]{5,4,3,2,1,0:T(8,128)(2,1)S(1)}, u32[]{:S(2)}, u32[]{:S(2)}) %collective-permute-start.22) | collective-permute-done | bytes 131104 | tf_op jit(solution)/shard_map/ppermute | solution.py:585
  131.8 3.3 %collective-permute-done.23.refs_5_ = bf16[4,2,2,4,8,128]{5,4,3,2,1,0:T(8,128)(2,1)S(1)} collective-permute-done((bf16[4,2,2,4,8,128]{5,4,3,2,1,0:T(8,128)(2,1)S(1)}, bf16[4,2,2,4,8,128]{5,4,3,2,1,0:T(8,128)(2,1)S(1)}, u32[]{:S(2)}, u32[]{:S(2)}) %collective-permute-start.23) | collective-permute-done | bytes 131104 | tf_op jit(solution)/shard_map/ppermute | solution.py:585
  (81 shorter events, 18.0 us)
Async XLA Ops:
  0.0 18.0 %copy-start.7 = (bf16[2,4,16,128]{3,2,1,0:T(8,128)(2,1)S(1)}, bf16[2,4,16,128]{3,2,1,0:T(8,128)(2,1)}, u32[]{:S(2)}) copy-start(bf16[2,4,16,128]{3,2,1,0:T(8,128)(2,1)} %constant.119.clone.refs_5_) | copy-start | bytes 98308
  2.6 6.0 %collective-permute-start = (bf16[2,8,64,128]{3,2,1,0:T(8,128)(2,1)S(1)}, bf16[2,8,64,128]{3,2,1,0:T(8,128)(2,1)S(1)}, u32[]{:S(2)}, u32[]{:S(2)}) collective-permute-start(bf16[2,8,64,128]{3,2,1,0:T(8,128)(2,1)S(1)} %get-tuple-element.53), channel_id=1, source_target_pairs={{0,1},{1,0},{2,3},{3,2},{4,5},{5,4},{6,7},{7,6},{8,9},{9,8},{10,11... | collective-permute-start | bytes 786440 | tf_op jit(solution)/shard_map/ppermute | solution.py:585
  3.2 9.7 %collective-permute-start.1 = (bf16[2,8,64,128]{3,2,1,0:T(8,128)(2,1)S(1)}, bf16[2,8,64,128]{3,2,1,0:T(8,128)(2,1)S(1)}, u32[]{:S(2)}, u32[]{:S(2)}) collective-permute-start(bf16[2,8,64,128]{3,2,1,0:T(8,128)(2,1)S(1)} %get-tuple-element.54), channel_id=1, source_target_pairs={{0,2},{1,3},{2,0},{3,1},{4,6},{5,7},{6,4},{7,5},{8,10},{9,11},{10,... | collective-permute-start | bytes 786440 | tf_op jit(solution)/shard_map/ppermute | solution.py:585
  5.8 12.3 %collective-permute-start.2 = (bf16[2,8,64,128]{3,2,1,0:T(8,128)(2,1)S(1)}, bf16[2,8,64,128]{3,2,1,0:T(8,128)(2,1)S(1)}, u32[]{:S(2)}, u32[]{:S(2)}) collective-permute-start(bf16[2,8,64,128]{3,2,1,0:T(8,128)(2,1)S(1)} %get-tuple-element.55), channel_id=1, source_target_pairs={{0,3},{1,2},{2,1},{3,0},{4,7},{5,6},{6,5},{7,4},{8,11},{9,10},{10,... | collective-permute-start | bytes 786440 | tf_op jit(solution)/shard_map/ppermute | solution.py:585
  22.1 74.0 %all-to-all-start = ((bf16[32,2,4,16,128]{4,3,2,1,0:T(8,128)(2,1)}), bf16[32,2,4,16,128]{4,3,2,1,0:T(8,128)(2,1)S(1)}, u32[]{:S(2)}, u32[]{:S(2)}) async-start(bf16[32,2,4,16,128]{4,3,2,1,0:T(8,128)(2,1)} %bitcast.5), calls=%async_computation | async-start | bytes 2097152 | tf_op jit(solution)/shard_map/all_to_all | solution.py:612
  27.9 37.7 %copy-start = (bf16[2,4,32,256]{3,2,1,0:T(8,128)(2,1)S(1)}, bf16[2,4,32,256]{3,2,1,0:T(8,128)(2,1)}, u32[]{:S(2)}) copy-start(bf16[2,4,32,256]{3,2,1,0:T(8,128)(2,1)} %constant.120.clone.table_ref.refs_4_) | copy-start | bytes 393220
  27.9 43.2 %copy-start.16 = (f32[128,64]{0,1:T(8,128)S(1)}, f32[128,64]{0,1:T(8,128)}, u32[]{:S(2)}) copy-start(f32[128,64]{0,1:T(8,128)} %param.7) | copy-start | bytes 98308
  28.0 43.3 %copy-start.12 = (s32[32]{0:T(128)S(1)}, s32[32]{0:T(128)}, u32[]{:S(2)}) copy-start(s32[32]{0:T(128)} %beam_ref.5) | copy-start | bytes 388
  28.0 43.3 %copy-start.13 = (s32[64]{0:T(128)S(1)}, s32[64]{0:T(128)}, u32[]{:S(2)}) copy-start(s32[64]{0:T(128)} %group_ref.5) | copy-start | bytes 772
  30.9 1.9 %collective-permute-start.3 = (bf16[2,8,64,128]{3,2,1,0:T(8,128)(2,1)S(1)}, bf16[2,8,64,128]{3,2,1,0:T(8,128)(2,1)S(1)}, u32[]{:S(2)}, u32[]{:S(2)}) collective-permute-start(bf16[2,8,64,128]{3,2,1,0:T(8,128)(2,1)S(1)} %get-tuple-element.60), channel_id=1, source_target_pairs={{0,1},{1,0},{2,3},{3,2},{4,5},{5,4},{6,7},{7,6},{8,9},{9,8},{10,11... | collective-permute-start | bytes 786440 | tf_op jit(solution)/shard_map/ppermute | solution.py:585
  31.2 15.5 %collective-permute-start.4 = (bf16[2,8,64,128]{3,2,1,0:T(8,128)(2,1)S(1)}, bf16[2,8,64,128]{3,2,1,0:T(8,128)(2,1)S(1)}, u32[]{:S(2)}, u32[]{:S(2)}) collective-permute-start(bf16[2,8,64,128]{3,2,1,0:T(8,128)(2,1)S(1)} %get-tuple-element.61), channel_id=1, source_target_pairs={{0,2},{1,3},{2,0},{3,1},{4,6},{5,7},{6,4},{7,5},{8,10},{9,11},{10,... | collective-permute-start | bytes 786440 | tf_op jit(solution)/shard_map/ppermute | solution.py:585
  32.8 21.2 %collective-permute-start.5 = (bf16[2,8,64,128]{3,2,1,0:T(8,128)(2,1)S(1)}, bf16[2,8,64,128]{3,2,1,0:T(8,128)(2,1)S(1)}, u32[]{:S(2)}, u32[]{:S(2)}) collective-permute-start(bf16[2,8,64,128]{3,2,1,0:T(8,128)(2,1)S(1)} %get-tuple-element.62), channel_id=1, source_target_pairs={{0,3},{1,2},{2,1},{3,0},{4,7},{5,6},{6,5},{7,4},{8,11},{9,10},{10,... | collective-permute-start | bytes 786440 | tf_op jit(solution)/shard_map/ppermute | solution.py:585
  57.4 3.0 %collective-permute-start.6 = (bf16[4,2,4,16,128]{4,3,2,1,0:T(8,128)(2,1)S(1)}, bf16[4,2,4,16,128]{4,3,2,1,0:T(8,128)(2,1)S(1)}, u32[]{:S(2)}, u32[]{:S(2)}) collective-permute-start(bf16[4,2,4,16,128]{4,3,2,1,0:T(8,128)(2,1)S(1)} %get-tuple-element.64), channel_id=1, source_target_pairs={{0,1},{1,0},{2,3},{3,2},{4,5},{5,4},{6,7},{7,6},{8,9},{9,8},{10,11... | collective-permute-start | bytes 393224 | tf_op jit(solution)/shard_map/ppermute | solution.py:585
  57.6 6.4 %collective-permute-start.7 = (bf16[4,2,4,16,128]{4,3,2,1,0:T(8,128)(2,1)S(1)}, bf16[4,2,4,16,128]{4,3,2,1,0:T(8,128)(2,1)S(1)}, u32[]{:S(2)}, u32[]{:S(2)}) collective-permute-start(bf16[4,2,4,16,128]{4,3,2,1,0:T(8,128)(2,1)S(1)} %get-tuple-element.65), channel_id=1, source_target_pairs={{0,2},{1,3},{2,0},{3,1},{4,6},{5,7},{6,4},{7,5},{8,10},{9,11},{10,... | collective-permute-start | bytes 393224 | tf_op jit(solution)/shard_map/ppermute | solution.py:585
  58.3 7.3 %collective-permute-start.8 = (bf16[4,2,4,16,128]{4,3,2,1,0:T(8,128)(2,1)S(1)}, bf16[4,2,4,16,128]{4,3,2,1,0:T(8,128)(2,1)S(1)}, u32[]{:S(2)}, u32[]{:S(2)}) collective-permute-start(bf16[4,2,4,16,128]{4,3,2,1,0:T(8,128)(2,1)S(1)} %get-tuple-element.66), channel_id=1, source_target_pairs={{0,3},{1,2},{2,1},{3,0},{4,7},{5,6},{6,5},{7,4},{8,11},{9,10},{10,... | collective-permute-start | bytes 393224 | tf_op jit(solution)/shard_map/ppermute | solution.py:585
  59.3 15.7 %collective-permute-start.13 = (bf16[4,2,4,16,128]{4,3,2,1,0:T(8,128)(2,1)S(1)}, bf16[4,2,4,16,128]{4,3,2,1,0:T(8,128)(2,1)S(1)}, u32[]{:S(2)}, u32[]{:S(2)}) collective-permute-start(bf16[4,2,4,16,128]{4,3,2,1,0:T(8,128)(2,1)S(1)} %get-tuple-element.72), channel_id=1, source_target_pairs={{0,1},{1,0},{2,3},{3,2},{4,5},{5,4},{6,7},{7,6},{8,9},{9,8},{10,11... | collective-permute-start | bytes 393224 | tf_op jit(solution)/shard_map/ppermute | solution.py:585
  59.7 17.2 %collective-permute-start.14 = (bf16[4,2,4,16,128]{4,3,2,1,0:T(8,128)(2,1)S(1)}, bf16[4,2,4,16,128]{4,3,2,1,0:T(8,128)(2,1)S(1)}, u32[]{:S(2)}, u32[]{:S(2)}) collective-permute-start(bf16[4,2,4,16,128]{4,3,2,1,0:T(8,128)(2,1)S(1)} %get-tuple-element.73), channel_id=1, source_target_pairs={{0,2},{1,3},{2,0},{3,1},{4,6},{5,7},{6,4},{7,5},{8,10},{9,11},{10,... | collective-permute-start | bytes 393224 | tf_op jit(solution)/shard_map/ppermute | solution.py:585
  60.5 21.1 %collective-permute-start.15 = (bf16[4,2,4,16,128]{4,3,2,1,0:T(8,128)(2,1)S(1)}, bf16[4,2,4,16,128]{4,3,2,1,0:T(8,128)(2,1)}, u32[]{:S(2)}, u32[]{:S(2)}) collective-permute-start(bf16[4,2,4,16,128]{4,3,2,1,0:T(8,128)(2,1)S(1)} %get-tuple-element.74), channel_id=1, source_target_pairs={{0,3},{1,2},{2,1},{3,0},{4,7},{5,6},{6,5},{7,4},{8,11},{9,10},{10,... | collective-permute-start | bytes 393224 | tf_op jit(solution)/shard_map/ppermute | solution.py:585
  67.5 20.0 %collective-permute-start.10 = (bf16[4,2,64,128]{3,2,1,0:T(8,128)(2,1)}, bf16[4,2,64,128]{3,2,1,0:T(8,128)(2,1)S(1)}, u32[]{:S(2)}, u32[]{:S(2)}) collective-permute-start(bf16[4,2,64,128]{3,2,1,0:T(8,128)(2,1)} %get-tuple-element.68), channel_id=1, source_target_pairs={{0,12},{4,8},{8,4},{12,0},{16,28},{20,24},{24,20},{28,16},{1,13},{... | collective-permute-start | bytes 393224 | tf_op jit(solution)/shard_map/ppermute | solution.py:585
  68.4 21.5 %collective-permute-start.11 = (bf16[4,2,64,128]{3,2,1,0:T(8,128)(2,1)}, bf16[4,2,64,128]{3,2,1,0:T(8,128)(2,1)S(1)}, u32[]{:S(2)}, u32[]{:S(2)}) collective-permute-start(bf16[4,2,64,128]{3,2,1,0:T(8,128)(2,1)} %get-tuple-element.69), channel_id=1, source_target_pairs={{0,16},{4,20},{8,24},{12,28},{16,0},{20,4},{24,8},{28,12},{1,17},{... | collective-permute-start | bytes 393224 | tf_op jit(solution)/shard_map/ppermute | solution.py:585
  75.7 26.1 %collective-permute-start.12 = (bf16[4,2,64,128]{3,2,1,0:T(8,128)(2,1)}, bf16[4,2,64,128]{3,2,1,0:T(8,128)(2,1)}, u32[]{:S(2)}, u32[]{:S(2)}) collective-permute-start(bf16[4,2,64,128]{3,2,1,0:T(8,128)(2,1)} %get-tuple-element.70), channel_id=1, source_target_pairs={{0,20},{4,16},{8,28},{12,24},{16,4},{20,0},{24,12},{28,8},{1,21},{... | collective-permute-start | bytes 393224 | tf_op jit(solution)/shard_map/ppermute | solution.py:585
  77.6 24.3 %collective-permute-start.9 = (bf16[4,2,64,128]{3,2,1,0:T(8,128)(2,1)}, bf16[4,2,64,128]{3,2,1,0:T(8,128)(2,1)}, u32[]{:S(2)}, u32[]{:S(2)}) collective-permute-start(bf16[4,2,64,128]{3,2,1,0:T(8,128)(2,1)} %get-tuple-element.67), channel_id=1, source_target_pairs={{0,8},{4,12},{8,0},{12,4},{16,24},{20,28},{24,16},{28,20},{1,9},{5... | collective-permute-start | bytes 393224 | tf_op jit(solution)/shard_map/ppermute | solution.py:585
  86.3 19.7 %collective-permute-start.16 = (bf16[4,2,64,128]{3,2,1,0:T(8,128)(2,1)}, bf16[4,2,64,128]{3,2,1,0:T(8,128)(2,1)}, u32[]{:S(2)}, u32[]{:S(2)}) collective-permute-start(bf16[4,2,64,128]{3,2,1,0:T(8,128)(2,1)} %get-tuple-element.76), channel_id=1, source_target_pairs={{0,4},{4,0},{8,12},{12,8},{16,20},{20,16},{24,28},{28,24},{1,5},{5... | collective-permute-start | bytes 393224 | tf_op jit(solution)/shard_map/ppermute | solution.py:585
  87.5 18.5 %collective-permute-start.17 = (bf16[4,2,64,128]{3,2,1,0:T(8,128)(2,1)}, bf16[4,2,64,128]{3,2,1,0:T(8,128)(2,1)}, u32[]{:S(2)}, u32[]{:S(2)}) collective-permute-start(bf16[4,2,64,128]{3,2,1,0:T(8,128)(2,1)} %get-tuple-element.77), channel_id=1, source_target_pairs={{0,24},{4,28},{8,16},{12,20},{16,8},{20,12},{24,0},{28,4},{1,25},{... | collective-permute-start | bytes 393224 | tf_op jit(solution)/shard_map/ppermute | solution.py:585
  90.5 15.5 %collective-permute-start.18 = (bf16[4,2,64,128]{3,2,1,0:T(8,128)(2,1)}, bf16[4,2,64,128]{3,2,1,0:T(8,128)(2,1)}, u32[]{:S(2)}, u32[]{:S(2)}) collective-permute-start(bf16[4,2,64,128]{3,2,1,0:T(8,128)(2,1)} %get-tuple-element.78), channel_id=1, source_target_pairs={{0,28},{4,24},{8,20},{12,16},{16,12},{20,8},{24,4},{28,0},{1,29},{... | collective-permute-start | bytes 393224 | tf_op jit(solution)/shard_map/ppermute | solution.py:585
  109.7 7.1 %collective-permute-start.19 = (bf16[4,2,2,4,8,128]{5,4,3,2,1,0:T(8,128)(2,1)S(1)}, bf16[4,2,2,4,8,128]{5,4,3,2,1,0:T(8,128)(2,1)S(1)}, u32[]{:S(2)}, u32[]{:S(2)}) collective-permute-start(bf16[4,2,2,4,8,128]{5,4,3,2,1,0:T(8,128)(2,1)S(1)} %get-tuple-element.80), channel_id=1, source_target_pairs={{0,4},{4,0},{8,12},{12,8},{16,20},{20,16},{24,28},{28,24},{1,5},{5... | collective-permute-start | bytes 393224 | tf_op jit(solution)/shard_map/ppermute | solution.py:585
  111.0 9.1 %collective-permute-start.20 = (bf16[4,2,2,4,8,128]{5,4,3,2,1,0:T(8,128)(2,1)S(1)}, bf16[4,2,2,4,8,128]{5,4,3,2,1,0:T(8,128)(2,1)S(1)}, u32[]{:S(2)}, u32[]{:S(2)}) collective-permute-start(bf16[4,2,2,4,8,128]{5,4,3,2,1,0:T(8,128)(2,1)S(1)} %get-tuple-element.81), channel_id=1, source_target_pairs={{0,8},{4,12},{8,0},{12,4},{16,24},{20,28},{24,16},{28,20},{1,9},{5... | collective-permute-start | bytes 393224 | tf_op jit(solution)/shard_map/ppermute | solution.py:585
  111.0 11.3 %collective-permute-start.21 = (bf16[4,2,2,4,8,128]{5,4,3,2,1,0:T(8,128)(2,1)S(1)}, bf16[4,2,2,4,8,128]{5,4,3,2,1,0:T(8,128)(2,1)S(1)}, u32[]{:S(2)}, u32[]{:S(2)}) collective-permute-start(bf16[4,2,2,4,8,128]{5,4,3,2,1,0:T(8,128)(2,1)S(1)} %get-tuple-element.82), channel_id=1, source_target_pairs={{0,12},{4,8},{8,4},{12,0},{16,28},{20,24},{24,20},{28,16},{1,13},{... | collective-permute-start | bytes 393224 | tf_op jit(solution)/shard_map/ppermute | solution.py:585
  113.3 18.5 %collective-permute-start.22 = (bf16[4,2,2,4,8,128]{5,4,3,2,1,0:T(8,128)(2,1)S(1)}, bf16[4,2,2,4,8,128]{5,4,3,2,1,0:T(8,128)(2,1)S(1)}, u32[]{:S(2)}, u32[]{:S(2)}) collective-permute-start(bf16[4,2,2,4,8,128]{5,4,3,2,1,0:T(8,128)(2,1)S(1)} %get-tuple-element.83), channel_id=1, source_target_pairs={{0,16},{4,20},{8,24},{12,28},{16,0},{20,4},{24,8},{28,12},{1,17},{... | collective-permute-start | bytes 393224 | tf_op jit(solution)/shard_map/ppermute | solution.py:585
  114.6 20.6 %collective-permute-start.23 = (bf16[4,2,2,4,8,128]{5,4,3,2,1,0:T(8,128)(2,1)S(1)}, bf16[4,2,2,4,8,128]{5,4,3,2,1,0:T(8,128)(2,1)S(1)}, u32[]{:S(2)}, u32[]{:S(2)}) collective-permute-start(bf16[4,2,2,4,8,128]{5,4,3,2,1,0:T(8,128)(2,1)S(1)} %get-tuple-element.84), channel_id=1, source_target_pairs={{0,20},{4,16},{8,28},{12,24},{16,4},{20,0},{24,12},{28,8},{1,21},{... | collective-permute-start | bytes 393224 | tf_op jit(solution)/shard_map/ppermute | solution.py:585
  116.9 18.2 %collective-permute-start.24 = (bf16[4,2,2,4,8,128]{5,4,3,2,1,0:T(8,128)(2,1)S(1)}, bf16[4,2,2,4,8,128]{5,4,3,2,1,0:T(8,128)(2,1)S(1)}, u32[]{:S(2)}, u32[]{:S(2)}) collective-permute-start(bf16[4,2,2,4,8,128]{5,4,3,2,1,0:T(8,128)(2,1)S(1)} %get-tuple-element.85), channel_id=1, source_target_pairs={{0,24},{4,28},{8,16},{12,20},{16,8},{20,12},{24,0},{28,4},{1,25},{... | collective-permute-start | bytes 393224 | tf_op jit(solution)/shard_map/ppermute | solution.py:585
  120.1 15.0 %collective-permute-start.25 = (bf16[4,2,2,4,8,128]{5,4,3,2,1,0:T(8,128)(2,1)S(1)}, bf16[4,2,2,4,8,128]{5,4,3,2,1,0:T(8,128)(2,1)S(1)}, u32[]{:S(2)}, u32[]{:S(2)}) collective-permute-start(bf16[4,2,2,4,8,128]{5,4,3,2,1,0:T(8,128)(2,1)S(1)} %get-tuple-element.86), channel_id=1, source_target_pairs={{0,28},{4,24},{8,20},{12,16},{16,12},{20,8},{24,4},{28,0},{1,29},{... | collective-permute-start | bytes 393224 | tf_op jit(solution)/shard_map/ppermute | solution.py:585
  (12 other events, 50.0 us)

commit v5 on v4

--- a/solution.py
+++ b/solution.py
@@ -335,7 +335,7 @@
     members = (HALF if chunk else STN) * PER
 
     def offset_of(place, owner):
-        return place if chosen is None else offset_in(chosen, place) ^ owner
+        return place if chosen is None else (chosen * HALF + place) ^ owner
 
     offsets = beam_pointing.shape[0] // GROUPS
     out = (members + 1, offsets, 2, LOW, LANES)
@@ -626,9 +626,9 @@
     weights = beam_weights(at, None, *args)
     partial = beams_early(turned, second, *weights)
     weights = beam_weights(at, 0, *args)
-    partial = beams_late(False, [late[e] for e in ROUNDS[0]], *weights, partial)
+    partial = beams_late(False, late[:HALF], *weights, partial)
     weights = beam_weights(at, 1, *args)
-    parts = list(beams_late(True, [late[e] for e in ROUNDS[1]], *weights, partial))
+    parts = list(beams_late(True, late[HALF:], *weights, partial))
     for d in range(1, STN):
         parts[d] = swapped(parts[d], "stn", d)
     return gather_frames(owner, parts)

time: 137 us -> 139 us (1.015); the launches traced: 136 us -> 137 us
  starting transfers between devices: 37.6 us -> 41.6 us
  local copies, waits for them, and re-layouts: 5.37 us -> 3.17 us
    ppermute x26, starting transfers between devices: 31.8 us -> 35.9 us  [swapped(): return lax.ppermute(value, axis, [(i, i ^ offset) for i in range(count)])]
    unnamed x35 -> x27, local copies, waits for them, and re-layouts: 5.37 us -> 3.17 us
  transfers between devices with their start and end apart: 27 -> 27, of which waited for: 9 -> 8; matrix products, arithmetic and copies ran while one was open for 2% -> 2% of each run, Pallas kernels for 22% -> 22%
where the time goes in v5:
time: 139 us; the launch traced here: 137 us
  waiting for transfers between devices  47.6 us (34%)
  starting transfers between devices  41.6 us (30%)
  Pallas kernels  41.1 us (30%)
  local copies, waits for them, and re-layouts  3.17 us (2%)
  other arithmetic  2.81 us (2%)
    ppermute x26, waiting for transfers between devices, swapped(): return lax.ppermute(value, axis, [(i, i ^ offset) for i in range(count)])  47.6 us
    ppermute x26, starting transfers between devices, swapped(): return lax.ppermute(value, axis, [(i, i ^ offset) for i in range(count)])  35.9 us
    pallas_call x3, Pallas kernels, beam_weights(): pl.pallas_call(functools.partial(weight_kernel, chunk, offset_of), name='...  9.63 us
    pallas_call x2, Pallas kernels, beams_late(): pl.pallas_call(functools.partial(late_kernel, last), name='beams_late', i...  7.95 us
    pallas_call x2, Pallas kernels, channel_step(): pl.pallas_call(functools.partial(channel_kernel, split), name='channel_st...  7.48 us
    all_to_all x1, starting transfers between devices, fast_body(): lax.all_to_all(value, ('stn', 'tf'), split_axis=0, concat_axis=0, tiled=T...  5.8 us
    pallas_call x1, Pallas kernels, beams_early(): pl.pallas_call(early_kernel, name='beams_early', in_specs=[VMEM] * 3 + [S...  5.7 us
    pallas_call x2, Pallas kernels, spread(): pl.pallas_call(functools.partial(spread_kernel, chunk), name='spread', in...  5.48 us
  transfers between devices with their start and end apart: 27, of which 8 were waited for; matrix products, arithmetic and copies ran while one was open for 2% of the time, Pallas kernels for 22%

profile of v5, /device:TPU:0, one launch (start us, length us, event | category | flops | bytes accessed | tf_op | source)
XLA Modules:
  0.0 136.8 jit_solution(7761263878587819009)
XLA Ops:
  0.0 2.6 %spread.2 = (bf16[2,8,64,128]{3,2,1,0:T(8,128)(2,1)S(1)}, bf16[2,8,64,128]{3,2,1,0:T(8,128)(2,1)S(1)}, bf16[2,8,64,128]{3,2,1,0:T(8,128)(2,1)S(1)}, bf16[2,8,64,128]{3,2,1,0:T(8,128)(2,1)S(1)}) custom-call(s32[1]{0:T(128)} %bitcast.1.me_ref, bf16[2,8,8,64,128]{4,3,2,1,0:T(8,128)(2,1)} %bitcast.10), custom_call_target="tpu_custom_call" | custom-call | bytes 4194304 | tf_op jit(solution)/shard_map/spread/pallas_call | solution.py:148
  3.2 2.6 %collective-permute-start.1 = (bf16[2,8,64,128]{3,2,1,0:T(8,128)(2,1)S(1)}, bf16[2,8,64,128]{3,2,1,0:T(8,128)(2,1)S(1)}, u32[]{:S(2)}, u32[]{:S(2)}) collective-permute-start(bf16[2,8,64,128]{3,2,1,0:T(8,128)(2,1)S(1)} %get-tuple-element.54), channel_id=1, source_target_pairs={{0,2},{1,3},{2,0},{3,1},{4,6},{5,7},{6,4},{7,5},{8,10},{9,11},{10,... | collective-permute-start | bytes 786440 | tf_op jit(solution)/shard_map/ppermute | solution.py:585
  5.9 2.5 %fusion.4.refs_4_ = f32[16,64,128]{2,1,0:T(8,128)S(1)} fusion(s32[128]{0:T(128)S(1)} %get-tuple-element.91, s32[128]{0:T(128)S(1)} %get-tuple-element.92, s32[]{:T(128)S(6)} %mul.101, s32[64]{0:T(128)S(1)} %get-tuple-element.89, s32[64]{0:T(128)S(1)} %get-tuple-element.90, s32[16]{0:T(128)S(1)} %iota_multiply_fusion.1, ...), kind=kLoop, calls=%fused_computation.10 | loop fusion | flops 6029312 | bytes 526084 | tf_op jit(solution)/shard_map/mul | solution.py:44
  8.7 4.2 %collective-permute-done.1.refs_2_ = bf16[2,8,64,128]{3,2,1,0:T(8,128)(2,1)S(1)} collective-permute-done((bf16[2,8,64,128]{3,2,1,0:T(8,128)(2,1)S(1)}, bf16[2,8,64,128]{3,2,1,0:T(8,128)(2,1)S(1)}, u32[]{:S(2)}, u32[]{:S(2)}) %collective-permute-start.1) | collective-permute-done | bytes 262176 | tf_op jit(solution)/shard_map/ppermute | solution.py:585
  12.9 5.1 %collective-permute-done.2.refs_3_ = bf16[2,8,64,128]{3,2,1,0:T(8,128)(2,1)S(1)} collective-permute-done((bf16[2,8,64,128]{3,2,1,0:T(8,128)(2,1)S(1)}, bf16[2,8,64,128]{3,2,1,0:T(8,128)(2,1)S(1)}, u32[]{:S(2)}, u32[]{:S(2)}) %collective-permute-start.2) | collective-permute-done | bytes 262176 | tf_op jit(solution)/shard_map/ppermute | solution.py:585
  18.0 4.1 %channel_step.2 = bf16[8,4,2,4,16,128]{5,4,3,2,1,0:T(8,128)(2,1)} custom-call(s32[2]{0:T(128)S(1)} %pad_add_fusion.at_ref, bf16[2,8,64,128]{3,2,1,0:T(8,128)(2,1)S(1)} %get-tuple-element.52.refs_0_, bf16[2,8,64,128]{3,2,1,0:T(8,128)(2,1)S(1)} %collective-permute-done.refs_1_, bf16[2,8,64,128]{3,2,1,0:T(8,128)(2,1)S(1)} %collective-permute-done.1.refs_2_, ...), custom_call_target="tpu_custom_call" | custom-call | flops 536870912 | bytes 8388608 | tf_op jit(solution)/shard_map/channel_step/pallas_call | solution.py:252
  22.1 5.8 %all-to-all-start = ((bf16[32,2,4,16,128]{4,3,2,1,0:T(8,128)(2,1)}), bf16[32,2,4,16,128]{4,3,2,1,0:T(8,128)(2,1)S(1)}, u32[]{:S(2)}, u32[]{:S(2)}) async-start(bf16[32,2,4,16,128]{4,3,2,1,0:T(8,128)(2,1)} %bitcast.5), calls=%async_computation | async-start | bytes 2097152 | tf_op jit(solution)/shard_map/all_to_all | solution.py:612
  28.0 2.9 %spread.3 = (bf16[2,8,64,128]{3,2,1,0:T(8,128)(2,1)S(1)}, bf16[2,8,64,128]{3,2,1,0:T(8,128)(2,1)S(1)}, bf16[2,8,64,128]{3,2,1,0:T(8,128)(2,1)S(1)}, bf16[2,8,64,128]{3,2,1,0:T(8,128)(2,1)S(1)}) custom-call(s32[1]{0:T(128)} %bitcast.1.me_ref, bf16[2,8,8,64,128]{4,3,2,1,0:T(8,128)(2,1)} %bitcast.11), custom_call_target="tpu_custom_call" | custom-call | bytes 4194304 | tf_op jit(solution)/shard_map/spread/pallas_call | solution.py:148
  31.2 1.6 %collective-permute-start.4 = (bf16[2,8,64,128]{3,2,1,0:T(8,128)(2,1)S(1)}, bf16[2,8,64,128]{3,2,1,0:T(8,128)(2,1)S(1)}, u32[]{:S(2)}, u32[]{:S(2)}) collective-permute-start(bf16[2,8,64,128]{3,2,1,0:T(8,128)(2,1)S(1)} %get-tuple-element.61), channel_id=1, source_target_pairs={{0,2},{1,3},{2,0},{3,1},{4,6},{5,7},{6,4},{7,5},{8,10},{9,11},{10,... | collective-permute-start | bytes 786440 | tf_op jit(solution)/shard_map/ppermute | solution.py:585
  32.8 13.9 %collective-permute-done.4.refs_2_ = bf16[2,8,64,128]{3,2,1,0:T(8,128)(2,1)S(1)} collective-permute-done((bf16[2,8,64,128]{3,2,1,0:T(8,128)(2,1)S(1)}, bf16[2,8,64,128]{3,2,1,0:T(8,128)(2,1)S(1)}, u32[]{:S(2)}, u32[]{:S(2)}) %collective-permute-start.4) | collective-permute-done | bytes 262176 | tf_op jit(solution)/shard_map/ppermute | solution.py:585
  46.6 7.4 %collective-permute-done.5.refs_3_ = bf16[2,8,64,128]{3,2,1,0:T(8,128)(2,1)S(1)} collective-permute-done((bf16[2,8,64,128]{3,2,1,0:T(8,128)(2,1)S(1)}, bf16[2,8,64,128]{3,2,1,0:T(8,128)(2,1)S(1)}, u32[]{:S(2)}, u32[]{:S(2)}) %collective-permute-start.5) | collective-permute-done | bytes 262176 | tf_op jit(solution)/shard_map/ppermute | solution.py:585
  54.0 3.4 %channel_step.3 = (bf16[4,2,4,16,128]{4,3,2,1,0:T(8,128)(2,1)S(1)}, bf16[4,2,4,16,128]{4,3,2,1,0:T(8,128)(2,1)S(1)}, bf16[4,2,4,16,128]{4,3,2,1,0:T(8,128)(2,1)S...) custom-call(s32[2]{0:T(128)S(1)} %pad_add_fusion.at_ref, ...), custom_call_target="tpu_custom_call" | custom-call | flops 536870912 | bytes 8388608 | tf_op jit(solution)/shard_map/channel_step/pallas_call | solution.py:252
  61.2 2.8 %collective-permute-done.11.refs_2_ = bf16[4,2,4,16,128]{4,3,2,1,0:T(8,128)(2,1)S(1)} collective-permute-done((bf16[4,2,4,16,128]{4,3,2,1,0:T(8,128)(2,1)S(1)}, bf16[4,2,4,16,128]{4,3,2,1,0:T(8,128)(2,1)S(1)}, u32[]{:S(2)}, u32[]{:S(2)}) %collective-permute-start.11) | collective-permute-done | bytes 131104 | tf_op jit(solution)/shard_map/ppermute | solution.py:585
  64.0 1.7 %collective-permute-done.12.refs_3_ = bf16[4,2,4,16,128]{4,3,2,1,0:T(8,128)(2,1)S(1)} collective-permute-done((bf16[4,2,4,16,128]{4,3,2,1,0:T(8,128)(2,1)S(1)}, bf16[4,2,4,16,128]{4,3,2,1,0:T(8,128)(2,1)S(1)}, u32[]{:S(2)}, u32[]{:S(2)}) %collective-permute-start.12) | collective-permute-done | bytes 131104 | tf_op jit(solution)/shard_map/ppermute | solution.py:585
  65.6 1.9 %middle_step.3 = (bf16[4,2,64,128]{3,2,1,0:T(8,128)(2,1)}, bf16[4,2,64,128]{3,2,1,0:T(8,128)(2,1)}, bf16[4,2,64,128]{3,2,1,0:T(8,128)(2,1)}, bf16[4,2,64,128]{3,2,1,0:T(8,128)(2,1)}) custom-call(s32[2]{0:T(128)S(1)} %pad_add_fusion.at_ref, bf16[4,2,4,16,128]{4,3,2,1,0:T(8,128)(2,1)S(1)} %get-tuple-element.69.refs_0_, ...), custom_call_target="tpu_custom_call" | custom-call | flops 268435456 | bytes 4194304 | tf_op jit(solution)/shard_map/middle_step/pallas_call | solution.py:390
  68.5 1.7 %collective-permute-start.14 = (bf16[4,2,64,128]{3,2,1,0:T(8,128)(2,1)}, bf16[4,2,64,128]{3,2,1,0:T(8,128)(2,1)S(1)}, u32[]{:S(2)}, u32[]{:S(2)}) collective-permute-start(bf16[4,2,64,128]{3,2,1,0:T(8,128)(2,1)} %get-tuple-element.74), channel_id=1, source_target_pairs={{0,12},{4,8},{8,4},{12,0},{16,28},{20,24},{24,20},{28,16},{1,13},{... | collective-permute-start | bytes 393224 | tf_op jit(solution)/shard_map/ppermute | solution.py:585
  70.4 3.8 %beam_weights.5 = (bf16[33,8,2,8,128]{4,3,2,1,0:T(8,128)(2,1)S(1)}, s32[4,34]{1,0:T(4,128)S(1)}, s32[4]{0:T(128)S(1)}) custom-call(s32[2]{0:T(128)S(1)} %pad_add_fusion.at_ref, f32[128,64]{1,0:T(8,128)S(1)} %copy.7.table_ref, s32[32]{0:T(128)S(1)} %copy-done.8, s32[64]{0:T(128)S(1)} %copy-done.9), custom_call_target="tpu_custom_call" | custom-call | flops 536870912 | bytes 8388608 | tf_op jit(solution)/shard_map/beam_weights/pallas_call | solution.py:342
  75.1 1.9 %middle_step.2 = (bf16[4,2,64,128]{3,2,1,0:T(8,128)(2,1)S(1)}, bf16[4,2,64,128]{3,2,1,0:T(8,128)(2,1)}, bf16[4,2,64,128]{3,2,1,0:T(8,128)(2,1)}, bf16[4,2,64,128]{3,2,1,0:T(8,128)(2,1)}) custom-call(s32[2]{0:T(128)S(1)} %pad_add_fusion.at_ref, bf16[4,2,4,16,128]{4,3,2,1,0:T(8,128)(2,1)S(1)} %copy-done.11, ...), custom_call_target="tpu_custom_call" | custom-call | flops 268435456 | bytes 4194304 | tf_op jit(solution)/shard_map/middle_step/pallas_call | solution.py:390
  78.4 2.9 %beam_weights.4 = (bf16[17,8,2,8,128]{4,3,2,1,0:T(8,128)(2,1)S(1)}, s32[4,18]{1,0:T(4,128)S(1)}, s32[4]{0:T(128)S(1)}) custom-call(s32[2]{0:T(128)S(1)} %pad_add_fusion.at_ref, f32[128,64]{1,0:T(8,128)S(1)} %copy.7.table_ref, s32[32]{0:T(128)S(1)} %copy-done.8, s32[64]{0:T(128)S(1)} %copy-done.9), custom_call_target="tpu_custom_call" | custom-call | flops 536870912 | bytes 8388608 | tf_op jit(solution)/shard_map/beam_weights/pallas_call | solution.py:342
  82.8 2.3 %collective-permute-start.16 = (bf16[4,2,64,128]{3,2,1,0:T(8,128)(2,1)}, bf16[4,2,64,128]{3,2,1,0:T(8,128)(2,1)}, u32[]{:S(2)}, u32[]{:S(2)}) collective-permute-start(bf16[4,2,64,128]{3,2,1,0:T(8,128)(2,1)} %get-tuple-element.76), channel_id=1, source_target_pairs={{0,20},{4,16},{8,28},{12,24},{16,4},{20,0},{24,12},{28,8},{1,21},{... | collective-permute-start | bytes 393224 | tf_op jit(solution)/shard_map/ppermute | solution.py:585
  85.0 2.4 %collective-permute-start.17 = (bf16[4,2,64,128]{3,2,1,0:T(8,128)(2,1)}, bf16[4,2,64,128]{3,2,1,0:T(8,128)(2,1)}, u32[]{:S(2)}, u32[]{:S(2)}) collective-permute-start(bf16[4,2,64,128]{3,2,1,0:T(8,128)(2,1)} %get-tuple-element.77), channel_id=1, source_target_pairs={{0,24},{4,28},{8,16},{12,20},{16,8},{20,12},{24,0},{28,4},{1,25},{... | collective-permute-start | bytes 393224 | tf_op jit(solution)/shard_map/ppermute | solution.py:585
  88.0 1.7 %collective-permute-start.18 = (bf16[4,2,64,128]{3,2,1,0:T(8,128)(2,1)}, bf16[4,2,64,128]{3,2,1,0:T(8,128)(2,1)}, u32[]{:S(2)}, u32[]{:S(2)}) collective-permute-start(bf16[4,2,64,128]{3,2,1,0:T(8,128)(2,1)} %get-tuple-element.78), channel_id=1, source_target_pairs={{0,28},{4,24},{8,20},{12,16},{16,12},{20,8},{24,4},{28,0},{1,29},{... | collective-permute-start | bytes 393224 | tf_op jit(solution)/shard_map/ppermute | solution.py:585
  90.6 2.9 %beam_weights.3 = (bf16[17,8,2,8,128]{4,3,2,1,0:T(8,128)(2,1)S(1)}, s32[4,18]{1,0:T(4,128)S(1)}, s32[4]{0:T(128)S(1)}) custom-call(s32[2]{0:T(128)S(1)} %pad_add_fusion.at_ref, f32[128,64]{1,0:T(8,128)S(1)} %copy-done.6, s32[32]{0:T(128)S(1)} %copy-done.8, s32[64]{0:T(128)S(1)} %copy-done.9), custom_call_target="tpu_custom_call" | custom-call | flops 536870912 | bytes 8388608 | tf_op jit(solution)/shard_map/beam_weights/pallas_call | solution.py:342
  93.5 5.7 %beams_early.1.sum_hbm = f32[8,4,2,2,4,8,128]{6,5,4,3,2,1,0:T(8,128)S(1)} custom-call(bf16[8,4,2,4,16,128]{5,4,3,2,1,0:T(8,128)(2,1)S(1)} %bitcast.9, bf16[2,4,32,256]{3,2,1,0:T(8,128)(2,1)S(1)} %copy-done, bf16[33,8,2,8,128]{4,3,2,1,0:T(8,128)(2,1)S(1)} %get-tuple-element.56.weight_ref, s32[4,34]{1,0:T(4,128)S(1)} %get-tuple-element.57.order_ref, ...), custom_call_target="tpu_custom_call" | custom-call | flops 536870912 | bytes 8388608 | tf_op jit(solution)/shard_map/beams_early/pallas_call | solution.py:515
  99.3 4.2 %beams_late.2.sum_hbm = f32[8,4,2,2,4,8,128]{6,5,4,3,2,1,0:T(8,128)S(1)} custom-call(bf16[17,8,2,8,128]{4,3,2,1,0:T(8,128)(2,1)S(1)} %get-tuple-element.49.weight_ref, s32[4,18]{1,0:T(4,128)S(1)} %get-tuple-element.50.order_ref, s32[4]{0:T(128)S(1)} %get-tuple-element.51.count_ref, f32[8,4,2,2,4,8,128]{6,5,4,3,2,1,0:T(8,128)S(1)} %beams_early.1.sum_hbm, ...), custom_call_target="tpu_custom_call" | custom-call | flops 536870912 | bytes 8388608 | tf_op jit(solution)/shard_map/beams_late/pallas_call | solution.py:539
  103.5 3.8 %beams_late.3 = (bf16[4,2,2,4,8,128]{5,4,3,2,1,0:T(8,128)(2,1)S(1)}, bf16[4,2,2,4,8,128]{5,4,3,2,1,0:T(8,128)(2,1)S(1)}, bf16[4,2,2,4,8,128]{5,4,3,2,1,0:T(8,128...) custom-call(bf16[17,8,2,8,128]{4,3,2,1,0:T(8,128)(2,1)S(1)} %get-tup, ...), custom_call_target="tpu_custom_call" | custom-call | flops 536870912 | bytes 8388608 | tf_op jit(solution)/shard_map/beams_late/pallas_call | solution.py:539
  108.6 5.1 %collective-permute-start.20 = (bf16[4,2,2,4,8,128]{5,4,3,2,1,0:T(8,128)(2,1)S(1)}, bf16[4,2,2,4,8,128]{5,4,3,2,1,0:T(8,128)(2,1)S(1)}, u32[]{:S(2)}, u32[]{:S(2)}) collective-permute-start(bf16[4,2,2,4,8,128]{5,4,3,2,1,0:T(8,128)(2,1)S(1)} %get-tuple-element.81), channel_id=1, source_target_pairs={{0,8},{4,12},{8,0},{12,4},{16,24},{20,28},{24,16},{28,20},{1,9},{5... | collective-permute-start | bytes 393224 | tf_op jit(solution)/shard_map/ppermute | solution.py:585
  114.5 2.9 %collective-permute-start.22 = (bf16[4,2,2,4,8,128]{5,4,3,2,1,0:T(8,128)(2,1)S(1)}, bf16[4,2,2,4,8,128]{5,4,3,2,1,0:T(8,128)(2,1)S(1)}, u32[]{:S(2)}, u32[]{:S(2)}) collective-permute-start(bf16[4,2,2,4,8,128]{5,4,3,2,1,0:T(8,128)(2,1)S(1)} %get-tuple-element.83), channel_id=1, source_target_pairs={{0,16},{4,20},{8,24},{12,28},{16,0},{20,4},{24,8},{28,12},{1,17},{... | collective-permute-start | bytes 393224 | tf_op jit(solution)/shard_map/ppermute | solution.py:585
  117.7 2.4 %collective-permute-start.24 = (bf16[4,2,2,4,8,128]{5,4,3,2,1,0:T(8,128)(2,1)S(1)}, bf16[4,2,2,4,8,128]{5,4,3,2,1,0:T(8,128)(2,1)S(1)}, u32[]{:S(2)}, u32[]{:S(2)}) collective-permute-start(bf16[4,2,2,4,8,128]{5,4,3,2,1,0:T(8,128)(2,1)S(1)} %get-tuple-element.85), channel_id=1, source_target_pairs={{0,24},{4,28},{8,16},{12,20},{16,8},{20,12},{24,0},{28,4},{1,25},{... | collective-permute-start | bytes 393224 | tf_op jit(solution)/shard_map/ppermute | solution.py:585
  120.0 3.0 %collective-permute-start.25 = (bf16[4,2,2,4,8,128]{5,4,3,2,1,0:T(8,128)(2,1)S(1)}, bf16[4,2,2,4,8,128]{5,4,3,2,1,0:T(8,128)(2,1)S(1)}, u32[]{:S(2)}, u32[]{:S(2)}) collective-permute-start(bf16[4,2,2,4,8,128]{5,4,3,2,1,0:T(8,128)(2,1)S(1)} %get-tuple-element.86), channel_id=1, source_target_pairs={{0,28},{4,24},{8,20},{12,16},{16,12},{20,8},{24,4},{28,0},{1,29},{... | collective-permute-start | bytes 393224 | tf_op jit(solution)/shard_map/ppermute | solution.py:585
  123.1 2.0 %collective-permute-done.21.refs_3_ = bf16[4,2,2,4,8,128]{5,4,3,2,1,0:T(8,128)(2,1)S(1)} collective-permute-done((bf16[4,2,2,4,8,128]{5,4,3,2,1,0:T(8,128)(2,1)S(1)}, bf16[4,2,2,4,8,128]{5,4,3,2,1,0:T(8,128)(2,1)S(1)}, u32[]{:S(2)}, u32[]{:S(2)}) %collective-permute-start.21) | collective-permute-done | bytes 131104 | tf_op jit(solution)/shard_map/ppermute | solution.py:585
  125.0 10.6 %collective-permute-done.23.refs_5_ = bf16[4,2,2,4,8,128]{5,4,3,2,1,0:T(8,128)(2,1)S(1)} collective-permute-done((bf16[4,2,2,4,8,128]{5,4,3,2,1,0:T(8,128)(2,1)S(1)}, bf16[4,2,2,4,8,128]{5,4,3,2,1,0:T(8,128)(2,1)S(1)}, u32[]{:S(2)}, u32[]{:S(2)}) %collective-permute-start.23) | collective-permute-done | bytes 131104 | tf_op jit(solution)/shard_map/ppermute | solution.py:585
  (73 shorter events, 14.8 us)
Async XLA Ops:
  0.0 18.0 %copy-start.7 = (bf16[2,4,16,128]{3,2,1,0:T(8,128)(2,1)S(1)}, bf16[2,4,16,128]{3,2,1,0:T(8,128)(2,1)}, u32[]{:S(2)}) copy-start(bf16[2,4,16,128]{3,2,1,0:T(8,128)(2,1)} %constant.119.clone.refs_5_) | copy-start | bytes 98308
  2.6 6.0 %collective-permute-start = (bf16[2,8,64,128]{3,2,1,0:T(8,128)(2,1)S(1)}, bf16[2,8,64,128]{3,2,1,0:T(8,128)(2,1)S(1)}, u32[]{:S(2)}, u32[]{:S(2)}) collective-permute-start(bf16[2,8,64,128]{3,2,1,0:T(8,128)(2,1)S(1)} %get-tuple-element.53), channel_id=1, source_target_pairs={{0,1},{1,0},{2,3},{3,2},{4,5},{5,4},{6,7},{7,6},{8,9},{9,8},{10,11... | collective-permute-start | bytes 786440 | tf_op jit(solution)/shard_map/ppermute | solution.py:585
  3.2 9.7 %collective-permute-start.1 = (bf16[2,8,64,128]{3,2,1,0:T(8,128)(2,1)S(1)}, bf16[2,8,64,128]{3,2,1,0:T(8,128)(2,1)S(1)}, u32[]{:S(2)}, u32[]{:S(2)}) collective-permute-start(bf16[2,8,64,128]{3,2,1,0:T(8,128)(2,1)S(1)} %get-tuple-element.54), channel_id=1, source_target_pairs={{0,2},{1,3},{2,0},{3,1},{4,6},{5,7},{6,4},{7,5},{8,10},{9,11},{10,... | collective-permute-start | bytes 786440 | tf_op jit(solution)/shard_map/ppermute | solution.py:585
  5.8 12.3 %collective-permute-start.2 = (bf16[2,8,64,128]{3,2,1,0:T(8,128)(2,1)S(1)}, bf16[2,8,64,128]{3,2,1,0:T(8,128)(2,1)S(1)}, u32[]{:S(2)}, u32[]{:S(2)}) collective-permute-start(bf16[2,8,64,128]{3,2,1,0:T(8,128)(2,1)S(1)} %get-tuple-element.55), channel_id=1, source_target_pairs={{0,3},{1,2},{2,1},{3,0},{4,7},{5,6},{6,5},{7,4},{8,11},{9,10},{10,... | collective-permute-start | bytes 786440 | tf_op jit(solution)/shard_map/ppermute | solution.py:585
  22.1 71.4 %all-to-all-start = ((bf16[32,2,4,16,128]{4,3,2,1,0:T(8,128)(2,1)}), bf16[32,2,4,16,128]{4,3,2,1,0:T(8,128)(2,1)S(1)}, u32[]{:S(2)}, u32[]{:S(2)}) async-start(bf16[32,2,4,16,128]{4,3,2,1,0:T(8,128)(2,1)} %bitcast.5), calls=%async_computation | async-start | bytes 2097152 | tf_op jit(solution)/shard_map/all_to_all | solution.py:612
  27.9 37.7 %copy-start = (bf16[2,4,32,256]{3,2,1,0:T(8,128)(2,1)S(1)}, bf16[2,4,32,256]{3,2,1,0:T(8,128)(2,1)}, u32[]{:S(2)}) copy-start(bf16[2,4,32,256]{3,2,1,0:T(8,128)(2,1)} %constant.120.clone.table_ref.refs_4_) | copy-start | bytes 393220
  27.9 42.3 %copy-start.12 = (f32[128,64]{0,1:T(8,128)S(1)}, f32[128,64]{0,1:T(8,128)}, u32[]{:S(2)}) copy-start(f32[128,64]{0,1:T(8,128)} %param.7) | copy-start | bytes 98308
  28.0 42.4 %copy-start.8 = (s32[32]{0:T(128)S(1)}, s32[32]{0:T(128)}, u32[]{:S(2)}) copy-start(s32[32]{0:T(128)} %beam_ref.5) | copy-start | bytes 388
  28.0 42.4 %copy-start.9 = (s32[64]{0:T(128)S(1)}, s32[64]{0:T(128)}, u32[]{:S(2)}) copy-start(s32[64]{0:T(128)} %group_ref.5) | copy-start | bytes 772
  30.9 1.9 %collective-permute-start.3 = (bf16[2,8,64,128]{3,2,1,0:T(8,128)(2,1)S(1)}, bf16[2,8,64,128]{3,2,1,0:T(8,128)(2,1)S(1)}, u32[]{:S(2)}, u32[]{:S(2)}) collective-permute-start(bf16[2,8,64,128]{3,2,1,0:T(8,128)(2,1)S(1)} %get-tuple-element.60), channel_id=1, source_target_pairs={{0,1},{1,0},{2,3},{3,2},{4,5},{5,4},{6,7},{7,6},{8,9},{9,8},{10,11... | collective-permute-start | bytes 786440 | tf_op jit(solution)/shard_map/ppermute | solution.py:585
  31.2 15.5 %collective-permute-start.4 = (bf16[2,8,64,128]{3,2,1,0:T(8,128)(2,1)S(1)}, bf16[2,8,64,128]{3,2,1,0:T(8,128)(2,1)S(1)}, u32[]{:S(2)}, u32[]{:S(2)}) collective-permute-start(bf16[2,8,64,128]{3,2,1,0:T(8,128)(2,1)S(1)} %get-tuple-element.61), channel_id=1, source_target_pairs={{0,2},{1,3},{2,0},{3,1},{4,6},{5,7},{6,4},{7,5},{8,10},{9,11},{10,... | collective-permute-start | bytes 786440 | tf_op jit(solution)/shard_map/ppermute | solution.py:585
  32.8 21.2 %collective-permute-start.5 = (bf16[2,8,64,128]{3,2,1,0:T(8,128)(2,1)S(1)}, bf16[2,8,64,128]{3,2,1,0:T(8,128)(2,1)S(1)}, u32[]{:S(2)}, u32[]{:S(2)}) collective-permute-start(bf16[2,8,64,128]{3,2,1,0:T(8,128)(2,1)S(1)} %get-tuple-element.62), channel_id=1, source_target_pairs={{0,3},{1,2},{2,1},{3,0},{4,7},{5,6},{6,5},{7,4},{8,11},{9,10},{10,... | collective-permute-start | bytes 786440 | tf_op jit(solution)/shard_map/ppermute | solution.py:585
  57.4 3.0 %collective-permute-start.10 = (bf16[4,2,4,16,128]{4,3,2,1,0:T(8,128)(2,1)S(1)}, bf16[4,2,4,16,128]{4,3,2,1,0:T(8,128)(2,1)S(1)}, u32[]{:S(2)}, u32[]{:S(2)}) collective-permute-start(bf16[4,2,4,16,128]{4,3,2,1,0:T(8,128)(2,1)S(1)} %get-tuple-element.70), channel_id=1, source_target_pairs={{0,1},{1,0},{2,3},{3,2},{4,5},{5,4},{6,7},{7,6},{8,9},{9,8},{10,11... | collective-permute-start | bytes 393224 | tf_op jit(solution)/shard_map/ppermute | solution.py:585
  57.6 6.4 %collective-permute-start.11 = (bf16[4,2,4,16,128]{4,3,2,1,0:T(8,128)(2,1)S(1)}, bf16[4,2,4,16,128]{4,3,2,1,0:T(8,128)(2,1)S(1)}, u32[]{:S(2)}, u32[]{:S(2)}) collective-permute-start(bf16[4,2,4,16,128]{4,3,2,1,0:T(8,128)(2,1)S(1)} %get-tuple-element.71), channel_id=1, source_target_pairs={{0,2},{1,3},{2,0},{3,1},{4,6},{5,7},{6,4},{7,5},{8,10},{9,11},{10,... | collective-permute-start | bytes 393224 | tf_op jit(solution)/shard_map/ppermute | solution.py:585
  58.3 7.3 %collective-permute-start.12 = (bf16[4,2,4,16,128]{4,3,2,1,0:T(8,128)(2,1)S(1)}, bf16[4,2,4,16,128]{4,3,2,1,0:T(8,128)(2,1)S(1)}, u32[]{:S(2)}, u32[]{:S(2)}) collective-permute-start(bf16[4,2,4,16,128]{4,3,2,1,0:T(8,128)(2,1)S(1)} %get-tuple-element.72), channel_id=1, source_target_pairs={{0,3},{1,2},{2,1},{3,0},{4,7},{5,6},{6,5},{7,4},{8,11},{9,10},{10,... | collective-permute-start | bytes 393224 | tf_op jit(solution)/shard_map/ppermute | solution.py:585
  59.3 14.8 %collective-permute-start.6 = (bf16[4,2,4,16,128]{4,3,2,1,0:T(8,128)(2,1)S(1)}, bf16[4,2,4,16,128]{4,3,2,1,0:T(8,128)(2,1)S(1)}, u32[]{:S(2)}, u32[]{:S(2)}) collective-permute-start(bf16[4,2,4,16,128]{4,3,2,1,0:T(8,128)(2,1)S(1)} %get-tuple-element.64), channel_id=1, source_target_pairs={{0,1},{1,0},{2,3},{3,2},{4,5},{5,4},{6,7},{7,6},{8,9},{9,8},{10,11... | collective-permute-start | bytes 393224 | tf_op jit(solution)/shard_map/ppermute | solution.py:585
  59.7 14.4 %collective-permute-start.7 = (bf16[4,2,4,16,128]{4,3,2,1,0:T(8,128)(2,1)S(1)}, bf16[4,2,4,16,128]{4,3,2,1,0:T(8,128)(2,1)S(1)}, u32[]{:S(2)}, u32[]{:S(2)}) collective-permute-start(bf16[4,2,4,16,128]{4,3,2,1,0:T(8,128)(2,1)S(1)} %get-tuple-element.65), channel_id=1, source_target_pairs={{0,2},{1,3},{2,0},{3,1},{4,6},{5,7},{6,4},{7,5},{8,10},{9,11},{10,... | collective-permute-start | bytes 393224 | tf_op jit(solution)/shard_map/ppermute | solution.py:585
  60.5 13.7 %collective-permute-start.8 = (bf16[4,2,4,16,128]{4,3,2,1,0:T(8,128)(2,1)S(1)}, bf16[4,2,4,16,128]{4,3,2,1,0:T(8,128)(2,1)S(1)}, u32[]{:S(2)}, u32[]{:S(2)}) collective-permute-start(bf16[4,2,4,16,128]{4,3,2,1,0:T(8,128)(2,1)S(1)} %get-tuple-element.66), channel_id=1, source_target_pairs={{0,3},{1,2},{2,1},{3,0},{4,7},{5,6},{6,5},{7,4},{8,11},{9,10},{10,... | collective-permute-start | bytes 393224 | tf_op jit(solution)/shard_map/ppermute | solution.py:585
  67.5 17.5 %collective-permute-start.13 = (bf16[4,2,64,128]{3,2,1,0:T(8,128)(2,1)}, bf16[4,2,64,128]{3,2,1,0:T(8,128)(2,1)S(1)}, u32[]{:S(2)}, u32[]{:S(2)}) collective-permute-start(bf16[4,2,64,128]{3,2,1,0:T(8,128)(2,1)} %get-tuple-element.73), channel_id=1, source_target_pairs={{0,8},{4,12},{8,0},{12,4},{16,24},{20,28},{24,16},{28,20},{1,9},{5... | collective-permute-start | bytes 393224 | tf_op jit(solution)/shard_map/ppermute | solution.py:585
  68.5 18.8 %collective-permute-start.14 = (bf16[4,2,64,128]{3,2,1,0:T(8,128)(2,1)}, bf16[4,2,64,128]{3,2,1,0:T(8,128)(2,1)S(1)}, u32[]{:S(2)}, u32[]{:S(2)}) collective-permute-start(bf16[4,2,64,128]{3,2,1,0:T(8,128)(2,1)} %get-tuple-element.74), channel_id=1, source_target_pairs={{0,12},{4,8},{8,4},{12,0},{16,28},{20,24},{24,20},{28,16},{1,13},{... | collective-permute-start | bytes 393224 | tf_op jit(solution)/shard_map/ppermute | solution.py:585
  77.6 21.6 %collective-permute-start.9 = (bf16[4,2,64,128]{3,2,1,0:T(8,128)(2,1)}, bf16[4,2,64,128]{3,2,1,0:T(8,128)(2,1)}, u32[]{:S(2)}, u32[]{:S(2)}) collective-permute-start(bf16[4,2,64,128]{3,2,1,0:T(8,128)(2,1)} %get-tuple-element.68), channel_id=1, source_target_pairs={{0,4},{4,0},{8,12},{12,8},{16,20},{20,16},{24,28},{28,24},{1,5},{5... | collective-permute-start | bytes 393224 | tf_op jit(solution)/shard_map/ppermute | solution.py:585
  81.4 22.1 %collective-permute-start.15 = (bf16[4,2,64,128]{3,2,1,0:T(8,128)(2,1)}, bf16[4,2,64,128]{3,2,1,0:T(8,128)(2,1)}, u32[]{:S(2)}, u32[]{:S(2)}) collective-permute-start(bf16[4,2,64,128]{3,2,1,0:T(8,128)(2,1)} %get-tuple-element.75), channel_id=1, source_target_pairs={{0,16},{4,20},{8,24},{12,28},{16,0},{20,4},{24,8},{28,12},{1,17},{... | collective-permute-start | bytes 393224 | tf_op jit(solution)/shard_map/ppermute | solution.py:585
  82.8 20.7 %collective-permute-start.16 = (bf16[4,2,64,128]{3,2,1,0:T(8,128)(2,1)}, bf16[4,2,64,128]{3,2,1,0:T(8,128)(2,1)}, u32[]{:S(2)}, u32[]{:S(2)}) collective-permute-start(bf16[4,2,64,128]{3,2,1,0:T(8,128)(2,1)} %get-tuple-element.76), channel_id=1, source_target_pairs={{0,20},{4,16},{8,28},{12,24},{16,4},{20,0},{24,12},{28,8},{1,21},{... | collective-permute-start | bytes 393224 | tf_op jit(solution)/shard_map/ppermute | solution.py:585
  85.0 18.4 %collective-permute-start.17 = (bf16[4,2,64,128]{3,2,1,0:T(8,128)(2,1)}, bf16[4,2,64,128]{3,2,1,0:T(8,128)(2,1)}, u32[]{:S(2)}, u32[]{:S(2)}) collective-permute-start(bf16[4,2,64,128]{3,2,1,0:T(8,128)(2,1)} %get-tuple-element.77), channel_id=1, source_target_pairs={{0,24},{4,28},{8,16},{12,20},{16,8},{20,12},{24,0},{28,4},{1,25},{... | collective-permute-start | bytes 393224 | tf_op jit(solution)/shard_map/ppermute | solution.py:585
  88.0 15.4 %collective-permute-start.18 = (bf16[4,2,64,128]{3,2,1,0:T(8,128)(2,1)}, bf16[4,2,64,128]{3,2,1,0:T(8,128)(2,1)}, u32[]{:S(2)}, u32[]{:S(2)}) collective-permute-start(bf16[4,2,64,128]{3,2,1,0:T(8,128)(2,1)} %get-tuple-element.78), channel_id=1, source_target_pairs={{0,28},{4,24},{8,20},{12,16},{16,12},{20,8},{24,4},{28,0},{1,29},{... | collective-permute-start | bytes 393224 | tf_op jit(solution)/shard_map/ppermute | solution.py:585
  107.3 10.4 %collective-permute-start.19 = (bf16[4,2,2,4,8,128]{5,4,3,2,1,0:T(8,128)(2,1)S(1)}, bf16[4,2,2,4,8,128]{5,4,3,2,1,0:T(8,128)(2,1)S(1)}, u32[]{:S(2)}, u32[]{:S(2)}) collective-permute-start(bf16[4,2,2,4,8,128]{5,4,3,2,1,0:T(8,128)(2,1)S(1)} %get-tuple-element.80), channel_id=1, source_target_pairs={{0,4},{4,0},{8,12},{12,8},{16,20},{20,16},{24,28},{28,24},{1,5},{5... | collective-permute-start | bytes 393224 | tf_op jit(solution)/shard_map/ppermute | solution.py:585
  108.6 11.5 %collective-permute-start.20 = (bf16[4,2,2,4,8,128]{5,4,3,2,1,0:T(8,128)(2,1)S(1)}, bf16[4,2,2,4,8,128]{5,4,3,2,1,0:T(8,128)(2,1)S(1)}, u32[]{:S(2)}, u32[]{:S(2)}) collective-permute-start(bf16[4,2,2,4,8,128]{5,4,3,2,1,0:T(8,128)(2,1)S(1)} %get-tuple-element.81), channel_id=1, source_target_pairs={{0,8},{4,12},{8,0},{12,4},{16,24},{20,28},{24,16},{28,20},{1,9},{5... | collective-permute-start | bytes 393224 | tf_op jit(solution)/shard_map/ppermute | solution.py:585
  113.7 11.3 %collective-permute-start.21 = (bf16[4,2,2,4,8,128]{5,4,3,2,1,0:T(8,128)(2,1)S(1)}, bf16[4,2,2,4,8,128]{5,4,3,2,1,0:T(8,128)(2,1)S(1)}, u32[]{:S(2)}, u32[]{:S(2)}) collective-permute-start(bf16[4,2,2,4,8,128]{5,4,3,2,1,0:T(8,128)(2,1)S(1)} %get-tuple-element.82), channel_id=1, source_target_pairs={{0,12},{4,8},{8,4},{12,0},{16,28},{20,24},{24,20},{28,16},{1,13},{... | collective-permute-start | bytes 393224 | tf_op jit(solution)/shard_map/ppermute | solution.py:585
  114.5 10.5 %collective-permute-start.22 = (bf16[4,2,2,4,8,128]{5,4,3,2,1,0:T(8,128)(2,1)S(1)}, bf16[4,2,2,4,8,128]{5,4,3,2,1,0:T(8,128)(2,1)S(1)}, u32[]{:S(2)}, u32[]{:S(2)}) collective-permute-start(bf16[4,2,2,4,8,128]{5,4,3,2,1,0:T(8,128)(2,1)S(1)} %get-tuple-element.83), channel_id=1, source_target_pairs={{0,16},{4,20},{8,24},{12,28},{16,0},{20,4},{24,8},{28,12},{1,17},{... | collective-permute-start | bytes 393224 | tf_op jit(solution)/shard_map/ppermute | solution.py:585
  117.4 18.2 %collective-permute-start.23 = (bf16[4,2,2,4,8,128]{5,4,3,2,1,0:T(8,128)(2,1)S(1)}, bf16[4,2,2,4,8,128]{5,4,3,2,1,0:T(8,128)(2,1)S(1)}, u32[]{:S(2)}, u32[]{:S(2)}) collective-permute-start(bf16[4,2,2,4,8,128]{5,4,3,2,1,0:T(8,128)(2,1)S(1)} %get-tuple-element.84), channel_id=1, source_target_pairs={{0,20},{4,16},{8,28},{12,24},{16,4},{20,0},{24,12},{28,8},{1,21},{... | collective-permute-start | bytes 393224 | tf_op jit(solution)/shard_map/ppermute | solution.py:585
  117.7 18.0 %collective-permute-start.24 = (bf16[4,2,2,4,8,128]{5,4,3,2,1,0:T(8,128)(2,1)S(1)}, bf16[4,2,2,4,8,128]{5,4,3,2,1,0:T(8,128)(2,1)S(1)}, u32[]{:S(2)}, u32[]{:S(2)}) collective-permute-start(bf16[4,2,2,4,8,128]{5,4,3,2,1,0:T(8,128)(2,1)S(1)} %get-tuple-element.85), channel_id=1, source_target_pairs={{0,24},{4,28},{8,16},{12,20},{16,8},{20,12},{24,0},{28,4},{1,25},{... | collective-permute-start | bytes 393224 | tf_op jit(solution)/shard_map/ppermute | solution.py:585
  120.0 15.6 %collective-permute-start.25 = (bf16[4,2,2,4,8,128]{5,4,3,2,1,0:T(8,128)(2,1)S(1)}, bf16[4,2,2,4,8,128]{5,4,3,2,1,0:T(8,128)(2,1)S(1)}, u32[]{:S(2)}, u32[]{:S(2)}) collective-permute-start(bf16[4,2,2,4,8,128]{5,4,3,2,1,0:T(8,128)(2,1)S(1)} %get-tuple-element.86), channel_id=1, source_target_pairs={{0,28},{4,24},{8,20},{12,16},{16,12},{20,8},{24,4},{28,0},{1,29},{... | collective-permute-start | bytes 393224 | tf_op jit(solution)/shard_map/ppermute | solution.py:585
  (8 other events, 35.7 us)
